TPU v7x, 32 devices: a whole 2x2x4 slice. The times are simulated.
32 devices in a mesh: dp: 2 (over x), ctx: 16 (over z, y, core).
Axes of the slice: x: 2, y: 2, z: 4, core: 2. Of those that a mesh axis runs over, the one named last changes fastest.
Arguments:
- query_rows: bfloat16 [2, 4096, 2048], P('dp', 'ctx')
- key_rows: bfloat16 [2, 4096, 512], P('dp', 'ctx')
- value_rows: bfloat16 [2, 4096, 512], P('dp', 'ctx'), may hold values from -6 to 6
- out_grad: bfloat16 [2, 4096, 2048], P('dp', 'ctx'), may hold values from -6 to 6
- lengths: int32 [2, 8], P('dp'), may hold values from 1 to 1024, 4096 in all within a row
- loss_mask: int32 [2, 4096], P('dp', 'ctx'), may hold values from 0 to 1
Outputs:
- query_grad: bfloat16 [2, 4096, 2048], P('dp', 'ctx')
- key_grad: bfloat16 [2, 4096, 512], P('dp', 'ctx')
- value_grad: bfloat16 [2, 4096, 512], P('dp', 'ctx')
Inputs may be any that keep to these rules, and one draw needn't show every extreme that they name: `lengths`: each row sums to 4096, and its largest entry is exactly 1024.
All inputs are finite; a program needn't handle non-finite values.
Results may differ from a plain program's by a relative error of at most 0.017.
Values may be sent and summed in bfloat16 or wider, within the bound.
No kernel may reach another device: no remote copies, remote signals or barrier semaphores. Data moves between devices by JAX's collectives and lax.ppermute only.
A program may use at most 64 MiB of HBM per device.

v0:
```python
import math

import jax
import jax.numpy as jnp
from jax import lax
from jax.experimental import pallas as pl
from jax.experimental.pallas import tpu as pltpu
from jax.sharding import PartitionSpec as P


HQ = 16
HK = 4
HD = 128
WIN = 4
GROUP = HQ // HK
MINE = HK // 2
BLOCKS = WIN + 2
EXP2_SCALE = HD ** (-0.5) * math.log2(math.e)


def shifted(value, by):
    count = lax.axis_size("ctx")
    pairs = [(i, i + by) for i in range(count) if 0 <= i + by < count]
    return lax.ppermute(value, "ctx", pairs)


def swapped(value, bit):
    count = lax.axis_size("ctx")
    return lax.ppermute(value, "ctx", [(i, i ^ bit) for i in range(count)])


def everywhere_sum(value):
    dp_count = lax.axis_size("dp")
    step = 1
    while step < dp_count:
        other = lax.ppermute(value, "dp", [(i, i ^ step) for i in range(dp_count)])
        value = value + other
        step *= 2
    step = 1
    while step < lax.axis_size("ctx"):
        other = swapped(value, step)
        value = value + other
        step *= 2
    return value


def nt(a, b):
    return lax.dot_general(a, b, (((1,), (1,)), ((), ())), preferred_element_type=jnp.float32)


def nn(a, b):
    return lax.dot_general(a, b, (((1,), (0,)), ((), ())), preferred_element_type=jnp.float32)


def mask_column(mask_ref):
    rows = mask_ref.shape[1]
    return jnp.broadcast_to(mask_ref[...].astype(jnp.float32), (HD, rows)).T


def in_vmem():
    return pl.BlockSpec(memory_space=pltpu.VMEM)


def simple_call(kernel, where, in_specs, out_shape, *args):
    if not isinstance(out_shape, (list, tuple)):
        out_shape = [out_shape]
    return pl.pallas_call(
        kernel,
        grid_spec=pltpu.PrefetchScalarGridSpec(
            num_scalar_prefetch=1,
            grid=(1,),
            in_specs=in_specs,
            out_specs=[in_vmem() for _ in out_shape],
        ),
        out_shape=out_shape,
        compiler_params=pltpu.CompilerParams(vmem_limit_bytes=8 * 1024 * 1024),
        cost_estimate=pl.CostEstimate(flops=0, transcendentals=0, bytes_accessed=1024 * 1024),
    )(where, *args)


def column_block(rows, width, pick):
    return pl.BlockSpec((None, rows, width), lambda i, w: (0, 0, pick(w[0])))


def give_kv_call(where, key_rows, value_rows):
    rows = key_rows.shape[1]
    width = MINE * HD

    def kernel(where_ref, k_ref, v_ref, out):
        for h in range(MINE):
            out[h, 0] = k_ref[:, h * HD : (h + 1) * HD]
            out[h, 1] = v_ref[:, h * HD : (h + 1) * HD]

    theirs = column_block(rows, width, lambda i: 1 - (i & 1))
    shape = jax.ShapeDtypeStruct((MINE, 2, rows, HD), jnp.bfloat16)
    return simple_call(kernel, where, [theirs, theirs], shape, key_rows, value_rows)[0]


def local_kv_call(where, key_rows, value_rows, got_kv):
    rows = key_rows.shape[1]
    width = MINE * HD

    def kernel(where_ref, k_ref, v_ref, got, *outs):
        for h, out in enumerate(outs):
            out[0, 0] = k_ref[:, h * HD : (h + 1) * HD]
            out[0, 1] = v_ref[:, h * HD : (h + 1) * HD]
            out[1] = got[h]

    own = column_block(rows, width, lambda i: i & 1)
    shape = [jax.ShapeDtypeStruct((2, 2, rows, HD), jnp.bfloat16) for _ in range(MINE)]
    return simple_call(kernel, where, [own, own, in_vmem()], shape, key_rows, value_rows, got_kv)


def give_qg_call(where, query_rows, out_grad, loss_mask, after):
    rows = query_rows.shape[1]
    width = MINE * GROUP * HD

    def kernel(where_ref, q_ref, g_ref, mask_ref, after_ref, out, token):
        keep_rows = mask_column(mask_ref)
        out[0] = q_ref[...]
        for h in range(MINE * GROUP):
            columns = slice(h * HD, (h + 1) * HD)
            out[1, :, columns] = (g_ref[:, columns].astype(jnp.float32) * keep_rows).astype(
                jnp.bfloat16
            )
        local = jnp.sum(mask_ref[...].astype(jnp.float32), axis=1, keepdims=True)
        token[...] = jnp.broadcast_to(local, token.shape)

    theirs = column_block(rows, width, lambda i: 1 - (i & 1))
    shape = [
        jax.ShapeDtypeStruct((2, rows, width), jnp.bfloat16),
        jax.ShapeDtypeStruct((8, HD), jnp.float32),
    ]
    return simple_call(
        kernel, where, [theirs, theirs, in_vmem(), pl.BlockSpec(memory_space=pl.ANY)], shape,
        query_rows, out_grad, loss_mask, after,
    )


def total_call(where, numerator, parts, count):
    rows = parts[0][0].shape[2]

    def kernel(where_ref, *refs):
        own, give = refs[-2:]
        scale = numerator / refs[-3][0:1, :]
        for h in range(MINE):
            d0, r1, r2 = refs[3 * h : 3 * h + 3]
            for kv, factor in enumerate((scale * HD ** (-0.5), scale)):
                for p, out in enumerate((own, give)):
                    out[h, kv] = (
                        (d0[p, kv] + r1[p, kv].astype(jnp.float32) + r2[p, kv].astype(jnp.float32))
                        * factor
                    ).astype(jnp.bfloat16)

    args = [a for part in parts for a in part] + [count]
    specs = [in_vmem() for _ in args]
    shape = [jax.ShapeDtypeStruct((MINE, 2, rows, HD), jnp.bfloat16)] * 2
    return simple_call(kernel, where, specs, shape, *args)


def finish_kv_call(where, own, got):
    rows = own.shape[2]
    width = MINE * HD

    def kernel(where_ref, own_ref, got_ref, *outs):
        parity = where_ref[0] & 1
        for kv, out in enumerate(outs):
            for h in range(MINE):
                mine = pl.multiple_of(parity * width + h * HD, HD)
                theirs = pl.multiple_of((1 - parity) * width + h * HD, HD)
                out[0, :, pl.ds(mine, HD)] = own_ref[h, kv]
                out[0, :, pl.ds(theirs, HD)] = got_ref[h, kv]

    shape = [jax.ShapeDtypeStruct((1, rows, 2 * width), jnp.bfloat16)] * 2
    return simple_call(kernel, where, [in_vmem()] * 2, shape, own, got)


def finish_q_call(where, numerator, own, got, count):
    rows = own[0].shape[0]
    wide = GROUP * HD
    width = MINE * wide

    def kernel(where_ref, *refs):
        own_refs = refs[:MINE]
        got_refs = refs[MINE : 2 * MINE]
        count_ref, out, token = refs[2 * MINE :]
        token[...] = count_ref[...]
        scale = numerator / count_ref[0:1, :] * HD ** (-0.5)
        parity = where_ref[0] & 1
        for base, parts in ((parity * width, own_refs), ((1 - parity) * width, got_refs)):
            for h, part in enumerate(parts):
                for j in range(GROUP):
                    at = pl.multiple_of(base + h * wide + j * HD, HD)
                    value = part[:, j * HD : (j + 1) * HD].astype(jnp.float32) * scale
                    out[0, :, pl.ds(at, HD)] = value.astype(out.dtype)

    shape = [
        jax.ShapeDtypeStruct((1, rows, 2 * width), jnp.bfloat16),
        jax.ShapeDtypeStruct(count.shape, count.dtype),
    ]
    args = list(own) + list(got) + [count]
    return simple_call(kernel, where, [in_vmem() for _ in args], shape, *args)


def grads_kernel(
    where_ref, lengths_ref, mask_ref, token_in, own_q, own_g, got_qg, kv0, kv1, kv2,
    own_dq, sib_dq, out0, out1, out2, token_out,
    q_s, g_s, k_s, v_s, kt_s, e_s, dp_s, mb_s, m_s, l_s, w_s, dqt_s, dk_s, dv_s,
):
    rows = own_q.shape[0]
    token_out[...] = token_in[...]
    keep_rows = mask_column(mask_ref)
    my_index = where_ref[0]
    doc_count = lengths_ref.shape[1]
    for h in range(GROUP):
        columns = slice(h * HD, (h + 1) * HD)
        q_s[h] = own_q[:, columns]
        q_s[GROUP + h] = got_qg[0, :, columns]
        g_s[h] = (own_g[:, columns].astype(jnp.float32) * keep_rows).astype(jnp.bfloat16)
        g_s[GROUP + h] = got_qg[1, :, columns]
    for d, kv in enumerate((kv0, kv1, kv2)):
        for p in range(2):
            k_s[2 * d + p] = kv[p, 0]
            v_s[2 * d + p] = kv[p, 1]
            kt_s[2 * d + p] = kv[p, 0].T
    dk_s[...] = jnp.zeros_like(dk_s)
    dv_s[...] = jnp.zeros_like(dv_s)

    def per_q(qb, _):
        q_start = (my_index ^ qb) * rows

        def doc_step(j, state):
            bound, first, lo = state
            bound = bound + lengths_ref[0, j]
            first = jnp.where(bound <= q_start, bound, first)
            t_pos = q_start + lax.broadcasted_iota(jnp.int32, (1, rows), 1)
            lo = jnp.where(bound <= t_pos, bound, lo)
            return bound, first, lo

        _, first, lo = lax.fori_loop(
            0, doc_count, doc_step, (jnp.int32(0), jnp.int32(0), jnp.zeros((1, rows), jnp.int32))
        )
        t_pos = q_start + lax.broadcasted_iota(jnp.int32, (1, rows), 1)
        m_s[...] = jnp.full_like(m_s, -jnp.inf)
        l_s[...] = jnp.zeros_like(l_s)
        w_s[...] = jnp.zeros_like(w_s)
        dqt_s[...] = jnp.zeros_like(dqt_s)

        def locate(j):
            kb = jnp.where(j < 2, j ^ qb, j)
            k_start = ((my_index ^ (kb & 1)) - (kb // 2) * 2) * rows
            live = (k_start >= 0) & (k_start <= q_start) & (k_start + rows > first)
            return kb, k_start, live

        def phase_a(j, _):
            kb, k_start, live = locate(j)

            @pl.when(live)
            def _():
                u_pos = k_start + lax.broadcasted_iota(jnp.int32, (rows, rows), 0)
                bias = jnp.where((u_pos >= lo) & (u_pos <= t_pos), 0.0, -jnp.inf)
                k = k_s[kb]
                v = v_s[kb]
                for h in range(GROUP):
                    s = nt(k, q_s[qb * GROUP + h]) * EXP2_SCALE + bias
                    dp = nt(v, g_s[qb * GROUP + h])
                    m_old = m_s[h]
                    m_new = jnp.maximum(m_old, jnp.max(s, axis=0, keepdims=True))
                    keep = jnp.exp2(m_old - m_new)
                    e = jnp.exp2(s - m_new)
                    l_s[h] = l_s[h] * keep + jnp.sum(e, axis=0, keepdims=True)
                    w_s[h] = w_s[h] * keep + jnp.sum(e * dp, axis=0, keepdims=True)
                    m_s[h] = m_new
                    mb_s[kb * GROUP + h] = m_new
                    e_s[kb * GROUP + h] = e
                    dp_s[kb * GROUP + h] = dp

            return 0

        lax.fori_loop(0, BLOCKS, phase_a, 0)

        def phase_b(j, _):
            kb, _, live = locate(j)

            @pl.when(live)
            def _():
                kt = kt_s[kb]
                dv = None
                dk = None
                for h in range(GROUP):
                    inverse = 1.0 / l_s[h]
                    grad_dot = w_s[h] * inverse
                    alpha = jnp.exp2(mb_s[kb * GROUP + h] - m_s[h]) * inverse
                    p = e_s[kb * GROUP + h] * alpha
                    ds = (p * (dp_s[kb * GROUP + h] - grad_dot)).astype(jnp.bfloat16)
                    dv_h = nn(p.astype(jnp.bfloat16), g_s[qb * GROUP + h])
                    dk_h = nn(ds, q_s[qb * GROUP + h])
                    dv = dv_h if dv is None else dv + dv_h
                    dk = dk_h if dk is None else dk + dk_h
                    dqt_s[h] += nn(kt, ds)
                dv_s[kb] += dv
                dk_s[kb] += dk

            return 0

        lax.fori_loop(0, BLOCKS, phase_b, 0)

        @pl.when(qb == 0)
        def _():
            for h in range(GROUP):
                own_dq[:, h * HD : (h + 1) * HD] = dqt_s[h].T.astype(own_dq.dtype)

        @pl.when(qb == 1)
        def _():
            for h in range(GROUP):
                sib_dq[:, h * HD : (h + 1) * HD] = dqt_s[h].T.astype(sib_dq.dtype)

        return 0

    lax.fori_loop(0, 2, per_q, 0)
    for d, out in enumerate((out0, out1, out2)):
        for p in range(2):
            out[p, 0] = dk_s[2 * d + p].astype(out.dtype)
            out[p, 1] = dv_s[2 * d + p].astype(out.dtype)


def grads_call(head, where, lengths, loss_mask, token, query_rows, out_grad, got_qg, kv0, kv1, kv2):
    rows = query_rows.shape[1]
    wide = GROUP * HD
    own = column_block(rows, wide, lambda i: (i & 1) * MINE + head)
    got = pl.BlockSpec((2, rows, wide), lambda i, w: (0, 0, head))
    f32 = jnp.float32
    bf16 = jnp.bfloat16
    pair = 2 * GROUP
    tiles = BLOCKS * GROUP
    tile_work = 2 * rows * rows * HD
    return pl.pallas_call(
        grads_kernel,
        grid_spec=pltpu.PrefetchScalarGridSpec(
            num_scalar_prefetch=1,
            grid=(1,),
            in_specs=[
                pl.BlockSpec(memory_space=pltpu.SMEM),
                in_vmem(), in_vmem(), own, own, got, in_vmem(), in_vmem(), in_vmem(),
            ],
            out_specs=[in_vmem() for _ in range(6)],
            scratch_shapes=[
                pltpu.VMEM((pair, rows, HD), bf16),
                pltpu.VMEM((pair, rows, HD), bf16),
                pltpu.VMEM((BLOCKS, rows, HD), bf16),
                pltpu.VMEM((BLOCKS, rows, HD), bf16),
                pltpu.VMEM((BLOCKS, HD, rows), bf16),
                pltpu.VMEM((tiles, rows, rows), f32),
                pltpu.VMEM((tiles, rows, rows), f32),
                pltpu.VMEM((tiles, 1, rows), f32),
                pltpu.VMEM((GROUP, 1, rows), f32),
                pltpu.VMEM((GROUP, 1, rows), f32),
                pltpu.VMEM((GROUP, 1, rows), f32),
                pltpu.VMEM((GROUP, HD, rows), f32),
                pltpu.VMEM((BLOCKS, rows, HD), f32),
                pltpu.VMEM((BLOCKS, rows, HD), f32),
            ],
        ),
        out_shape=[
            jax.ShapeDtypeStruct((rows, wide), bf16),
            jax.ShapeDtypeStruct((rows, wide), bf16),
            jax.ShapeDtypeStruct((2, 2, rows, HD), f32),
            jax.ShapeDtypeStruct((2, 2, rows, HD), bf16),
            jax.ShapeDtypeStruct((2, 2, rows, HD), bf16),
            jax.ShapeDtypeStruct((8, HD), f32),
        ],
        compiler_params=pltpu.CompilerParams(vmem_limit_bytes=26 * 1024 * 1024),
        name="grads",
        cost_estimate=pl.CostEstimate(
            flops=5 * 6 * GROUP * tile_work, transcendentals=6 * GROUP * rows * rows,
            bytes_accessed=6 * 1024 * 1024,
        ),
    )(where, lengths, loss_mask, token, query_rows, out_grad, got_qg, kv0, kv1, kv2)


def work(query_rows, key_rows, value_rows, out_grad, lengths, loss_mask):
    rows = query_rows.shape[1]
    numerator = float(lax.axis_size("dp") * rows * lax.axis_size("ctx"))
    where = lax.axis_index("ctx").astype(jnp.int32).reshape(1)

    give_kv = give_kv_call(where, key_rows, value_rows)
    got_kv = swapped(give_kv, 1)
    give_qg, token = give_qg_call(where, query_rows, out_grad, loss_mask, give_kv)
    got_qg = swapped(give_qg, 1)
    local = local_kv_call(where, key_rows, value_rows, got_kv)
    near = []
    far = []
    for kv in local:
        near.append(shifted(kv, 2))
        far.append(shifted(kv, 4))

    own_dq = []
    got_dq = []
    parts = []
    for h in range(MINE):
        dq_o, dq_s, d0, d1, d2, token = grads_call(
            h, where, lengths, loss_mask, token, query_rows, out_grad, got_qg,
            local[h], near[h], far[h],
        )
        own_dq.append(dq_o)
        r1 = shifted(d1, -2)
        r2 = shifted(d2, -4)
        parts.append((d0, r1, r2))
        got_dq.append(swapped(dq_s, 1))
    count = everywhere_sum(token)
    query_grad, count = finish_q_call(where, numerator, own_dq, got_dq, count)
    own_total, give_total = total_call(where, numerator, parts, count)
    key_grad, value_grad = finish_kv_call(where, own_total, swapped(give_total, 1))
    return query_grad, key_grad, value_grad


def solution(mesh):
    placed = (
        P("dp", "ctx", None),
        P("dp", "ctx", None),
        P("dp", "ctx", None),
        P("dp", "ctx", None),
        P("dp", None),
        P("dp", "ctx"),
    )
    return jax.shard_map(
        work,
        mesh=mesh,
        in_specs=placed,
        out_specs=(P("dp", "ctx", None), P("dp", "ctx", None), P("dp", "ctx", None)),
        check_vma=False,
    )
```

profile of v0, /device:TPU:0, one launch (start us, length us, event | category | flops | bytes accessed | tf_op | source)
XLA Modules:
  0.0 93.5 jit_solution(3359198253890505407)
XLA Ops:
  0.6 0.9 %copy-done.4 = bf16[1,256,512]{2,1,0:T(8,128)(2,1)S(1)} copy-done((bf16[1,256,512]{2,1,0:T(8,128)(2,1)S(1)}, bf16[1,256,512]{2,1,0:T(8,128)(2,1)}, u32[]{:S(2)}) %copy-start.4) | copy-done | bytes 262168
  1.6 0.9 %copy-done.5 = bf16[1,256,512]{2,1,0:T(8,128)(2,1)S(1)} copy-done((bf16[1,256,512]{2,1,0:T(8,128)(2,1)S(1)}, bf16[1,256,512]{2,1,0:T(8,128)(2,1)}, u32[]{:S(2)}) %copy-start.5) | copy-done | bytes 262168
  2.5 0.1 shard_map.85.after_ref
  2.6 0.6 copy-done.7
  3.2 1.2 %copy-done = bf16[1,256,2048]{2,1,0:T(8,128)(2,1)S(1)} copy-done((bf16[1,256,2048]{2,1,0:T(8,128)(2,1)S(1)}, bf16[1,256,2048]{2,1,0:T(8,128)(2,1)}, u32[]{:S(2)}) %copy-start) | copy-done | bytes 1048600
  4.4 1.2 %copy-done.2 = bf16[1,256,2048]{2,1,0:T(8,128)(2,1)S(1)} copy-done((bf16[1,256,2048]{2,1,0:T(8,128)(2,1)S(1)}, bf16[1,256,2048]{2,1,0:T(8,128)(2,1)}, u32[]{:S(2)}) %copy-start.2) | copy-done | bytes 1048600
  5.7 0.2 shard_map.86
  5.9 0.6 collective-permute-start
  6.4 0.1 collective-permute-start.1
  6.5 2.6 %collective-permute-done.1.got = bf16[2,2,256,128]{3,2,1,0:T(8,128)(2,1)S(1)} collective-permute-done((bf16[2,2,256,128]{3,2,1,0:T(8,128)(2,1)S(1)}, bf16[2,2,256,128]{3,2,1,0:T(8,128)(2,1)S(1)}, u32[]{:S(2)}, u32[]{:S(2)}) %collective-permute-start.1) | collective-permute-done | bytes 262176 | tf_op jit(solution)/shard_map/ppermute | solution.py:29
  9.1 0.1 shard_map.87
  9.2 4.9 %collective-permute-start.3 = (bf16[2,2,256,128]{3,2,1,0:T(8,128)(2,1)S(1)}, bf16[2,2,256,128]{3,2,1,0:T(8,128)(2,1)S(1)}, u32[]{:S(2)}, u32[]{:S(2)}) collective-permute-start(bf16[2,2,256,128]{3,2,1,0:T(8,128)(2,1)S(1)} %get-tuple-element.27.kv0), channel_id=1, source_target_pairs={{0,4},{1,5},{2,6},{3,7},{4,8},{5,9},{6,10},{7,11},{8,12},{9,13},{1... | collective-permute-start | bytes 786440 | tf_op jit(solution)/shard_map/ppermute | solution.py:24
  14.0 3.4 %collective-permute-start.2 = (bf16[2,2,256,128]{3,2,1,0:T(8,128)(2,1)S(1)}, bf16[2,2,256,128]{3,2,1,0:T(8,128)(2,1)S(1)}, u32[]{:S(2)}, u32[]{:S(2)}) collective-permute-start(bf16[2,2,256,128]{3,2,1,0:T(8,128)(2,1)S(1)} %get-tuple-element.27.kv0), channel_id=1, source_target_pairs={{0,2},{1,3},{2,4},{3,5},{4,6},{5,7},{6,8},{7,9},{8,10},{9,11},{10,... | collective-permute-start | bytes 786440 | tf_op jit(solution)/shard_map/ppermute | solution.py:24
  17.5 0.0 copy-start.8
  17.5 3.5 %collective-permute-start.5 = (bf16[2,2,256,128]{3,2,1,0:T(8,128)(2,1)S(1)}, bf16[2,2,256,128]{3,2,1,0:T(8,128)(2,1)S(1)}, u32[]{:S(2)}, u32[]{:S(2)}) collective-permute-start(bf16[2,2,256,128]{3,2,1,0:T(8,128)(2,1)S(1)} %get-tuple-element.30.kv0), channel_id=1, source_target_pairs={{0,4},{1,5},{2,6},{3,7},{4,8},{5,9},{6,10},{7,11},{8,12},{9,13},{1... | collective-permute-start | bytes 786440 | tf_op jit(solution)/shard_map/ppermute | solution.py:24
  21.0 3.4 %collective-permute-start.4 = (bf16[2,2,256,128]{3,2,1,0:T(8,128)(2,1)S(1)}, bf16[2,2,256,128]{3,2,1,0:T(8,128)(2,1)S(1)}, u32[]{:S(2)}, u32[]{:S(2)}) collective-permute-start(bf16[2,2,256,128]{3,2,1,0:T(8,128)(2,1)S(1)} %get-tuple-element.30.kv0), channel_id=1, source_target_pairs={{0,2},{1,3},{2,4},{3,5},{4,6},{5,7},{6,8},{7,9},{8,10},{9,11},{10,... | collective-permute-start | bytes 786440 | tf_op jit(solution)/shard_map/ppermute | solution.py:24
  24.4 0.0 collective-permute-done.3.kv2
  24.4 0.0 collective-permute-done.2.kv1
  24.4 0.0 collective-permute-done.got_qg
  24.5 5.2 %grads.2 = (bf16[256,512]{1,0:T(8,128)(2,1)S(1)}, bf16[256,512]{1,0:T(8,128)(2,1)S(1)}, f32[2,2,256,128]{3,2,1,0:T(8,128)S(1)}, bf16[2,2,256,128]{3,2,1,0:T(8,12...) custom-call(s32[1]{0:T(128)} %bitcast.where_ref, s32[1,8]{1,0:T(1,128)S(1)} %copy-done.8, ...), custom_call_target="tpu_custom_call" | custom-call | flops 2013265920 | bytes 6291456 | tf_op jit(solution)/shard_map/grads/pallas_call | solution.py:337
  29.7 0.0 collective-permute-done.4.kv1
  29.7 5.2 %grads.3 = (bf16[256,512]{1,0:T(8,128)(2,1)S(1)}, bf16[256,512]{1,0:T(8,128)(2,1)S(1)}, f32[2,2,256,128]{3,2,1,0:T(8,128)S(1)}, bf16[2,2,256,128]{3,2,1,0:T(8,12...) custom-call(s32[1]{0:T(128)} %bitcast.where_ref, s32[1,8]{1,0:T(1,128)S(1)} %copy-done.8, ...), custom_call_target="tpu_custom_call" | custom-call | flops 2013265920 | bytes 6291456 | tf_op jit(solution)/shard_map/grads/pallas_call | solution.py:337
  35.0 0.1 collective-permute-start.7
  35.0 1.6 %collective-permute-start.8 = (f32[8,128]{1,0:T(8,128)S(1)}, f32[8,128]{1,0:T(8,128)S(1)}, u32[]{:S(2)}, u32[]{:S(2)}) collective-permute-start(f32[8,128]{1,0:T(8,128)S(1)} %get-tuple-element.34), channel_id=1, source_target_pairs={{0,16},{16,0},{1,17},{17,1},{2,18},{18,2},{3,19},{19,3},{4,20},{20... | collective-permute-start | bytes 12296 | tf_op jit(solution)/shard_map/ppermute | solution.py:36
  36.6 2.1 %collective-permute-done.8 = f32[8,128]{1,0:T(8,128)S(1)} collective-permute-done((f32[8,128]{1,0:T(8,128)S(1)}, f32[8,128]{1,0:T(8,128)S(1)}, u32[]{:S(2)}, u32[]{:S(2)}) %collective-permute-start.8) | collective-permute-done | bytes 4128 | tf_op jit(solution)/shard_map/ppermute | solution.py:36
  38.7 0.0 collective-permute-start.9
  38.7 1.2 %collective-permute-done.9 = f32[8,128]{1,0:T(8,128)S(1)} collective-permute-done((f32[8,128]{1,0:T(8,128)S(1)}, f32[8,128]{1,0:T(8,128)S(1)}, u32[]{:S(2)}, u32[]{:S(2)}) %collective-permute-start.9) | collective-permute-done | bytes 4128 | tf_op jit(solution)/shard_map/ppermute | solution.py:29
  39.9 12.2 %collective-permute-start.10 = (f32[8,128]{1,0:T(8,128)S(1)}, f32[8,128]{1,0:T(8,128)S(1)}, u32[]{:S(2)}, u32[]{:S(2)}) collective-permute-start(f32[8,128]{1,0:T(8,128)S(1)} %add.16), channel_id=1, source_target_pairs={{0,2},{1,3},{2,0},{3,1},{4,6},{5,7},{6,4},{7,5},{8,10},{9,11},{10,... | collective-permute-start | bytes 12296 | tf_op jit(solution)/shard_map/ppermute | solution.py:29
  52.1 1.6 %collective-permute-done.10 = f32[8,128]{1,0:T(8,128)S(1)} collective-permute-done((f32[8,128]{1,0:T(8,128)S(1)}, f32[8,128]{1,0:T(8,128)S(1)}, u32[]{:S(2)}, u32[]{:S(2)}) %collective-permute-start.10) | collective-permute-done | bytes 4128 | tf_op jit(solution)/shard_map/ppermute | solution.py:29
  53.7 5.0 %collective-permute-start.11 = (f32[8,128]{1,0:T(8,128)S(1)}, f32[8,128]{1,0:T(8,128)S(1)}, u32[]{:S(2)}, u32[]{:S(2)}) collective-permute-start(f32[8,128]{1,0:T(8,128)S(1)} %add.17), channel_id=1, source_target_pairs={{0,4},{1,5},{2,6},{3,7},{4,0},{5,1},{6,2},{7,3},{8,12},{9,13},{10,... | collective-permute-start | bytes 12296 | tf_op jit(solution)/shard_map/ppermute | solution.py:29
  58.7 1.6 %collective-permute-done.11 = f32[8,128]{1,0:T(8,128)S(1)} collective-permute-done((f32[8,128]{1,0:T(8,128)S(1)}, f32[8,128]{1,0:T(8,128)S(1)}, u32[]{:S(2)}, u32[]{:S(2)}) %collective-permute-start.11) | collective-permute-done | bytes 4128 | tf_op jit(solution)/shard_map/ppermute | solution.py:29
  60.3 5.9 %collective-permute-start.12 = (f32[8,128]{1,0:T(8,128)S(1)}, f32[8,128]{1,0:T(8,128)S(1)}, u32[]{:S(2)}, u32[]{:S(2)}) collective-permute-start(f32[8,128]{1,0:T(8,128)S(1)} %add.18), channel_id=1, source_target_pairs={{0,8},{1,9},{2,10},{3,11},{4,12},{5,13},{6,14},{7,15},{8,0},{9,1},... | collective-permute-start | bytes 12296 | tf_op jit(solution)/shard_map/ppermute | solution.py:29
  66.2 1.3 %collective-permute-start.15 = (bf16[2,2,256,128]{3,2,1,0:T(8,128)(2,1)S(1)}, bf16[2,2,256,128]{3,2,1,0:T(8,128)(2,1)S(1)}, u32[]{:S(2)}, u32[]{:S(2)}) collective-permute-start(bf16[2,2,256,128]{3,2,1,0:T(8,128)(2,1)S(1)} %get-tuple-element.40), channel_id=1, source_target_pairs={{2,0},{3,1},{4,2},{5,3},{6,4},{7,5},{8,6},{9,7},{10,8},{11,9},{12,... | collective-permute-start | bytes 786440 | tf_op jit(solution)/shard_map/ppermute | solution.py:24
  67.5 0.1 collective-permute-start.6
  67.6 1.3 %collective-permute-start.16 = (bf16[2,2,256,128]{3,2,1,0:T(8,128)(2,1)S(1)}, bf16[2,2,256,128]{3,2,1,0:T(8,128)(2,1)S(1)}, u32[]{:S(2)}, u32[]{:S(2)}) collective-permute-start(bf16[2,2,256,128]{3,2,1,0:T(8,128)(2,1)S(1)} %get-tuple-element.41), channel_id=1, source_target_pairs={{4,0},{5,1},{6,2},{7,3},{8,4},{9,5},{10,6},{11,7},{12,8},{13,9},{1... | collective-permute-start | bytes 786440 | tf_op jit(solution)/shard_map/ppermute | solution.py:24
  68.9 0.0 collective-permute-done.12
  68.9 1.3 %collective-permute-start.13 = (bf16[2,2,256,128]{3,2,1,0:T(8,128)(2,1)S(1)}, bf16[2,2,256,128]{3,2,1,0:T(8,128)(2,1)S(1)}, u32[]{:S(2)}, u32[]{:S(2)}) collective-permute-start(bf16[2,2,256,128]{3,2,1,0:T(8,128)(2,1)S(1)} %get-tuple-element.37), channel_id=1, source_target_pairs={{2,0},{3,1},{4,2},{5,3},{6,4},{7,5},{8,6},{9,7},{10,8},{11,9},{12,... | collective-permute-start | bytes 786440 | tf_op jit(solution)/shard_map/ppermute | solution.py:24
  70.2 0.0 collective-permute-done.7.refs_3_
  70.2 1.3 %collective-permute-start.14 = (bf16[2,2,256,128]{3,2,1,0:T(8,128)(2,1)S(1)}, bf16[2,2,256,128]{3,2,1,0:T(8,128)(2,1)S(1)}, u32[]{:S(2)}, u32[]{:S(2)}) collective-permute-start(bf16[2,2,256,128]{3,2,1,0:T(8,128)(2,1)S(1)} %get-tuple-element.38), channel_id=1, source_target_pairs={{4,0},{5,1},{6,2},{7,3},{8,4},{9,5},{10,6},{11,7},{12,8},{13,9},{1... | collective-permute-start | bytes 786440 | tf_op jit(solution)/shard_map/ppermute | solution.py:24
  71.6 1.3 %shard_map.88 = (bf16[1,256,2048]{2,1,0:T(8,128)(2,1)}, f32[8,128]{1,0:T(8,128)S(1)}) custom-call(s32[1]{0:T(128)} %bitcast.where_ref, bf16[256,512]{1,0:T(8,128)(2,1)S(1)} %get-tuple-element.28.refs_0_, bf16[256,512]{1,0:T(8,128)(2,1)S(1)} %get-tuple-element.31.refs_1_, bf16[256,512]{1,0:T(8,128)(2,1)S(1)} %collective-permute-done.6.refs_2_, ...), custom_call_target="tpu_custom_call" | custom-call | bytes 1048576 | tf_op jit(solution)/shard_map/pallas_call | solution.py:67
  72.8 1.7 %collective-permute-done.15.refs_4_ = bf16[2,2,256,128]{3,2,1,0:T(8,128)(2,1)S(1)} collective-permute-done((bf16[2,2,256,128]{3,2,1,0:T(8,128)(2,1)S(1)}, bf16[2,2,256,128]{3,2,1,0:T(8,128)(2,1)S(1)}, u32[]{:S(2)}, u32[]{:S(2)}) %collective-permute-start.15) | collective-permute-done | bytes 262176 | tf_op jit(solution)/shard_map/ppermute | solution.py:24
  74.5 6.1 %collective-permute-done.16.refs_5_ = bf16[2,2,256,128]{3,2,1,0:T(8,128)(2,1)S(1)} collective-permute-done((bf16[2,2,256,128]{3,2,1,0:T(8,128)(2,1)S(1)}, bf16[2,2,256,128]{3,2,1,0:T(8,128)(2,1)S(1)}, u32[]{:S(2)}, u32[]{:S(2)}) %collective-permute-start.16) | collective-permute-done | bytes 262176 | tf_op jit(solution)/shard_map/ppermute | solution.py:24
  80.6 0.0 collective-permute-done.13.refs_1_
  80.6 10.2 %collective-permute-done.14.refs_2_ = bf16[2,2,256,128]{3,2,1,0:T(8,128)(2,1)S(1)} collective-permute-done((bf16[2,2,256,128]{3,2,1,0:T(8,128)(2,1)S(1)}, bf16[2,2,256,128]{3,2,1,0:T(8,128)(2,1)S(1)}, u32[]{:S(2)}, u32[]{:S(2)}) %collective-permute-start.14) | collective-permute-done | bytes 262176 | tf_op jit(solution)/shard_map/ppermute | solution.py:24
  90.8 0.2 shard_map.89
  91.0 0.1 collective-permute-start.17
  91.1 1.5 %collective-permute-done.17.got_ref = bf16[2,2,256,128]{3,2,1,0:T(8,128)(2,1)S(1)} collective-permute-done((bf16[2,2,256,128]{3,2,1,0:T(8,128)(2,1)S(1)}, bf16[2,2,256,128]{3,2,1,0:T(8,128)(2,1)S(1)}, u32[]{:S(2)}, u32[]{:S(2)}) %collective-permute-start.17) | collective-permute-done | bytes 262176 | tf_op jit(solution)/shard_map/ppermute | solution.py:29
  92.6 0.9 shard_map.90
  (19 shorter events, 0.0 us)
Async XLA Ops:
  0.6 1.0 %copy-start.4 = (bf16[1,256,512]{2,1,0:T(8,128)(2,1)S(1)}, bf16[1,256,512]{2,1,0:T(8,128)(2,1)}, u32[]{:S(2)}) copy-start(bf16[1,256,512]{2,1,0:T(8,128)(2,1)} %k_ref.3) | copy-start | bytes 786436
  1.6 0.9 %copy-start.5 = (bf16[1,256,512]{2,1,0:T(8,128)(2,1)S(1)}, bf16[1,256,512]{2,1,0:T(8,128)(2,1)}, u32[]{:S(2)}) copy-start(bf16[1,256,512]{2,1,0:T(8,128)(2,1)} %v_ref.3) | copy-start | bytes 786436
  2.5 0.7 copy-start.7
  3.2 1.2 %copy-start = (bf16[1,256,2048]{2,1,0:T(8,128)(2,1)S(1)}, bf16[1,256,2048]{2,1,0:T(8,128)(2,1)}, u32[]{:S(2)}) copy-start(bf16[1,256,2048]{2,1,0:T(8,128)(2,1)} %own_q.3) | copy-start | bytes 3145732
  4.4 1.2 %copy-start.2 = (bf16[1,256,2048]{2,1,0:T(8,128)(2,1)S(1)}, bf16[1,256,2048]{2,1,0:T(8,128)(2,1)}, u32[]{:S(2)}) copy-start(bf16[1,256,2048]{2,1,0:T(8,128)(2,1)} %own_g.3) | copy-start | bytes 3145732
  5.7 3.4 %copy-start.6 = (bf16[1,256,512]{2,1,0:T(8,128)(2,1)S(1)}, bf16[1,256,512]{2,1,0:T(8,128)(2,1)}, u32[]{:S(2)}) copy-start(bf16[1,256,512]{2,1,0:T(8,128)(2,1)} %v_ref.3) | copy-start | bytes 786436
  5.7 18.8 %copy-start.1 = (bf16[1,256,2048]{2,1,0:T(8,128)(2,1)S(1)}, bf16[1,256,2048]{2,1,0:T(8,128)(2,1)}, u32[]{:S(2)}) copy-start(bf16[1,256,2048]{2,1,0:T(8,128)(2,1)} %own_q.3) | copy-start | bytes 3145732
  5.7 18.8 %copy-start.3 = (bf16[1,256,2048]{2,1,0:T(8,128)(2,1)S(1)}, bf16[1,256,2048]{2,1,0:T(8,128)(2,1)}, u32[]{:S(2)}) copy-start(bf16[1,256,2048]{2,1,0:T(8,128)(2,1)} %own_g.3) | copy-start | bytes 3145732
  5.9 18.6 %collective-permute-start = (bf16[2,256,1024]{2,1,0:T(8,128)(2,1)S(1)}, bf16[2,256,1024]{2,1,0:T(8,128)(2,1)S(1)}, u32[]{:S(2)}, u32[]{:S(2)}) collective-permute-start(bf16[2,256,1024]{2,1,0:T(8,128)(2,1)S(1)} %get-tuple-element.26), channel_id=1, source_target_pairs={{0,1},{1,0},{2,3},{3,2},{4,5},{5,4},{6,7},{7,6},{8,9},{9,8},{10,11... | collective-permute-start | bytes 3145736 | tf_op jit(solution)/shard_map/ppermute | solution.py:29
  6.4 2.7 %collective-permute-start.1 = (bf16[2,2,256,128]{3,2,1,0:T(8,128)(2,1)S(1)}, bf16[2,2,256,128]{3,2,1,0:T(8,128)(2,1)S(1)}, u32[]{:S(2)}, u32[]{:S(2)}) collective-permute-start(bf16[2,2,256,128]{3,2,1,0:T(8,128)(2,1)S(1)} %shard_map.85.after_ref), channel_id=1, source_target_pairs={{0,1},{1,0},{2,3},{3,2},{4,5},{5,4},{6,7},{7,6},{8,9},{9,8},{10,11... | collective-permute-start | bytes 786440 | tf_op jit(solution)/shard_map/ppermute | solution.py:29
  9.2 15.3 %collective-permute-start.3 = (bf16[2,2,256,128]{3,2,1,0:T(8,128)(2,1)S(1)}, bf16[2,2,256,128]{3,2,1,0:T(8,128)(2,1)S(1)}, u32[]{:S(2)}, u32[]{:S(2)}) collective-permute-start(bf16[2,2,256,128]{3,2,1,0:T(8,128)(2,1)S(1)} %get-tuple-element.27.kv0), channel_id=1, source_target_pairs={{0,4},{1,5},{2,6},{3,7},{4,8},{5,9},{6,10},{7,11},{8,12},{9,13},{1... | collective-permute-start | bytes 786440 | tf_op jit(solution)/shard_map/ppermute | solution.py:24
  14.0 10.4 %collective-permute-start.2 = (bf16[2,2,256,128]{3,2,1,0:T(8,128)(2,1)S(1)}, bf16[2,2,256,128]{3,2,1,0:T(8,128)(2,1)S(1)}, u32[]{:S(2)}, u32[]{:S(2)}) collective-permute-start(bf16[2,2,256,128]{3,2,1,0:T(8,128)(2,1)S(1)} %get-tuple-element.27.kv0), channel_id=1, source_target_pairs={{0,2},{1,3},{2,4},{3,5},{4,6},{5,7},{6,8},{7,9},{8,10},{9,11},{10,... | collective-permute-start | bytes 786440 | tf_op jit(solution)/shard_map/ppermute | solution.py:24
  17.5 7.0 %copy-start.8 = (s32[1,8]{1,0:T(1,128)S(1)}, s32[1,8]{1,0:T(1,128)}, u32[]{:S(2)}) copy-start(s32[1,8]{1,0:T(1,128)} %lengths_ref.3) | copy-start | bytes 100
  17.5 12.2 %collective-permute-start.5 = (bf16[2,2,256,128]{3,2,1,0:T(8,128)(2,1)S(1)}, bf16[2,2,256,128]{3,2,1,0:T(8,128)(2,1)S(1)}, u32[]{:S(2)}, u32[]{:S(2)}) collective-permute-start(bf16[2,2,256,128]{3,2,1,0:T(8,128)(2,1)S(1)} %get-tuple-element.30.kv0), channel_id=1, source_target_pairs={{0,4},{1,5},{2,6},{3,7},{4,8},{5,9},{6,10},{7,11},{8,12},{9,13},{1... | collective-permute-start | bytes 786440 | tf_op jit(solution)/shard_map/ppermute | solution.py:24
  21.0 8.8 %collective-permute-start.4 = (bf16[2,2,256,128]{3,2,1,0:T(8,128)(2,1)S(1)}, bf16[2,2,256,128]{3,2,1,0:T(8,128)(2,1)S(1)}, u32[]{:S(2)}, u32[]{:S(2)}) collective-permute-start(bf16[2,2,256,128]{3,2,1,0:T(8,128)(2,1)S(1)} %get-tuple-element.30.kv0), channel_id=1, source_target_pairs={{0,2},{1,3},{2,4},{3,5},{4,6},{5,7},{6,8},{7,9},{8,10},{9,11},{10,... | collective-permute-start | bytes 786440 | tf_op jit(solution)/shard_map/ppermute | solution.py:24
  35.0 35.3 %collective-permute-start.7 = (bf16[256,512]{1,0:T(8,128)(2,1)S(1)}, bf16[256,512]{1,0:T(8,128)(2,1)S(1)}, u32[]{:S(2)}, u32[]{:S(2)}) collective-permute-start(bf16[256,512]{1,0:T(8,128)(2,1)S(1)} %get-tuple-element.33), channel_id=1, source_target_pairs={{0,1},{1,0},{2,3},{3,2},{4,5},{5,4},{6,7},{7,6},{8,9},{9,8},{10,11... | collective-permute-start | bytes 786440 | tf_op jit(solution)/shard_map/ppermute | solution.py:29
  35.0 3.7 %collective-permute-start.8 = (f32[8,128]{1,0:T(8,128)S(1)}, f32[8,128]{1,0:T(8,128)S(1)}, u32[]{:S(2)}, u32[]{:S(2)}) collective-permute-start(f32[8,128]{1,0:T(8,128)S(1)} %get-tuple-element.34), channel_id=1, source_target_pairs={{0,16},{16,0},{1,17},{17,1},{2,18},{18,2},{3,19},{19,3},{4,20},{20... | collective-permute-start | bytes 12296 | tf_op jit(solution)/shard_map/ppermute | solution.py:36
  38.7 1.2 %collective-permute-start.9 = (f32[8,128]{1,0:T(8,128)S(1)}, f32[8,128]{1,0:T(8,128)S(1)}, u32[]{:S(2)}, u32[]{:S(2)}) collective-permute-start(f32[8,128]{1,0:T(8,128)S(1)} %add.15), channel_id=1, source_target_pairs={{0,1},{1,0},{2,3},{3,2},{4,5},{5,4},{6,7},{7,6},{8,9},{9,8},{10,11... | collective-permute-start | bytes 12296 | tf_op jit(solution)/shard_map/ppermute | solution.py:29
  39.9 13.8 %collective-permute-start.10 = (f32[8,128]{1,0:T(8,128)S(1)}, f32[8,128]{1,0:T(8,128)S(1)}, u32[]{:S(2)}, u32[]{:S(2)}) collective-permute-start(f32[8,128]{1,0:T(8,128)S(1)} %add.16), channel_id=1, source_target_pairs={{0,2},{1,3},{2,0},{3,1},{4,6},{5,7},{6,4},{7,5},{8,10},{9,11},{10,... | collective-permute-start | bytes 12296 | tf_op jit(solution)/shard_map/ppermute | solution.py:29
  53.7 6.6 %collective-permute-start.11 = (f32[8,128]{1,0:T(8,128)S(1)}, f32[8,128]{1,0:T(8,128)S(1)}, u32[]{:S(2)}, u32[]{:S(2)}) collective-permute-start(f32[8,128]{1,0:T(8,128)S(1)} %add.17), channel_id=1, source_target_pairs={{0,4},{1,5},{2,6},{3,7},{4,0},{5,1},{6,2},{7,3},{8,12},{9,13},{10,... | collective-permute-start | bytes 12296 | tf_op jit(solution)/shard_map/ppermute | solution.py:29
  60.3 8.6 %collective-permute-start.12 = (f32[8,128]{1,0:T(8,128)S(1)}, f32[8,128]{1,0:T(8,128)S(1)}, u32[]{:S(2)}, u32[]{:S(2)}) collective-permute-start(f32[8,128]{1,0:T(8,128)S(1)} %add.18), channel_id=1, source_target_pairs={{0,8},{1,9},{2,10},{3,11},{4,12},{5,13},{6,14},{7,15},{8,0},{9,1},... | collective-permute-start | bytes 12296 | tf_op jit(solution)/shard_map/ppermute | solution.py:29
  66.2 8.3 %collective-permute-start.15 = (bf16[2,2,256,128]{3,2,1,0:T(8,128)(2,1)S(1)}, bf16[2,2,256,128]{3,2,1,0:T(8,128)(2,1)S(1)}, u32[]{:S(2)}, u32[]{:S(2)}) collective-permute-start(bf16[2,2,256,128]{3,2,1,0:T(8,128)(2,1)S(1)} %get-tuple-element.40), channel_id=1, source_target_pairs={{2,0},{3,1},{4,2},{5,3},{6,4},{7,5},{8,6},{9,7},{10,8},{11,9},{12,... | collective-permute-start | bytes 786440 | tf_op jit(solution)/shard_map/ppermute | solution.py:24
  67.5 4.0 %collective-permute-start.6 = (bf16[256,512]{1,0:T(8,128)(2,1)S(1)}, bf16[256,512]{1,0:T(8,128)(2,1)S(1)}, u32[]{:S(2)}, u32[]{:S(2)}) collective-permute-start(bf16[256,512]{1,0:T(8,128)(2,1)S(1)} %get-tuple-element.32), channel_id=1, source_target_pairs={{0,1},{1,0},{2,3},{3,2},{4,5},{5,4},{6,7},{7,6},{8,9},{9,8},{10,11... | collective-permute-start | bytes 786440 | tf_op jit(solution)/shard_map/ppermute | solution.py:29
  67.6 12.9 %collective-permute-start.16 = (bf16[2,2,256,128]{3,2,1,0:T(8,128)(2,1)S(1)}, bf16[2,2,256,128]{3,2,1,0:T(8,128)(2,1)S(1)}, u32[]{:S(2)}, u32[]{:S(2)}) collective-permute-start(bf16[2,2,256,128]{3,2,1,0:T(8,128)(2,1)S(1)} %get-tuple-element.41), channel_id=1, source_target_pairs={{4,0},{5,1},{6,2},{7,3},{8,4},{9,5},{10,6},{11,7},{12,8},{13,9},{1... | collective-permute-start | bytes 786440 | tf_op jit(solution)/shard_map/ppermute | solution.py:24
  68.9 11.6 %collective-permute-start.13 = (bf16[2,2,256,128]{3,2,1,0:T(8,128)(2,1)S(1)}, bf16[2,2,256,128]{3,2,1,0:T(8,128)(2,1)S(1)}, u32[]{:S(2)}, u32[]{:S(2)}) collective-permute-start(bf16[2,2,256,128]{3,2,1,0:T(8,128)(2,1)S(1)} %get-tuple-element.37), channel_id=1, source_target_pairs={{2,0},{3,1},{4,2},{5,3},{6,4},{7,5},{8,6},{9,7},{10,8},{11,9},{12,... | collective-permute-start | bytes 786440 | tf_op jit(solution)/shard_map/ppermute | solution.py:24
  70.2 20.6 %collective-permute-start.14 = (bf16[2,2,256,128]{3,2,1,0:T(8,128)(2,1)S(1)}, bf16[2,2,256,128]{3,2,1,0:T(8,128)(2,1)S(1)}, u32[]{:S(2)}, u32[]{:S(2)}) collective-permute-start(bf16[2,2,256,128]{3,2,1,0:T(8,128)(2,1)S(1)} %get-tuple-element.38), channel_id=1, source_target_pairs={{4,0},{5,1},{6,2},{7,3},{8,4},{9,5},{10,6},{11,7},{12,8},{13,9},{1... | collective-permute-start | bytes 786440 | tf_op jit(solution)/shard_map/ppermute | solution.py:24
  91.0 1.6 %collective-permute-start.17 = (bf16[2,2,256,128]{3,2,1,0:T(8,128)(2,1)S(1)}, bf16[2,2,256,128]{3,2,1,0:T(8,128)(2,1)S(1)}, u32[]{:S(2)}, u32[]{:S(2)}) collective-permute-start(bf16[2,2,256,128]{3,2,1,0:T(8,128)(2,1)S(1)} %get-tuple-element.44), channel_id=1, source_target_pairs={{0,1},{1,0},{2,3},{3,2},{4,5},{5,4},{6,7},{7,6},{8,9},{9,8},{10,11... | collective-permute-start | bytes 786440 | tf_op jit(solution)/shard_map/ppermute | solution.py:29
where the time goes:
time: 93.9 us; the launch traced here: 93.5 us
  starting transfers between devices  45.9 us (49%)
  waiting for transfers between devices  28.5 us (30%)
  Pallas kernels  13.1 us (14%)
  local copies, waits for them, and re-layouts  4.97 us (5%)
    ppermute x9, starting transfers between devices, swapped(): return lax.ppermute(value, 'ctx', [(i, i ^ bit) for i in range(count)])  24 us
    ppermute x8, starting transfers between devices, shifted(): return lax.ppermute(value, 'ctx', pairs)  20.4 us
    ppermute x8, waiting for transfers between devices, shifted(): return lax.ppermute(value, 'ctx', pairs)  18 us
    pallas_call x2, Pallas kernels, grads_call(): pl.pallas_call(grads_kernel, grid_spec=pltpu.PrefetchScalarGridSpec(num_s...  10.5 us
    ppermute x9, waiting for transfers between devices, swapped(): return lax.ppermute(value, 'ctx', [(i, i ^ bit) for i in range(count)])  8.45 us
    unnamed x18, local copies, waits for them, and re-layouts  4.97 us
    pallas_call x6, Pallas kernels, simple_call(): pl.pallas_call(kernel, grid_spec=pltpu.PrefetchScalarGridSpec(num_scalar_...  2.67 us
    ppermute x1, waiting for transfers between devices, everywhere_sum(): other = lax.ppermute(value, 'dp', [(i, i ^ step) for i in range(dp_count)])  2.11 us
  transfers between devices with their start and end apart: 18, of which 9 were waited for; matrix products, arithmetic and copies ran while one was open for 0% of the time, Pallas kernels for 7%

commit v1 on v0

--- a/solution.py
+++ b/solution.py
@@ -61,7 +61,7 @@
     return pl.BlockSpec(memory_space=pltpu.VMEM)
 
 
-def simple_call(kernel, where, in_specs, out_shape, *args):
+def simple_call(kernel, where, in_specs, out_shape, *args, scratch=(), vmem_mib=8):
     if not isinstance(out_shape, (list, tuple)):
         out_shape = [out_shape]
     return pl.pallas_call(
@@ -71,69 +71,90 @@
             grid=(1,),
             in_specs=in_specs,
             out_specs=[in_vmem() for _ in out_shape],
+            scratch_shapes=scratch,
         ),
         out_shape=out_shape,
-        compiler_params=pltpu.CompilerParams(vmem_limit_bytes=8 * 1024 * 1024),
+        compiler_params=pltpu.CompilerParams(vmem_limit_bytes=vmem_mib * 1024 * 1024),
         cost_estimate=pl.CostEstimate(flops=0, transcendentals=0, bytes_accessed=1024 * 1024),
     )(where, *args)
 
 
-def column_block(rows, width, pick):
-    return pl.BlockSpec((None, rows, width), lambda i, w: (0, 0, pick(w[0])))
-
-
-def give_kv_call(where, key_rows, value_rows):
+def in_hbm():
+    return pl.BlockSpec(memory_space=pltpu.HBM)
+
+
+def split_kv_call(where, key_rows, value_rows):
     rows = key_rows.shape[1]
-    width = MINE * HD
-
-    def kernel(where_ref, k_ref, v_ref, out):
-        for h in range(MINE):
-            out[h, 0] = k_ref[:, h * HD : (h + 1) * HD]
-            out[h, 1] = v_ref[:, h * HD : (h + 1) * HD]
-
-    theirs = column_block(rows, width, lambda i: 1 - (i & 1))
-    shape = jax.ShapeDtypeStruct((MINE, 2, rows, HD), jnp.bfloat16)
-    return simple_call(kernel, where, [theirs, theirs], shape, key_rows, value_rows)[0]
-
-
-def local_kv_call(where, key_rows, value_rows, got_kv):
-    rows = key_rows.shape[1]
-    width = MINE * HD
-
-    def kernel(where_ref, k_ref, v_ref, got, *outs):
+
+    def kernel(where_ref, k_ref, v_ref, give, own, sems):
+        parity = where_ref[0] & 1
+        copies = []
+        for base, out in ((1 - parity, give), (parity, own)):
+            for h in range(MINE):
+                columns = pl.ds(pl.multiple_of((base * MINE + h) * HD, HD), HD)
+                for kv, source in enumerate((k_ref, v_ref)):
+                    copies.append(
+                        pltpu.make_async_copy(
+                            source.at[0, :, columns], out.at[h, kv], sems.at[len(copies)]
+                        )
+                    )
+        for copy in copies:
+            copy.start()
+        for copy in copies:
+            copy.wait()
+
+    shape = [jax.ShapeDtypeStruct((MINE, 2, rows, HD), jnp.bfloat16)] * 2
+    return simple_call(
+        kernel, where, [in_hbm(), in_hbm()], shape, key_rows, value_rows,
+        scratch=[pltpu.SemaphoreType.DMA((4 * MINE,))],
+    )
+
+
+def local_kv_call(where, own_kv, got_kv):
+    def kernel(where_ref, own, got, *outs):
         for h, out in enumerate(outs):
-            out[0, 0] = k_ref[:, h * HD : (h + 1) * HD]
-            out[0, 1] = v_ref[:, h * HD : (h + 1) * HD]
+            out[0] = own[h]
             out[1] = got[h]
 
-    own = column_block(rows, width, lambda i: i & 1)
-    shape = [jax.ShapeDtypeStruct((2, 2, rows, HD), jnp.bfloat16) for _ in range(MINE)]
-    return simple_call(kernel, where, [own, own, in_vmem()], shape, key_rows, value_rows, got_kv)
-
-
-def give_qg_call(where, query_rows, out_grad, loss_mask, after):
+    shape = [jax.ShapeDtypeStruct((2,) + own_kv.shape[1:], jnp.bfloat16) for _ in range(MINE)]
+    return simple_call(kernel, where, [in_vmem()] * 2, shape, own_kv, got_kv)
+
+
+def split_qg_call(where, query_rows, out_grad, loss_mask, after):
     rows = query_rows.shape[1]
     width = MINE * GROUP * HD
 
-    def kernel(where_ref, q_ref, g_ref, mask_ref, after_ref, out, token):
+    def kernel(where_ref, q_ref, g_ref, mask_ref, after_ref, give, own, token, g_s, sems):
+        parity = where_ref[0] & 1
+        pieces = []
+        for i, (base, out) in enumerate(((1 - parity, give), (parity, own))):
+            columns = pl.ds(pl.multiple_of(base * width, width), width)
+            g_copy = pltpu.make_async_copy(g_ref.at[0, :, columns], g_s.at[i], sems.at[i, 0])
+            q_copy = pltpu.make_async_copy(q_ref.at[0, :, columns], out.at[0], sems.at[i, 1])
+            g_copy.start()
+            q_copy.start()
+            pieces.append((g_copy, q_copy, out))
         keep_rows = mask_column(mask_ref)
-        out[0] = q_ref[...]
-        for h in range(MINE * GROUP):
-            columns = slice(h * HD, (h + 1) * HD)
-            out[1, :, columns] = (g_ref[:, columns].astype(jnp.float32) * keep_rows).astype(
-                jnp.bfloat16
-            )
         local = jnp.sum(mask_ref[...].astype(jnp.float32), axis=1, keepdims=True)
         token[...] = jnp.broadcast_to(local, token.shape)
-
-    theirs = column_block(rows, width, lambda i: 1 - (i & 1))
+        for i, (g_copy, q_copy, out) in enumerate(pieces):
+            g_copy.wait()
+            for h in range(MINE * GROUP):
+                columns = slice(h * HD, (h + 1) * HD)
+                out[1, :, columns] = (g_s[i, :, columns].astype(jnp.float32) * keep_rows).astype(
+                    jnp.bfloat16
+                )
+            q_copy.wait()
+
     shape = [
+        jax.ShapeDtypeStruct((2, rows, width), jnp.bfloat16),
         jax.ShapeDtypeStruct((2, rows, width), jnp.bfloat16),
         jax.ShapeDtypeStruct((8, HD), jnp.float32),
     ]
     return simple_call(
-        kernel, where, [theirs, theirs, in_vmem(), pl.BlockSpec(memory_space=pl.ANY)], shape,
+        kernel, where, [in_hbm(), in_hbm(), in_vmem(), pl.BlockSpec(memory_space=pl.ANY)], shape,
         query_rows, out_grad, loss_mask, after,
+        scratch=[pltpu.VMEM((2, rows, width), jnp.bfloat16), pltpu.SemaphoreType.DMA((2, 2))],
     )
 
 
@@ -203,21 +224,20 @@
 
 
 def grads_kernel(
-    where_ref, lengths_ref, mask_ref, token_in, own_q, own_g, got_qg, kv0, kv1, kv2,
-    own_dq, sib_dq, out0, out1, out2, token_out,
+    where_ref, lengths_ref, own_qg, got_qg, kv0, kv1, kv2,
+    own_dq, sib_dq, out0, out1, out2,
     q_s, g_s, k_s, v_s, kt_s, e_s, dp_s, mb_s, m_s, l_s, w_s, dqt_s, dk_s, dv_s,
 ):
-    rows = own_q.shape[0]
-    token_out[...] = token_in[...]
-    keep_rows = mask_column(mask_ref)
+    rows = own_qg.shape[1]
     my_index = where_ref[0]
     doc_count = lengths_ref.shape[1]
     for h in range(GROUP):
         columns = slice(h * HD, (h + 1) * HD)
-        q_s[h] = own_q[:, columns]
-        q_s[GROUP + h] = got_qg[0, :, columns]
-        g_s[h] = (own_g[:, columns].astype(jnp.float32) * keep_rows).astype(jnp.bfloat16)
-        g_s[GROUP + h] = got_qg[1, :, columns]
+        at = slice(h * rows, (h + 1) * rows)
+        q_s[0, at] = own_qg[0, :, columns]
+        q_s[1, at] = got_qg[0, :, columns]
+        g_s[0, at] = own_qg[1, :, columns]
+        g_s[1, at] = got_qg[1, :, columns]
     for d, kv in enumerate((kv0, kv1, kv2)):
         for p in range(2):
             k_s[2 * d + p] = kv[p, 0]
@@ -230,15 +250,17 @@
         q_start = (my_index ^ qb) * rows
 
         def doc_step(j, state):
-            bound, first, lo = state
+            bound, first, last, lo = state
             bound = bound + lengths_ref[0, j]
             first = jnp.where(bound <= q_start, bound, first)
+            last = jnp.where(bound <= q_start + rows - 1, bound, last)
             t_pos = q_start + lax.broadcasted_iota(jnp.int32, (1, rows), 1)
             lo = jnp.where(bound <= t_pos, bound, lo)
-            return bound, first, lo
-
-        _, first, lo = lax.fori_loop(
-            0, doc_count, doc_step, (jnp.int32(0), jnp.int32(0), jnp.zeros((1, rows), jnp.int32))
+            return bound, first, last, lo
+
+        zero = jnp.int32(0)
+        _, first, last, lo = lax.fori_loop(
+            0, doc_count, doc_step, (zero, zero, zero, jnp.zeros((1, rows), jnp.int32))
         )
         t_pos = q_start + lax.broadcasted_iota(jnp.int32, (1, rows), 1)
         m_s[...] = jnp.full_like(m_s, -jnp.inf)
@@ -255,15 +277,14 @@
         def phase_a(j, _):
             kb, k_start, live = locate(j)
 
-            @pl.when(live)
-            def _():
-                u_pos = k_start + lax.broadcasted_iota(jnp.int32, (rows, rows), 0)
-                bias = jnp.where((u_pos >= lo) & (u_pos <= t_pos), 0.0, -jnp.inf)
+            def scores(bias):
                 k = k_s[kb]
                 v = v_s[kb]
                 for h in range(GROUP):
-                    s = nt(k, q_s[qb * GROUP + h]) * EXP2_SCALE + bias
-                    dp = nt(v, g_s[qb * GROUP + h])
+                    s = nt(k, q_s[qb, h * rows : (h + 1) * rows]) * EXP2_SCALE
+                    if bias is not None:
+                        s = s + bias
+                    dp = nt(v, g_s[qb, h * rows : (h + 1) * rows])
                     m_old = m_s[h]
                     m_new = jnp.maximum(m_old, jnp.max(s, axis=0, keepdims=True))
                     keep = jnp.exp2(m_old - m_new)
@@ -275,6 +296,17 @@
                     e_s[kb * GROUP + h] = e
                     dp_s[kb * GROUP + h] = dp
 
+            full = (k_start < q_start) & (k_start >= last)
+
+            @pl.when(live & full)
+            def _():
+                scores(None)
+
+            @pl.when(live & jnp.logical_not(full))
+            def _():
+                u_pos = k_start + lax.broadcasted_iota(jnp.int32, (rows, rows), 0)
+                scores(jnp.where((u_pos >= lo) & (u_pos <= t_pos), 0.0, -jnp.inf))
+
             return 0
 
         lax.fori_loop(0, BLOCKS, phase_a, 0)
@@ -284,22 +316,19 @@
 
             @pl.when(live)
             def _():
-                kt = kt_s[kb]
-                dv = None
-                dk = None
+                p_all = []
+                ds_all = []
                 for h in range(GROUP):
                     inverse = 1.0 / l_s[h]
                     grad_dot = w_s[h] * inverse
                     alpha = jnp.exp2(mb_s[kb * GROUP + h] - m_s[h]) * inverse
                     p = e_s[kb * GROUP + h] * alpha
-                    ds = (p * (dp_s[kb * GROUP + h] - grad_dot)).astype(jnp.bfloat16)
-                    dv_h = nn(p.astype(jnp.bfloat16), g_s[qb * GROUP + h])
-                    dk_h = nn(ds, q_s[qb * GROUP + h])
-                    dv = dv_h if dv is None else dv + dv_h
-                    dk = dk_h if dk is None else dk + dk_h
-                    dqt_s[h] += nn(kt, ds)
-                dv_s[kb] += dv
-                dk_s[kb] += dk
+                    ds_all.append((p * (dp_s[kb * GROUP + h] - grad_dot)).astype(jnp.bfloat16))
+                    p_all.append(p.astype(jnp.bfloat16))
+                ds = jnp.concatenate(ds_all, 1)
+                dv_s[kb] += nn(jnp.concatenate(p_all, 1), g_s[qb])
+                dk_s[kb] += nn(ds, q_s[qb])
+                dqt_s[...] += nn(kt_s[kb], ds)
 
             return 0
 
@@ -308,12 +337,12 @@
         @pl.when(qb == 0)
         def _():
             for h in range(GROUP):
-                own_dq[:, h * HD : (h + 1) * HD] = dqt_s[h].T.astype(own_dq.dtype)
+                own_dq[:, h * HD : (h + 1) * HD] = dqt_s[:, h * rows : (h + 1) * rows].T.astype(own_dq.dtype)
 
         @pl.when(qb == 1)
         def _():
             for h in range(GROUP):
-                sib_dq[:, h * HD : (h + 1) * HD] = dqt_s[h].T.astype(sib_dq.dtype)
+                sib_dq[:, h * HD : (h + 1) * HD] = dqt_s[:, h * rows : (h + 1) * rows].T.astype(sib_dq.dtype)
 
         return 0
 
@@ -324,14 +353,12 @@
             out[p, 1] = dv_s[2 * d + p].astype(out.dtype)
 
 
-def grads_call(head, where, lengths, loss_mask, token, query_rows, out_grad, got_qg, kv0, kv1, kv2):
-    rows = query_rows.shape[1]
+def grads_call(head, where, lengths, own_qg, got_qg, kv0, kv1, kv2):
+    rows = own_qg.shape[1]
     wide = GROUP * HD
-    own = column_block(rows, wide, lambda i: (i & 1) * MINE + head)
-    got = pl.BlockSpec((2, rows, wide), lambda i, w: (0, 0, head))
+    half = pl.BlockSpec((2, rows, wide), lambda i, w: (0, 0, head))
     f32 = jnp.float32
     bf16 = jnp.bfloat16
-    pair = 2 * GROUP
     tiles = BLOCKS * GROUP
     tile_work = 2 * rows * rows * HD
     return pl.pallas_call(
@@ -341,12 +368,12 @@
             grid=(1,),
             in_specs=[
                 pl.BlockSpec(memory_space=pltpu.SMEM),
-                in_vmem(), in_vmem(), own, own, got, in_vmem(), in_vmem(), in_vmem(),
+                half, half, in_vmem(), in_vmem(), in_vmem(),
             ],
-            out_specs=[in_vmem() for _ in range(6)],
+            out_specs=[in_vmem() for _ in range(5)],
             scratch_shapes=[
-                pltpu.VMEM((pair, rows, HD), bf16),
-                pltpu.VMEM((pair, rows, HD), bf16),
+                pltpu.VMEM((2, GROUP * rows, HD), bf16),
+                pltpu.VMEM((2, GROUP * rows, HD), bf16),
                 pltpu.VMEM((BLOCKS, rows, HD), bf16),
                 pltpu.VMEM((BLOCKS, rows, HD), bf16),
                 pltpu.VMEM((BLOCKS, HD, rows), bf16),
@@ -356,7 +383,7 @@
                 pltpu.VMEM((GROUP, 1, rows), f32),
                 pltpu.VMEM((GROUP, 1, rows), f32),
                 pltpu.VMEM((GROUP, 1, rows), f32),
-                pltpu.VMEM((GROUP, HD, rows), f32),
+                pltpu.VMEM((HD, GROUP * rows), f32),
                 pltpu.VMEM((BLOCKS, rows, HD), f32),
                 pltpu.VMEM((BLOCKS, rows, HD), f32),
             ],
@@ -367,7 +394,6 @@
             jax.ShapeDtypeStruct((2, 2, rows, HD), f32),
             jax.ShapeDtypeStruct((2, 2, rows, HD), bf16),
             jax.ShapeDtypeStruct((2, 2, rows, HD), bf16),
-            jax.ShapeDtypeStruct((8, HD), f32),
         ],
         compiler_params=pltpu.CompilerParams(vmem_limit_bytes=26 * 1024 * 1024),
         name="grads",
@@ -375,7 +401,7 @@
             flops=5 * 6 * GROUP * tile_work, transcendentals=6 * GROUP * rows * rows,
             bytes_accessed=6 * 1024 * 1024,
         ),
-    )(where, lengths, loss_mask, token, query_rows, out_grad, got_qg, kv0, kv1, kv2)
+    )(where, lengths, own_qg, got_qg, kv0, kv1, kv2)
 
 
 def work(query_rows, key_rows, value_rows, out_grad, lengths, loss_mask):
@@ -383,11 +409,15 @@
     numerator = float(lax.axis_size("dp") * rows * lax.axis_size("ctx"))
     where = lax.axis_index("ctx").astype(jnp.int32).reshape(1)
 
-    give_kv = give_kv_call(where, key_rows, value_rows)
+    query_rows, key_rows, value_rows, out_grad = (
+        pltpu.with_memory_space_constraint(x, pltpu.HBM)
+        for x in (query_rows, key_rows, value_rows, out_grad)
+    )
+    give_kv, own_kv = split_kv_call(where, key_rows, value_rows)
     got_kv = swapped(give_kv, 1)
-    give_qg, token = give_qg_call(where, query_rows, out_grad, loss_mask, give_kv)
+    give_qg, own_qg, token = split_qg_call(where, query_rows, out_grad, loss_mask, give_kv)
     got_qg = swapped(give_qg, 1)
-    local = local_kv_call(where, key_rows, value_rows, got_kv)
+    local = local_kv_call(where, own_kv, got_kv)
     near = []
     far = []
     for kv in local:
@@ -398,9 +428,8 @@
     got_dq = []
     parts = []
     for h in range(MINE):
-        dq_o, dq_s, d0, d1, d2, token = grads_call(
-            h, where, lengths, loss_mask, token, query_rows, out_grad, got_qg,
-            local[h], near[h], far[h],
+        dq_o, dq_s, d0, d1, d2 = grads_call(
+            h, where, lengths, own_qg, got_qg, local[h], near[h], far[h]
         )
         own_dq.append(dq_o)
         r1 = shifted(d1, -2)

time: 93.9 us -> 88.7 us (0.945)
  starting transfers between devices: 45.9 us -> 39.4 us
  local copies, waits for them, and re-layouts: 4.97 us -> 0.68 us
  waiting for transfers between devices: 28.5 us -> 31.7 us
  Pallas kernels: 13.1 us -> 15.6 us
    ppermute x9, starting transfers between devices: 24 us -> 17.5 us  [swapped(): return lax.ppermute(value, 'ctx', [(i, i ^ bit) for i in range(count)])]
    unnamed x18 -> x4, local copies, waits for them, and re-layouts: 4.97 us -> 0.68 us
    ppermute x8, waiting for transfers between devices: 18 us -> 21.2 us  [shifted(): return lax.ppermute(value, 'ctx', pairs)]
    pallas_call x6, Pallas kernels: 2.67 us -> 5.08 us  [simple_call(): pl.pallas_call(kernel, grid_spec=pltpu.PrefetchScalarGridSpec(num_scalar_...]
  transfers between devices with their start and end apart: 18 -> 18, of which waited for: 9 -> 8; matrix products, arithmetic and copies ran while one was open for 0% -> 0% of each run, Pallas kernels for 7% -> 13%
where the time goes in v1:
time: 88.7 us; the launch traced here: 88.3 us
  starting transfers between devices  39.4 us (44%)
  waiting for transfers between devices  31.7 us (36%)
  Pallas kernels  15.6 us (18%)
    ppermute x8, waiting for transfers between devices, shifted(): return lax.ppermute(value, 'ctx', pairs)  21.2 us
    ppermute x8, starting transfers between devices, shifted(): return lax.ppermute(value, 'ctx', pairs)  20.4 us
    ppermute x9, starting transfers between devices, swapped(): return lax.ppermute(value, 'ctx', [(i, i ^ bit) for i in range(count)])  17.5 us
    pallas_call x2, Pallas kernels, grads_call(): pl.pallas_call(grads_kernel, grid_spec=pltpu.PrefetchScalarGridSpec(num_s...  10.5 us
    ppermute x9, waiting for transfers between devices, swapped(): return lax.ppermute(value, 'ctx', [(i, i ^ bit) for i in range(count)])  8.45 us
    pallas_call x6, Pallas kernels, simple_call(): pl.pallas_call(kernel, grid_spec=pltpu.PrefetchScalarGridSpec(num_scalar_...  5.08 us
    ppermute x1, waiting for transfers between devices, everywhere_sum(): other = lax.ppermute(value, 'dp', [(i, i ^ step) for i in range(dp_count)])  2.11 us
  transfers between devices with their start and end apart: 18, of which 8 were waited for; matrix products, arithmetic and copies ran while one was open for 0% of the time, Pallas kernels for 13%

profile of v1, /device:TPU:0, one launch (start us, length us, event | category | flops | bytes accessed | tf_op | source)
XLA Modules:
  0.0 88.3 jit_solution(8838853361289742654)
XLA Ops:
  0.6 1.1 %shard_map.85 = (bf16[2,2,256,128]{3,2,1,0:T(8,128)(2,1)S(1)}, bf16[2,2,256,128]{3,2,1,0:T(8,128)(2,1)S(1)}) custom-call(s32[1]{0:T(128)} %bitcast.where_ref, bf16[1,256,512]{2,1,0:T(8,128)(2,1)} %k_ref.1, bf16[1,256,512]{2,1,0:T(8,128)(2,1)} %v_ref.1), custom_call_target="tpu_custom_call" | custom-call | bytes 1048576 | tf_op jit(solution)/shard_map/pallas_call | solution.py:67
  1.8 0.0 copy-start
  1.8 0.7 copy-done
  2.5 1.6 %shard_map.86 = (bf16[2,256,1024]{2,1,0:T(8,128)(2,1)S(1)}, bf16[2,256,1024]{2,1,0:T(8,128)(2,1)S(1)}, f32[8,128]{1,0:T(8,128)S(1)}) custom-call(s32[1]{0:T(128)} %bitcast.where_ref, bf16[1,256,2048]{2,1,0:T(8,128)(2,1)} %q_ref.1, bf16[1,256,2048]{2,1,0:T(8,128)(2,1)} %g_ref.1, s32[1,256]{1,0:T(1,128)S(1)} %copy-done, ...), custom_call_target="tpu_custom_call" | custom-call | bytes 1048576 | tf_op jit(solution)/shard_map/pallas_call | solution.py:67
  4.0 0.6 collective-permute-start
  4.6 0.1 collective-permute-start.1
  4.7 2.6 %collective-permute-done.1.got = bf16[2,2,256,128]{3,2,1,0:T(8,128)(2,1)S(1)} collective-permute-done((bf16[2,2,256,128]{3,2,1,0:T(8,128)(2,1)S(1)}, bf16[2,2,256,128]{3,2,1,0:T(8,128)(2,1)S(1)}, u32[]{:S(2)}, u32[]{:S(2)}) %collective-permute-start.1) | collective-permute-done | bytes 262176 | tf_op jit(solution)/shard_map/ppermute | solution.py:29
  7.3 4.9 %collective-permute-start.5 = (bf16[2,2,256,128]{3,2,1,0:T(8,128)(2,1)S(1)}, bf16[2,2,256,128]{3,2,1,0:T(8,128)(2,1)S(1)}, u32[]{:S(2)}, u32[]{:S(2)}) collective-permute-start(bf16[2,2,256,128]{3,2,1,0:T(8,128)(2,1)S(1)} %get-tuple-element.32.kv0), channel_id=1, source_target_pairs={{0,4},{1,5},{2,6},{3,7},{4,8},{5,9},{6,10},{7,11},{8,12},{9,13},{1... | collective-permute-start | bytes 786440 | tf_op jit(solution)/shard_map/ppermute | solution.py:24
  12.2 3.4 %collective-permute-start.4 = (bf16[2,2,256,128]{3,2,1,0:T(8,128)(2,1)S(1)}, bf16[2,2,256,128]{3,2,1,0:T(8,128)(2,1)S(1)}, u32[]{:S(2)}, u32[]{:S(2)}) collective-permute-start(bf16[2,2,256,128]{3,2,1,0:T(8,128)(2,1)S(1)} %get-tuple-element.32.kv0), channel_id=1, source_target_pairs={{0,2},{1,3},{2,4},{3,5},{4,6},{5,7},{6,8},{7,9},{8,10},{9,11},{10,... | collective-permute-start | bytes 786440 | tf_op jit(solution)/shard_map/ppermute | solution.py:24
  15.6 0.0 copy-start.1
  15.6 3.5 %collective-permute-start.3 = (bf16[2,2,256,128]{3,2,1,0:T(8,128)(2,1)S(1)}, bf16[2,2,256,128]{3,2,1,0:T(8,128)(2,1)S(1)}, u32[]{:S(2)}, u32[]{:S(2)}) collective-permute-start(bf16[2,2,256,128]{3,2,1,0:T(8,128)(2,1)S(1)} %get-tuple-element.30.kv0), channel_id=1, source_target_pairs={{0,4},{1,5},{2,6},{3,7},{4,8},{5,9},{6,10},{7,11},{8,12},{9,13},{1... | collective-permute-start | bytes 786440 | tf_op jit(solution)/shard_map/ppermute | solution.py:24
  19.1 3.4 %collective-permute-start.2 = (bf16[2,2,256,128]{3,2,1,0:T(8,128)(2,1)S(1)}, bf16[2,2,256,128]{3,2,1,0:T(8,128)(2,1)S(1)}, u32[]{:S(2)}, u32[]{:S(2)}) collective-permute-start(bf16[2,2,256,128]{3,2,1,0:T(8,128)(2,1)S(1)} %get-tuple-element.30.kv0), channel_id=1, source_target_pairs={{0,2},{1,3},{2,4},{3,5},{4,6},{5,7},{6,8},{7,9},{8,10},{9,11},{10,... | collective-permute-start | bytes 786440 | tf_op jit(solution)/shard_map/ppermute | solution.py:24
  22.5 0.0 collective-permute-done.5.kv2
  22.6 0.0 collective-permute-done.4.kv1
  22.6 0.0 collective-permute-done.got_qg
  22.6 0.0 copy-done.1
  22.6 5.2 %grads.3 = (bf16[256,512]{1,0:T(8,128)(2,1)S(1)}, bf16[256,512]{1,0:T(8,128)(2,1)S(1)}, f32[2,2,256,128]{3,2,1,0:T(8,128)S(1)}, bf16[2,2,256,128]{3,2,1,0:T(8,128)(2,1)S(1)}, bf16[2,2,256,128]{3,2,1,0:T(8,128)(2,1)S(1)}) custom-call(s32[1]{0:T(128)} %bitcast.where_ref, s32[1,8]{1,0:T(1,128)S(1)} %copy-done.1, ...), custom_call_target="tpu_custom_call" | custom-call | flops 2013265920 | bytes 6291456 | tf_op jit(solution)/shard_map/grads/pallas_call | solution.py:364
  27.8 0.1 collective-permute-start.7
  27.9 1.6 %collective-permute-start.8 = (f32[8,128]{1,0:T(8,128)S(1)}, f32[8,128]{1,0:T(8,128)S(1)}, u32[]{:S(2)}, u32[]{:S(2)}) collective-permute-start(f32[8,128]{1,0:T(8,128)S(1)} %get-tuple-element.36), channel_id=1, source_target_pairs={{0,16},{16,0},{1,17},{17,1},{2,18},{18,2},{3,19},{19,3},{4,20},{20... | collective-permute-start | bytes 12296 | tf_op jit(solution)/shard_map/ppermute | solution.py:36
  29.5 2.1 %collective-permute-done.8 = f32[8,128]{1,0:T(8,128)S(1)} collective-permute-done((f32[8,128]{1,0:T(8,128)S(1)}, f32[8,128]{1,0:T(8,128)S(1)}, u32[]{:S(2)}, u32[]{:S(2)}) %collective-permute-start.8) | collective-permute-done | bytes 4128 | tf_op jit(solution)/shard_map/ppermute | solution.py:36
  31.6 0.0 collective-permute-start.9
  31.6 1.2 %collective-permute-done.9 = f32[8,128]{1,0:T(8,128)S(1)} collective-permute-done((f32[8,128]{1,0:T(8,128)S(1)}, f32[8,128]{1,0:T(8,128)S(1)}, u32[]{:S(2)}, u32[]{:S(2)}) %collective-permute-start.9) | collective-permute-done | bytes 4128 | tf_op jit(solution)/shard_map/ppermute | solution.py:29
  32.8 7.1 %collective-permute-start.10 = (f32[8,128]{1,0:T(8,128)S(1)}, f32[8,128]{1,0:T(8,128)S(1)}, u32[]{:S(2)}, u32[]{:S(2)}) collective-permute-start(f32[8,128]{1,0:T(8,128)S(1)} %add.16), channel_id=1, source_target_pairs={{0,2},{1,3},{2,0},{3,1},{4,6},{5,7},{6,4},{7,5},{8,10},{9,11},{10,... | collective-permute-start | bytes 12296 | tf_op jit(solution)/shard_map/ppermute | solution.py:29
  39.8 1.6 %collective-permute-done.10 = f32[8,128]{1,0:T(8,128)S(1)} collective-permute-done((f32[8,128]{1,0:T(8,128)S(1)}, f32[8,128]{1,0:T(8,128)S(1)}, u32[]{:S(2)}, u32[]{:S(2)}) %collective-permute-start.10) | collective-permute-done | bytes 4128 | tf_op jit(solution)/shard_map/ppermute | solution.py:29
  41.4 4.5 %collective-permute-start.11 = (f32[8,128]{1,0:T(8,128)S(1)}, f32[8,128]{1,0:T(8,128)S(1)}, u32[]{:S(2)}, u32[]{:S(2)}) collective-permute-start(f32[8,128]{1,0:T(8,128)S(1)} %add.17), channel_id=1, source_target_pairs={{0,4},{1,5},{2,6},{3,7},{4,0},{5,1},{6,2},{7,3},{8,12},{9,13},{10,... | collective-permute-start | bytes 12296 | tf_op jit(solution)/shard_map/ppermute | solution.py:29
  45.9 1.6 %collective-permute-done.11 = f32[8,128]{1,0:T(8,128)S(1)} collective-permute-done((f32[8,128]{1,0:T(8,128)S(1)}, f32[8,128]{1,0:T(8,128)S(1)}, u32[]{:S(2)}, u32[]{:S(2)}) %collective-permute-start.11) | collective-permute-done | bytes 4128 | tf_op jit(solution)/shard_map/ppermute | solution.py:29
  47.5 5.1 %collective-permute-start.12 = (f32[8,128]{1,0:T(8,128)S(1)}, f32[8,128]{1,0:T(8,128)S(1)}, u32[]{:S(2)}, u32[]{:S(2)}) collective-permute-start(f32[8,128]{1,0:T(8,128)S(1)} %add.18), channel_id=1, source_target_pairs={{0,8},{1,9},{2,10},{3,11},{4,12},{5,13},{6,14},{7,15},{8,0},{9,1},... | collective-permute-start | bytes 12296 | tf_op jit(solution)/shard_map/ppermute | solution.py:29
  52.6 1.3 %collective-permute-start.15 = (bf16[2,2,256,128]{3,2,1,0:T(8,128)(2,1)S(1)}, bf16[2,2,256,128]{3,2,1,0:T(8,128)(2,1)S(1)}, u32[]{:S(2)}, u32[]{:S(2)}) collective-permute-start(bf16[2,2,256,128]{3,2,1,0:T(8,128)(2,1)S(1)} %get-tuple-element.42), channel_id=1, source_target_pairs={{2,0},{3,1},{4,2},{5,3},{6,4},{7,5},{8,6},{9,7},{10,8},{11,9},{12,... | collective-permute-start | bytes 786440 | tf_op jit(solution)/shard_map/ppermute | solution.py:24
  53.9 0.0 collective-permute-done.3.kv2
  53.9 0.0 collective-permute-done.2.kv1
  53.9 5.2 %grads.2 = (bf16[256,512]{1,0:T(8,128)(2,1)S(1)}, bf16[256,512]{1,0:T(8,128)(2,1)S(1)}, f32[2,2,256,128]{3,2,1,0:T(8,128)S(1)}, bf16[2,2,256,128]{3,2,1,0:T(8,128)(2,1)S(1)}, bf16[2,2,256,128]{3,2,1,0:T(8,128)(2,1)S(1)}) custom-call(s32[1]{0:T(128)} %bitcast.where_ref, s32[1,8]{1,0:T(1,128)S(1)} %copy-done.1, ...), custom_call_target="tpu_custom_call" | custom-call | flops 2013265920 | bytes 6291456 | tf_op jit(solution)/shard_map/grads/pallas_call | solution.py:364
  59.1 0.1 collective-permute-start.6
  59.2 1.3 %collective-permute-start.16 = (bf16[2,2,256,128]{3,2,1,0:T(8,128)(2,1)S(1)}, bf16[2,2,256,128]{3,2,1,0:T(8,128)(2,1)S(1)}, u32[]{:S(2)}, u32[]{:S(2)}) collective-permute-start(bf16[2,2,256,128]{3,2,1,0:T(8,128)(2,1)S(1)} %get-tuple-element.43), channel_id=1, source_target_pairs={{4,0},{5,1},{6,2},{7,3},{8,4},{9,5},{10,6},{11,7},{12,8},{13,9},{1... | collective-permute-start | bytes 786440 | tf_op jit(solution)/shard_map/ppermute | solution.py:24
  60.5 0.0 collective-permute-done.12
  60.5 1.3 %collective-permute-start.13 = (bf16[2,2,256,128]{3,2,1,0:T(8,128)(2,1)S(1)}, bf16[2,2,256,128]{3,2,1,0:T(8,128)(2,1)S(1)}, u32[]{:S(2)}, u32[]{:S(2)}) collective-permute-start(bf16[2,2,256,128]{3,2,1,0:T(8,128)(2,1)S(1)} %get-tuple-element.39), channel_id=1, source_target_pairs={{2,0},{3,1},{4,2},{5,3},{6,4},{7,5},{8,6},{9,7},{10,8},{11,9},{12,... | collective-permute-start | bytes 786440 | tf_op jit(solution)/shard_map/ppermute | solution.py:24
  61.8 0.0 collective-permute-done.7.refs_3_
  61.8 1.3 %collective-permute-start.14 = (bf16[2,2,256,128]{3,2,1,0:T(8,128)(2,1)S(1)}, bf16[2,2,256,128]{3,2,1,0:T(8,128)(2,1)S(1)}, u32[]{:S(2)}, u32[]{:S(2)}) collective-permute-start(bf16[2,2,256,128]{3,2,1,0:T(8,128)(2,1)S(1)} %get-tuple-element.40), channel_id=1, source_target_pairs={{4,0},{5,1},{6,2},{7,3},{8,4},{9,5},{10,6},{11,7},{12,8},{13,9},{1... | collective-permute-start | bytes 786440 | tf_op jit(solution)/shard_map/ppermute | solution.py:24
  63.2 0.0 collective-permute-done.6.refs_2_
  63.2 1.3 %shard_map.88 = (bf16[1,256,2048]{2,1,0:T(8,128)(2,1)}, f32[8,128]{1,0:T(8,128)S(1)}) custom-call(s32[1]{0:T(128)} %bitcast.where_ref, bf16[256,512]{1,0:T(8,128)(2,1)S(1)} %get-tuple-element.31.refs_0_, bf16[256,512]{1,0:T(8,128)(2,1)S(1)} %get-tuple-element.33.refs_1_, bf16[256,512]{1,0:T(8,128)(2,1)S(1)} %collective-permute-done.6.refs_2_, ...), custom_call_target="tpu_custom_call" | custom-call | bytes 1048576 | tf_op jit(solution)/shard_map/pallas_call | solution.py:67
  64.4 0.0 collective-permute-done.15.refs_4_
  64.4 10.1 %collective-permute-done.16.refs_5_ = bf16[2,2,256,128]{3,2,1,0:T(8,128)(2,1)S(1)} collective-permute-done((bf16[2,2,256,128]{3,2,1,0:T(8,128)(2,1)S(1)}, bf16[2,2,256,128]{3,2,1,0:T(8,128)(2,1)S(1)}, u32[]{:S(2)}, u32[]{:S(2)}) %collective-permute-start.16) | collective-permute-done | bytes 262176 | tf_op jit(solution)/shard_map/ppermute | solution.py:24
  74.6 0.0 collective-permute-done.13.refs_1_
  74.6 11.0 %collective-permute-done.14.refs_2_ = bf16[2,2,256,128]{3,2,1,0:T(8,128)(2,1)S(1)} collective-permute-done((bf16[2,2,256,128]{3,2,1,0:T(8,128)(2,1)S(1)}, bf16[2,2,256,128]{3,2,1,0:T(8,128)(2,1)S(1)}, u32[]{:S(2)}, u32[]{:S(2)}) %collective-permute-start.14) | collective-permute-done | bytes 262176 | tf_op jit(solution)/shard_map/ppermute | solution.py:24
  85.6 0.2 shard_map.89
  85.8 0.1 collective-permute-start.17
  85.9 1.5 %collective-permute-done.17.got_ref = bf16[2,2,256,128]{3,2,1,0:T(8,128)(2,1)S(1)} collective-permute-done((bf16[2,2,256,128]{3,2,1,0:T(8,128)(2,1)S(1)}, bf16[2,2,256,128]{3,2,1,0:T(8,128)(2,1)S(1)}, u32[]{:S(2)}, u32[]{:S(2)}) %collective-permute-start.17) | collective-permute-done | bytes 262176 | tf_op jit(solution)/shard_map/ppermute | solution.py:29
  87.4 0.9 shard_map.90
  (6 shorter events, 0.1 us)
Async XLA Ops:
  1.8 0.7 copy-start
  4.0 18.5 %collective-permute-start = (bf16[2,256,1024]{2,1,0:T(8,128)(2,1)S(1)}, bf16[2,256,1024]{2,1,0:T(8,128)(2,1)S(1)}, u32[]{:S(2)}, u32[]{:S(2)}) collective-permute-start(bf16[2,256,1024]{2,1,0:T(8,128)(2,1)S(1)} %get-tuple-element.28), channel_id=1, source_target_pairs={{0,1},{1,0},{2,3},{3,2},{4,5},{5,4},{6,7},{7,6},{8,9},{9,8},{10,11... | collective-permute-start | bytes 3145736 | tf_op jit(solution)/shard_map/ppermute | solution.py:29
  4.6 2.7 %collective-permute-start.1 = (bf16[2,2,256,128]{3,2,1,0:T(8,128)(2,1)S(1)}, bf16[2,2,256,128]{3,2,1,0:T(8,128)(2,1)S(1)}, u32[]{:S(2)}, u32[]{:S(2)}) collective-permute-start(bf16[2,2,256,128]{3,2,1,0:T(8,128)(2,1)S(1)} %get-tuple-element.26.after_ref), channel_id=1, source_target_pairs={{0,1},{1,0},{2,3},{3,2},{4,5},{5,4},{6,7},{7,6},{8,9},{9,8},{10,11... | collective-permute-start | bytes 786440 | tf_op jit(solution)/shard_map/ppermute | solution.py:29
  7.3 15.3 %collective-permute-start.5 = (bf16[2,2,256,128]{3,2,1,0:T(8,128)(2,1)S(1)}, bf16[2,2,256,128]{3,2,1,0:T(8,128)(2,1)S(1)}, u32[]{:S(2)}, u32[]{:S(2)}) collective-permute-start(bf16[2,2,256,128]{3,2,1,0:T(8,128)(2,1)S(1)} %get-tuple-element.32.kv0), channel_id=1, source_target_pairs={{0,4},{1,5},{2,6},{3,7},{4,8},{5,9},{6,10},{7,11},{8,12},{9,13},{1... | collective-permute-start | bytes 786440 | tf_op jit(solution)/shard_map/ppermute | solution.py:24
  12.2 10.4 %collective-permute-start.4 = (bf16[2,2,256,128]{3,2,1,0:T(8,128)(2,1)S(1)}, bf16[2,2,256,128]{3,2,1,0:T(8,128)(2,1)S(1)}, u32[]{:S(2)}, u32[]{:S(2)}) collective-permute-start(bf16[2,2,256,128]{3,2,1,0:T(8,128)(2,1)S(1)} %get-tuple-element.32.kv0), channel_id=1, source_target_pairs={{0,2},{1,3},{2,4},{3,5},{4,6},{5,7},{6,8},{7,9},{8,10},{9,11},{10,... | collective-permute-start | bytes 786440 | tf_op jit(solution)/shard_map/ppermute | solution.py:24
  15.6 7.0 %copy-start.1 = (s32[1,8]{1,0:T(1,128)S(1)}, s32[1,8]{1,0:T(1,128)}, u32[]{:S(2)}) copy-start(s32[1,8]{1,0:T(1,128)} %lengths_ref.3) | copy-start | bytes 100
  15.6 38.3 %collective-permute-start.3 = (bf16[2,2,256,128]{3,2,1,0:T(8,128)(2,1)S(1)}, bf16[2,2,256,128]{3,2,1,0:T(8,128)(2,1)S(1)}, u32[]{:S(2)}, u32[]{:S(2)}) collective-permute-start(bf16[2,2,256,128]{3,2,1,0:T(8,128)(2,1)S(1)} %get-tuple-element.30.kv0), channel_id=1, source_target_pairs={{0,4},{1,5},{2,6},{3,7},{4,8},{5,9},{6,10},{7,11},{8,12},{9,13},{1... | collective-permute-start | bytes 786440 | tf_op jit(solution)/shard_map/ppermute | solution.py:24
  19.1 34.8 %collective-permute-start.2 = (bf16[2,2,256,128]{3,2,1,0:T(8,128)(2,1)S(1)}, bf16[2,2,256,128]{3,2,1,0:T(8,128)(2,1)S(1)}, u32[]{:S(2)}, u32[]{:S(2)}) collective-permute-start(bf16[2,2,256,128]{3,2,1,0:T(8,128)(2,1)S(1)} %get-tuple-element.30.kv0), channel_id=1, source_target_pairs={{0,2},{1,3},{2,4},{3,5},{4,6},{5,7},{6,8},{7,9},{8,10},{9,11},{10,... | collective-permute-start | bytes 786440 | tf_op jit(solution)/shard_map/ppermute | solution.py:24
  27.8 34.0 %collective-permute-start.7 = (bf16[256,512]{1,0:T(8,128)(2,1)S(1)}, bf16[256,512]{1,0:T(8,128)(2,1)S(1)}, u32[]{:S(2)}, u32[]{:S(2)}) collective-permute-start(bf16[256,512]{1,0:T(8,128)(2,1)S(1)} %get-tuple-element.35), channel_id=1, source_target_pairs={{0,1},{1,0},{2,3},{3,2},{4,5},{5,4},{6,7},{7,6},{8,9},{9,8},{10,11... | collective-permute-start | bytes 786440 | tf_op jit(solution)/shard_map/ppermute | solution.py:29
  27.9 3.7 %collective-permute-start.8 = (f32[8,128]{1,0:T(8,128)S(1)}, f32[8,128]{1,0:T(8,128)S(1)}, u32[]{:S(2)}, u32[]{:S(2)}) collective-permute-start(f32[8,128]{1,0:T(8,128)S(1)} %get-tuple-element.36), channel_id=1, source_target_pairs={{0,16},{16,0},{1,17},{17,1},{2,18},{18,2},{3,19},{19,3},{4,20},{20... | collective-permute-start | bytes 12296 | tf_op jit(solution)/shard_map/ppermute | solution.py:36
  31.6 1.2 %collective-permute-start.9 = (f32[8,128]{1,0:T(8,128)S(1)}, f32[8,128]{1,0:T(8,128)S(1)}, u32[]{:S(2)}, u32[]{:S(2)}) collective-permute-start(f32[8,128]{1,0:T(8,128)S(1)} %add.15), channel_id=1, source_target_pairs={{0,1},{1,0},{2,3},{3,2},{4,5},{5,4},{6,7},{7,6},{8,9},{9,8},{10,11... | collective-permute-start | bytes 12296 | tf_op jit(solution)/shard_map/ppermute | solution.py:29
  32.8 8.6 %collective-permute-start.10 = (f32[8,128]{1,0:T(8,128)S(1)}, f32[8,128]{1,0:T(8,128)S(1)}, u32[]{:S(2)}, u32[]{:S(2)}) collective-permute-start(f32[8,128]{1,0:T(8,128)S(1)} %add.16), channel_id=1, source_target_pairs={{0,2},{1,3},{2,0},{3,1},{4,6},{5,7},{6,4},{7,5},{8,10},{9,11},{10,... | collective-permute-start | bytes 12296 | tf_op jit(solution)/shard_map/ppermute | solution.py:29
  41.4 6.1 %collective-permute-start.11 = (f32[8,128]{1,0:T(8,128)S(1)}, f32[8,128]{1,0:T(8,128)S(1)}, u32[]{:S(2)}, u32[]{:S(2)}) collective-permute-start(f32[8,128]{1,0:T(8,128)S(1)} %add.17), channel_id=1, source_target_pairs={{0,4},{1,5},{2,6},{3,7},{4,0},{5,1},{6,2},{7,3},{8,12},{9,13},{10,... | collective-permute-start | bytes 12296 | tf_op jit(solution)/shard_map/ppermute | solution.py:29
  47.5 13.1 %collective-permute-start.12 = (f32[8,128]{1,0:T(8,128)S(1)}, f32[8,128]{1,0:T(8,128)S(1)}, u32[]{:S(2)}, u32[]{:S(2)}) collective-permute-start(f32[8,128]{1,0:T(8,128)S(1)} %add.18), channel_id=1, source_target_pairs={{0,8},{1,9},{2,10},{3,11},{4,12},{5,13},{6,14},{7,15},{8,0},{9,1},... | collective-permute-start | bytes 12296 | tf_op jit(solution)/shard_map/ppermute | solution.py:29
  52.6 11.9 %collective-permute-start.15 = (bf16[2,2,256,128]{3,2,1,0:T(8,128)(2,1)S(1)}, bf16[2,2,256,128]{3,2,1,0:T(8,128)(2,1)S(1)}, u32[]{:S(2)}, u32[]{:S(2)}) collective-permute-start(bf16[2,2,256,128]{3,2,1,0:T(8,128)(2,1)S(1)} %get-tuple-element.42), channel_id=1, source_target_pairs={{2,0},{3,1},{4,2},{5,3},{6,4},{7,5},{8,6},{9,7},{10,8},{11,9},{12,... | collective-permute-start | bytes 786440 | tf_op jit(solution)/shard_map/ppermute | solution.py:24
  59.1 4.0 %collective-permute-start.6 = (bf16[256,512]{1,0:T(8,128)(2,1)S(1)}, bf16[256,512]{1,0:T(8,128)(2,1)S(1)}, u32[]{:S(2)}, u32[]{:S(2)}) collective-permute-start(bf16[256,512]{1,0:T(8,128)(2,1)S(1)} %get-tuple-element.34), channel_id=1, source_target_pairs={{0,1},{1,0},{2,3},{3,2},{4,5},{5,4},{6,7},{7,6},{8,9},{9,8},{10,11... | collective-permute-start | bytes 786440 | tf_op jit(solution)/shard_map/ppermute | solution.py:29
  59.2 15.3 %collective-permute-start.16 = (bf16[2,2,256,128]{3,2,1,0:T(8,128)(2,1)S(1)}, bf16[2,2,256,128]{3,2,1,0:T(8,128)(2,1)S(1)}, u32[]{:S(2)}, u32[]{:S(2)}) collective-permute-start(bf16[2,2,256,128]{3,2,1,0:T(8,128)(2,1)S(1)} %get-tuple-element.43), channel_id=1, source_target_pairs={{4,0},{5,1},{6,2},{7,3},{8,4},{9,5},{10,6},{11,7},{12,8},{13,9},{1... | collective-permute-start | bytes 786440 | tf_op jit(solution)/shard_map/ppermute | solution.py:24
  60.5 14.0 %collective-permute-start.13 = (bf16[2,2,256,128]{3,2,1,0:T(8,128)(2,1)S(1)}, bf16[2,2,256,128]{3,2,1,0:T(8,128)(2,1)S(1)}, u32[]{:S(2)}, u32[]{:S(2)}) collective-permute-start(bf16[2,2,256,128]{3,2,1,0:T(8,128)(2,1)S(1)} %get-tuple-element.39), channel_id=1, source_target_pairs={{2,0},{3,1},{4,2},{5,3},{6,4},{7,5},{8,6},{9,7},{10,8},{11,9},{12,... | collective-permute-start | bytes 786440 | tf_op jit(solution)/shard_map/ppermute | solution.py:24
  61.8 23.8 %collective-permute-start.14 = (bf16[2,2,256,128]{3,2,1,0:T(8,128)(2,1)S(1)}, bf16[2,2,256,128]{3,2,1,0:T(8,128)(2,1)S(1)}, u32[]{:S(2)}, u32[]{:S(2)}) collective-permute-start(bf16[2,2,256,128]{3,2,1,0:T(8,128)(2,1)S(1)} %get-tuple-element.40), channel_id=1, source_target_pairs={{4,0},{5,1},{6,2},{7,3},{8,4},{9,5},{10,6},{11,7},{12,8},{13,9},{1... | collective-permute-start | bytes 786440 | tf_op jit(solution)/shard_map/ppermute | solution.py:24
  85.8 1.6 %collective-permute-start.17 = (bf16[2,2,256,128]{3,2,1,0:T(8,128)(2,1)S(1)}, bf16[2,2,256,128]{3,2,1,0:T(8,128)(2,1)S(1)}, u32[]{:S(2)}, u32[]{:S(2)}) collective-permute-start(bf16[2,2,256,128]{3,2,1,0:T(8,128)(2,1)S(1)} %get-tuple-element.46), channel_id=1, source_target_pairs={{0,1},{1,0},{2,3},{3,2},{4,5},{5,4},{6,7},{7,6},{8,9},{9,8},{10,11... | collective-permute-start | bytes 786440 | tf_op jit(solution)/shard_map/ppermute | solution.py:29

commit v2 on v1

--- a/solution.py
+++ b/solution.py
@@ -30,18 +30,17 @@
 
 
 def everywhere_sum(value):
+    count = lax.axis_size("ctx")
+    steps = [2**k for k in range(1, count.bit_length() - 1)] + [1]
+    for step in steps[:-1]:
+        other = swapped(value, step)
+        value = value + other
     dp_count = lax.axis_size("dp")
-    step = 1
-    while step < dp_count:
+    for step in (2**k for k in range(dp_count.bit_length() - 1)):
         other = lax.ppermute(value, "dp", [(i, i ^ step) for i in range(dp_count)])
         value = value + other
-        step *= 2
-    step = 1
-    while step < lax.axis_size("ctx"):
-        other = swapped(value, step)
-        value = value + other
-        step *= 2
-    return value
+    other = swapped(value, 1)
+    return value + other
 
 
 def nt(a, b):

time: 88.7 us -> 90.7 us (1.023)
  the two profiles are of different devices: /device:TPU:0 before, /device:TPU:17 now
where the time goes in v2:
time: 90.7 us; the launch traced here: 90.3 us
  waiting for transfers between devices  33.9 us (37%)
  Pallas kernels  28.2 us (31%)
  starting transfers between devices  26.7 us (29%)
    pallas_call x2, Pallas kernels, grads_call(): pl.pallas_call(grads_kernel, grid_spec=pltpu.PrefetchScalarGridSpec(num_s...  23.1 us
    ppermute x8, waiting for transfers between devices, shifted(): return lax.ppermute(value, 'ctx', pairs)  19.1 us
    ppermute x8, starting transfers between devices, shifted(): return lax.ppermute(value, 'ctx', pairs)  17.9 us
    ppermute x9, waiting for transfers between devices, swapped(): return lax.ppermute(value, 'ctx', [(i, i ^ bit) for i in range(count)])  12 us
    ppermute x9, starting transfers between devices, swapped(): return lax.ppermute(value, 'ctx', [(i, i ^ bit) for i in range(count)])  8.79 us
    pallas_call x6, Pallas kernels, simple_call(): pl.pallas_call(kernel, grid_spec=pltpu.PrefetchScalarGridSpec(num_scalar_...  5.08 us
    ppermute x1, waiting for transfers between devices, everywhere_sum(): other = lax.ppermute(value, 'dp', [(i, i ^ step) for i in range(dp_count)])  2.75 us
  transfers between devices with their start and end apart: 18, of which 10 were waited for; matrix products, arithmetic and copies ran while one was open for 0% of the time, Pallas kernels for 27%

profile of v2, /device:TPU:17, one launch (start us, length us, event | category | flops | bytes accessed | tf_op | source)
XLA Modules:
  0.0 90.3 jit_solution(15578476222933539789)
XLA Ops:
  0.6 1.1 %shard_map.85 = (bf16[2,2,256,128]{3,2,1,0:T(8,128)(2,1)S(1)}, bf16[2,2,256,128]{3,2,1,0:T(8,128)(2,1)S(1)}) custom-call(s32[1]{0:T(128)} %bitcast.where_ref, bf16[1,256,512]{2,1,0:T(8,128)(2,1)} %k_ref.1, bf16[1,256,512]{2,1,0:T(8,128)(2,1)} %v_ref.1), custom_call_target="tpu_custom_call" | custom-call | bytes 1048576 | tf_op jit(solution)/shard_map/pallas_call | solution.py:66
  1.8 0.0 copy-start
  1.8 0.7 copy-done
  2.5 1.6 %shard_map.86 = (bf16[2,256,1024]{2,1,0:T(8,128)(2,1)S(1)}, bf16[2,256,1024]{2,1,0:T(8,128)(2,1)S(1)}, f32[8,128]{1,0:T(8,128)S(1)}) custom-call(s32[1]{0:T(128)} %bitcast.where_ref, bf16[1,256,2048]{2,1,0:T(8,128)(2,1)} %q_ref.1, bf16[1,256,2048]{2,1,0:T(8,128)(2,1)} %g_ref.1, s32[1,256]{1,0:T(1,128)S(1)} %copy-done, ...), custom_call_target="tpu_custom_call" | custom-call | bytes 1048576 | tf_op jit(solution)/shard_map/pallas_call | solution.py:66
  4.0 0.7 collective-permute-start
  4.8 0.1 collective-permute-start.1
  4.9 2.6 %collective-permute-done.1.got = bf16[2,2,256,128]{3,2,1,0:T(8,128)(2,1)S(1)} collective-permute-done((bf16[2,2,256,128]{3,2,1,0:T(8,128)(2,1)S(1)}, bf16[2,2,256,128]{3,2,1,0:T(8,128)(2,1)S(1)}, u32[]{:S(2)}, u32[]{:S(2)}) %collective-permute-start.1) | collective-permute-done | bytes 262176 | tf_op jit(solution)/shard_map/ppermute | solution.py:29
  7.5 3.2 %collective-permute-start.5 = (bf16[2,2,256,128]{3,2,1,0:T(8,128)(2,1)S(1)}, bf16[2,2,256,128]{3,2,1,0:T(8,128)(2,1)S(1)}, u32[]{:S(2)}, u32[]{:S(2)}) collective-permute-start(bf16[2,2,256,128]{3,2,1,0:T(8,128)(2,1)S(1)} %get-tuple-element.32.kv0), channel_id=1, source_target_pairs={{0,4},{1,5},{2,6},{3,7},{4,8},{5,9},{6,10},{7,11},{8,12},{9,13},{1... | collective-permute-start | bytes 786440 | tf_op jit(solution)/shard_map/ppermute | solution.py:24
  10.7 3.1 %collective-permute-start.4 = (bf16[2,2,256,128]{3,2,1,0:T(8,128)(2,1)S(1)}, bf16[2,2,256,128]{3,2,1,0:T(8,128)(2,1)S(1)}, u32[]{:S(2)}, u32[]{:S(2)}) collective-permute-start(bf16[2,2,256,128]{3,2,1,0:T(8,128)(2,1)S(1)} %get-tuple-element.32.kv0), channel_id=1, source_target_pairs={{0,2},{1,3},{2,4},{3,5},{4,6},{5,7},{6,8},{7,9},{8,10},{9,11},{10,... | collective-permute-start | bytes 786440 | tf_op jit(solution)/shard_map/ppermute | solution.py:24
  13.8 0.0 copy-start.1
  13.9 1.9 %collective-permute-start.3 = (bf16[2,2,256,128]{3,2,1,0:T(8,128)(2,1)S(1)}, bf16[2,2,256,128]{3,2,1,0:T(8,128)(2,1)S(1)}, u32[]{:S(2)}, u32[]{:S(2)}) collective-permute-start(bf16[2,2,256,128]{3,2,1,0:T(8,128)(2,1)S(1)} %get-tuple-element.30.kv0), channel_id=1, source_target_pairs={{0,4},{1,5},{2,6},{3,7},{4,8},{5,9},{6,10},{7,11},{8,12},{9,13},{1... | collective-permute-start | bytes 786440 | tf_op jit(solution)/shard_map/ppermute | solution.py:24
  15.8 1.9 %collective-permute-start.2 = (bf16[2,2,256,128]{3,2,1,0:T(8,128)(2,1)S(1)}, bf16[2,2,256,128]{3,2,1,0:T(8,128)(2,1)S(1)}, u32[]{:S(2)}, u32[]{:S(2)}) collective-permute-start(bf16[2,2,256,128]{3,2,1,0:T(8,128)(2,1)S(1)} %get-tuple-element.30.kv0), channel_id=1, source_target_pairs={{0,2},{1,3},{2,4},{3,5},{4,6},{5,7},{6,8},{7,9},{8,10},{9,11},{10,... | collective-permute-start | bytes 786440 | tf_op jit(solution)/shard_map/ppermute | solution.py:24
  17.7 0.0 collective-permute-done.5.kv2
  17.7 5.7 %collective-permute-done.4.kv1 = bf16[2,2,256,128]{3,2,1,0:T(8,128)(2,1)S(1)} collective-permute-done((bf16[2,2,256,128]{3,2,1,0:T(8,128)(2,1)S(1)}, bf16[2,2,256,128]{3,2,1,0:T(8,128)(2,1)S(1)}, u32[]{:S(2)}, u32[]{:S(2)}) %collective-permute-start.4) | collective-permute-done | bytes 262176 | tf_op jit(solution)/shard_map/ppermute | solution.py:24
  23.4 0.0 collective-permute-done.got_qg
  23.4 0.0 copy-done.1
  23.4 11.6 %grads.3 = (bf16[256,512]{1,0:T(8,128)(2,1)S(1)}, bf16[256,512]{1,0:T(8,128)(2,1)S(1)}, f32[2,2,256,128]{3,2,1,0:T(8,128)S(1)}, bf16[2,2,256,128]{3,2,1,0:T(8,128)(2,1)S(1)}, bf16[2,2,256,128]{3,2,1,0:T(8,128)(2,1)S(1)}) custom-call(s32[1]{0:T(128)} %bitcast.where_ref, s32[1,8]{1,0:T(1,128)S(1)} %copy-done.1, ...), custom_call_target="tpu_custom_call" | custom-call | flops 2013265920 | bytes 6291456 | tf_op jit(solution)/shard_map/grads/pallas_call | solution.py:363
  35.0 2.1 %collective-permute-start.7 = (bf16[256,512]{1,0:T(8,128)(2,1)S(1)}, bf16[256,512]{1,0:T(8,128)(2,1)S(1)}, u32[]{:S(2)}, u32[]{:S(2)}) collective-permute-start(bf16[256,512]{1,0:T(8,128)(2,1)S(1)} %get-tuple-element.35), channel_id=1, source_target_pairs={{0,1},{1,0},{2,3},{3,2},{4,5},{5,4},{6,7},{7,6},{8,9},{9,8},{10,11... | collective-permute-start | bytes 786440 | tf_op jit(solution)/shard_map/ppermute | solution.py:29
  37.1 0.0 collective-permute-start.8
  37.1 2.5 %collective-permute-done.8 = f32[8,128]{1,0:T(8,128)S(1)} collective-permute-done((f32[8,128]{1,0:T(8,128)S(1)}, f32[8,128]{1,0:T(8,128)S(1)}, u32[]{:S(2)}, u32[]{:S(2)}) %collective-permute-start.8) | collective-permute-done | bytes 4128 | tf_op jit(solution)/shard_map/ppermute | solution.py:29
  39.6 0.0 collective-permute-start.9
  39.6 2.5 %collective-permute-done.9 = f32[8,128]{1,0:T(8,128)S(1)} collective-permute-done((f32[8,128]{1,0:T(8,128)S(1)}, f32[8,128]{1,0:T(8,128)S(1)}, u32[]{:S(2)}, u32[]{:S(2)}) %collective-permute-start.9) | collective-permute-done | bytes 4128 | tf_op jit(solution)/shard_map/ppermute | solution.py:29
  42.0 0.0 collective-permute-start.10
  42.0 3.4 %collective-permute-done.10 = f32[8,128]{1,0:T(8,128)S(1)} collective-permute-done((f32[8,128]{1,0:T(8,128)S(1)}, f32[8,128]{1,0:T(8,128)S(1)}, u32[]{:S(2)}, u32[]{:S(2)}) %collective-permute-start.10) | collective-permute-done | bytes 4128 | tf_op jit(solution)/shard_map/ppermute | solution.py:29
  45.4 0.0 collective-permute-start.11
  45.4 2.7 %collective-permute-done.11 = f32[8,128]{1,0:T(8,128)S(1)} collective-permute-done((f32[8,128]{1,0:T(8,128)S(1)}, f32[8,128]{1,0:T(8,128)S(1)}, u32[]{:S(2)}, u32[]{:S(2)}) %collective-permute-start.11) | collective-permute-done | bytes 4128 | tf_op jit(solution)/shard_map/ppermute | solution.py:40
  48.2 4.4 %collective-permute-start.12 = (f32[8,128]{1,0:T(8,128)S(1)}, f32[8,128]{1,0:T(8,128)S(1)}, u32[]{:S(2)}, u32[]{:S(2)}) collective-permute-start(f32[8,128]{1,0:T(8,128)S(1)} %add.18), channel_id=1, source_target_pairs={{0,1},{1,0},{2,3},{3,2},{4,5},{5,4},{6,7},{7,6},{8,9},{9,8},{10,11... | collective-permute-start | bytes 12296 | tf_op jit(solution)/shard_map/ppermute | solution.py:29
  52.5 1.9 %collective-permute-start.15 = (bf16[2,2,256,128]{3,2,1,0:T(8,128)(2,1)S(1)}, bf16[2,2,256,128]{3,2,1,0:T(8,128)(2,1)S(1)}, u32[]{:S(2)}, u32[]{:S(2)}) collective-permute-start(bf16[2,2,256,128]{3,2,1,0:T(8,128)(2,1)S(1)} %get-tuple-element.42), channel_id=1, source_target_pairs={{2,0},{3,1},{4,2},{5,3},{6,4},{7,5},{8,6},{9,7},{10,8},{11,9},{12,... | collective-permute-start | bytes 786440 | tf_op jit(solution)/shard_map/ppermute | solution.py:24
  54.5 0.0 collective-permute-done.3.kv2
  54.5 0.0 collective-permute-done.2.kv1
  54.5 11.6 %grads.2 = (bf16[256,512]{1,0:T(8,128)(2,1)S(1)}, bf16[256,512]{1,0:T(8,128)(2,1)S(1)}, f32[2,2,256,128]{3,2,1,0:T(8,128)S(1)}, bf16[2,2,256,128]{3,2,1,0:T(8,128)(2,1)S(1)}, bf16[2,2,256,128]{3,2,1,0:T(8,128)(2,1)S(1)}) custom-call(s32[1]{0:T(128)} %bitcast.where_ref, s32[1,8]{1,0:T(1,128)S(1)} %copy-done.1, ...), custom_call_target="tpu_custom_call" | custom-call | flops 2013265920 | bytes 6291456 | tf_op jit(solution)/shard_map/grads/pallas_call | solution.py:363
  66.0 0.1 collective-permute-start.6
  66.1 1.9 %collective-permute-start.16 = (bf16[2,2,256,128]{3,2,1,0:T(8,128)(2,1)S(1)}, bf16[2,2,256,128]{3,2,1,0:T(8,128)(2,1)S(1)}, u32[]{:S(2)}, u32[]{:S(2)}) collective-permute-start(bf16[2,2,256,128]{3,2,1,0:T(8,128)(2,1)S(1)} %get-tuple-element.43), channel_id=1, source_target_pairs={{4,0},{5,1},{6,2},{7,3},{8,4},{9,5},{10,6},{11,7},{12,8},{13,9},{1... | collective-permute-start | bytes 786440 | tf_op jit(solution)/shard_map/ppermute | solution.py:24
  68.0 0.0 collective-permute-done.12
  68.1 1.9 %collective-permute-start.13 = (bf16[2,2,256,128]{3,2,1,0:T(8,128)(2,1)S(1)}, bf16[2,2,256,128]{3,2,1,0:T(8,128)(2,1)S(1)}, u32[]{:S(2)}, u32[]{:S(2)}) collective-permute-start(bf16[2,2,256,128]{3,2,1,0:T(8,128)(2,1)S(1)} %get-tuple-element.39), channel_id=1, source_target_pairs={{2,0},{3,1},{4,2},{5,3},{6,4},{7,5},{8,6},{9,7},{10,8},{11,9},{12,... | collective-permute-start | bytes 786440 | tf_op jit(solution)/shard_map/ppermute | solution.py:24
  70.0 0.0 collective-permute-done.7.refs_3_
  70.0 1.9 %collective-permute-start.14 = (bf16[2,2,256,128]{3,2,1,0:T(8,128)(2,1)S(1)}, bf16[2,2,256,128]{3,2,1,0:T(8,128)(2,1)S(1)}, u32[]{:S(2)}, u32[]{:S(2)}) collective-permute-start(bf16[2,2,256,128]{3,2,1,0:T(8,128)(2,1)S(1)} %get-tuple-element.40), channel_id=1, source_target_pairs={{4,0},{5,1},{6,2},{7,3},{8,4},{9,5},{10,6},{11,7},{12,8},{13,9},{1... | collective-permute-start | bytes 786440 | tf_op jit(solution)/shard_map/ppermute | solution.py:24
  71.9 0.0 collective-permute-done.6.refs_2_
  71.9 1.3 %shard_map.88 = (bf16[1,256,2048]{2,1,0:T(8,128)(2,1)}, f32[8,128]{1,0:T(8,128)S(1)}) custom-call(s32[1]{0:T(128)} %bitcast.where_ref, bf16[256,512]{1,0:T(8,128)(2,1)S(1)} %get-tuple-element.31.refs_0_, bf16[256,512]{1,0:T(8,128)(2,1)S(1)} %get-tuple-element.33.refs_1_, bf16[256,512]{1,0:T(8,128)(2,1)S(1)} %collective-permute-done.6.refs_2_, ...), custom_call_target="tpu_custom_call" | custom-call | bytes 1048576 | tf_op jit(solution)/shard_map/pallas_call | solution.py:66
  73.2 0.0 collective-permute-done.15.refs_4_
  73.2 2.2 %collective-permute-done.16.refs_5_ = bf16[2,2,256,128]{3,2,1,0:T(8,128)(2,1)S(1)} collective-permute-done((bf16[2,2,256,128]{3,2,1,0:T(8,128)(2,1)S(1)}, bf16[2,2,256,128]{3,2,1,0:T(8,128)(2,1)S(1)}, u32[]{:S(2)}, u32[]{:S(2)}) %collective-permute-start.16) | collective-permute-done | bytes 262176 | tf_op jit(solution)/shard_map/ppermute | solution.py:24
  75.4 3.7 %collective-permute-done.13.refs_1_ = bf16[2,2,256,128]{3,2,1,0:T(8,128)(2,1)S(1)} collective-permute-done((bf16[2,2,256,128]{3,2,1,0:T(8,128)(2,1)S(1)}, bf16[2,2,256,128]{3,2,1,0:T(8,128)(2,1)S(1)}, u32[]{:S(2)}, u32[]{:S(2)}) %collective-permute-start.13) | collective-permute-done | bytes 262176 | tf_op jit(solution)/shard_map/ppermute | solution.py:24
  79.1 7.5 %collective-permute-done.14.refs_2_ = bf16[2,2,256,128]{3,2,1,0:T(8,128)(2,1)S(1)} collective-permute-done((bf16[2,2,256,128]{3,2,1,0:T(8,128)(2,1)S(1)}, bf16[2,2,256,128]{3,2,1,0:T(8,128)(2,1)S(1)}, u32[]{:S(2)}, u32[]{:S(2)}) %collective-permute-start.14) | collective-permute-done | bytes 262176 | tf_op jit(solution)/shard_map/ppermute | solution.py:24
  86.6 0.2 shard_map.89
  86.8 1.4 %collective-permute-start.17 = (bf16[2,2,256,128]{3,2,1,0:T(8,128)(2,1)S(1)}, bf16[2,2,256,128]{3,2,1,0:T(8,128)(2,1)S(1)}, u32[]{:S(2)}, u32[]{:S(2)}) collective-permute-start(bf16[2,2,256,128]{3,2,1,0:T(8,128)(2,1)S(1)} %get-tuple-element.46), channel_id=1, source_target_pairs={{0,1},{1,0},{2,3},{3,2},{4,5},{5,4},{6,7},{7,6},{8,9},{9,8},{10,11... | collective-permute-start | bytes 786440 | tf_op jit(solution)/shard_map/ppermute | solution.py:29
  88.2 1.2 %collective-permute-done.17.got_ref = bf16[2,2,256,128]{3,2,1,0:T(8,128)(2,1)S(1)} collective-permute-done((bf16[2,2,256,128]{3,2,1,0:T(8,128)(2,1)S(1)}, bf16[2,2,256,128]{3,2,1,0:T(8,128)(2,1)S(1)}, u32[]{:S(2)}, u32[]{:S(2)}) %collective-permute-start.17) | collective-permute-done | bytes 262176 | tf_op jit(solution)/shard_map/ppermute | solution.py:29
  89.4 0.9 shard_map.90
  (6 shorter events, 0.1 us)
Async XLA Ops:
  1.8 0.7 copy-start
  4.0 19.4 %collective-permute-start = (bf16[2,256,1024]{2,1,0:T(8,128)(2,1)S(1)}, bf16[2,256,1024]{2,1,0:T(8,128)(2,1)S(1)}, u32[]{:S(2)}, u32[]{:S(2)}) collective-permute-start(bf16[2,256,1024]{2,1,0:T(8,128)(2,1)S(1)} %get-tuple-element.28), channel_id=1, source_target_pairs={{0,1},{1,0},{2,3},{3,2},{4,5},{5,4},{6,7},{7,6},{8,9},{9,8},{10,11... | collective-permute-start | bytes 3145736 | tf_op jit(solution)/shard_map/ppermute | solution.py:29
  4.8 2.7 %collective-permute-start.1 = (bf16[2,2,256,128]{3,2,1,0:T(8,128)(2,1)S(1)}, bf16[2,2,256,128]{3,2,1,0:T(8,128)(2,1)S(1)}, u32[]{:S(2)}, u32[]{:S(2)}) collective-permute-start(bf16[2,2,256,128]{3,2,1,0:T(8,128)(2,1)S(1)} %get-tuple-element.26.after_ref), channel_id=1, source_target_pairs={{0,1},{1,0},{2,3},{3,2},{4,5},{5,4},{6,7},{7,6},{8,9},{9,8},{10,11... | collective-permute-start | bytes 786440 | tf_op jit(solution)/shard_map/ppermute | solution.py:29
  7.5 10.2 %collective-permute-start.5 = (bf16[2,2,256,128]{3,2,1,0:T(8,128)(2,1)S(1)}, bf16[2,2,256,128]{3,2,1,0:T(8,128)(2,1)S(1)}, u32[]{:S(2)}, u32[]{:S(2)}) collective-permute-start(bf16[2,2,256,128]{3,2,1,0:T(8,128)(2,1)S(1)} %get-tuple-element.32.kv0), channel_id=1, source_target_pairs={{0,4},{1,5},{2,6},{3,7},{4,8},{5,9},{6,10},{7,11},{8,12},{9,13},{1... | collective-permute-start | bytes 786440 | tf_op jit(solution)/shard_map/ppermute | solution.py:24
  10.7 12.7 %collective-permute-start.4 = (bf16[2,2,256,128]{3,2,1,0:T(8,128)(2,1)S(1)}, bf16[2,2,256,128]{3,2,1,0:T(8,128)(2,1)S(1)}, u32[]{:S(2)}, u32[]{:S(2)}) collective-permute-start(bf16[2,2,256,128]{3,2,1,0:T(8,128)(2,1)S(1)} %get-tuple-element.32.kv0), channel_id=1, source_target_pairs={{0,2},{1,3},{2,4},{3,5},{4,6},{5,7},{6,8},{7,9},{8,10},{9,11},{10,... | collective-permute-start | bytes 786440 | tf_op jit(solution)/shard_map/ppermute | solution.py:24
  13.8 9.6 %copy-start.1 = (s32[1,8]{1,0:T(1,128)S(1)}, s32[1,8]{1,0:T(1,128)}, u32[]{:S(2)}) copy-start(s32[1,8]{1,0:T(1,128)} %lengths_ref.3) | copy-start | bytes 100
  13.9 40.6 %collective-permute-start.3 = (bf16[2,2,256,128]{3,2,1,0:T(8,128)(2,1)S(1)}, bf16[2,2,256,128]{3,2,1,0:T(8,128)(2,1)S(1)}, u32[]{:S(2)}, u32[]{:S(2)}) collective-permute-start(bf16[2,2,256,128]{3,2,1,0:T(8,128)(2,1)S(1)} %get-tuple-element.30.kv0), channel_id=1, source_target_pairs={{0,4},{1,5},{2,6},{3,7},{4,8},{5,9},{6,10},{7,11},{8,12},{9,13},{1... | collective-permute-start | bytes 786440 | tf_op jit(solution)/shard_map/ppermute | solution.py:24
  15.8 38.7 %collective-permute-start.2 = (bf16[2,2,256,128]{3,2,1,0:T(8,128)(2,1)S(1)}, bf16[2,2,256,128]{3,2,1,0:T(8,128)(2,1)S(1)}, u32[]{:S(2)}, u32[]{:S(2)}) collective-permute-start(bf16[2,2,256,128]{3,2,1,0:T(8,128)(2,1)S(1)} %get-tuple-element.30.kv0), channel_id=1, source_target_pairs={{0,2},{1,3},{2,4},{3,5},{4,6},{5,7},{6,8},{7,9},{8,10},{9,11},{10,... | collective-permute-start | bytes 786440 | tf_op jit(solution)/shard_map/ppermute | solution.py:24
  35.0 35.0 %collective-permute-start.7 = (bf16[256,512]{1,0:T(8,128)(2,1)S(1)}, bf16[256,512]{1,0:T(8,128)(2,1)S(1)}, u32[]{:S(2)}, u32[]{:S(2)}) collective-permute-start(bf16[256,512]{1,0:T(8,128)(2,1)S(1)} %get-tuple-element.35), channel_id=1, source_target_pairs={{0,1},{1,0},{2,3},{3,2},{4,5},{5,4},{6,7},{7,6},{8,9},{9,8},{10,11... | collective-permute-start | bytes 786440 | tf_op jit(solution)/shard_map/ppermute | solution.py:29
  37.1 2.5 %collective-permute-start.8 = (f32[8,128]{1,0:T(8,128)S(1)}, f32[8,128]{1,0:T(8,128)S(1)}, u32[]{:S(2)}, u32[]{:S(2)}) collective-permute-start(f32[8,128]{1,0:T(8,128)S(1)} %get-tuple-element.36), channel_id=1, source_target_pairs={{0,2},{1,3},{2,0},{3,1},{4,6},{5,7},{6,4},{7,5},{8,10},{9,11},{10,... | collective-permute-start | bytes 12296 | tf_op jit(solution)/shard_map/ppermute | solution.py:29
  39.6 2.5 %collective-permute-start.9 = (f32[8,128]{1,0:T(8,128)S(1)}, f32[8,128]{1,0:T(8,128)S(1)}, u32[]{:S(2)}, u32[]{:S(2)}) collective-permute-start(f32[8,128]{1,0:T(8,128)S(1)} %add.15), channel_id=1, source_target_pairs={{0,4},{1,5},{2,6},{3,7},{4,0},{5,1},{6,2},{7,3},{8,12},{9,13},{10,... | collective-permute-start | bytes 12296 | tf_op jit(solution)/shard_map/ppermute | solution.py:29
  42.0 3.4 %collective-permute-start.10 = (f32[8,128]{1,0:T(8,128)S(1)}, f32[8,128]{1,0:T(8,128)S(1)}, u32[]{:S(2)}, u32[]{:S(2)}) collective-permute-start(f32[8,128]{1,0:T(8,128)S(1)} %add.16), channel_id=1, source_target_pairs={{0,8},{1,9},{2,10},{3,11},{4,12},{5,13},{6,14},{7,15},{8,0},{9,1},... | collective-permute-start | bytes 12296 | tf_op jit(solution)/shard_map/ppermute | solution.py:29
  45.4 2.8 %collective-permute-start.11 = (f32[8,128]{1,0:T(8,128)S(1)}, f32[8,128]{1,0:T(8,128)S(1)}, u32[]{:S(2)}, u32[]{:S(2)}) collective-permute-start(f32[8,128]{1,0:T(8,128)S(1)} %add.17), channel_id=1, source_target_pairs={{0,16},{16,0},{1,17},{17,1},{2,18},{18,2},{3,19},{19,3},{4,20},{20... | collective-permute-start | bytes 12296 | tf_op jit(solution)/shard_map/ppermute | solution.py:40
  48.2 19.9 %collective-permute-start.12 = (f32[8,128]{1,0:T(8,128)S(1)}, f32[8,128]{1,0:T(8,128)S(1)}, u32[]{:S(2)}, u32[]{:S(2)}) collective-permute-start(f32[8,128]{1,0:T(8,128)S(1)} %add.18), channel_id=1, source_target_pairs={{0,1},{1,0},{2,3},{3,2},{4,5},{5,4},{6,7},{7,6},{8,9},{9,8},{10,11... | collective-permute-start | bytes 12296 | tf_op jit(solution)/shard_map/ppermute | solution.py:29
  52.5 20.7 %collective-permute-start.15 = (bf16[2,2,256,128]{3,2,1,0:T(8,128)(2,1)S(1)}, bf16[2,2,256,128]{3,2,1,0:T(8,128)(2,1)S(1)}, u32[]{:S(2)}, u32[]{:S(2)}) collective-permute-start(bf16[2,2,256,128]{3,2,1,0:T(8,128)(2,1)S(1)} %get-tuple-element.42), channel_id=1, source_target_pairs={{2,0},{3,1},{4,2},{5,3},{6,4},{7,5},{8,6},{9,7},{10,8},{11,9},{12,... | collective-permute-start | bytes 786440 | tf_op jit(solution)/shard_map/ppermute | solution.py:24
  66.0 5.9 %collective-permute-start.6 = (bf16[256,512]{1,0:T(8,128)(2,1)S(1)}, bf16[256,512]{1,0:T(8,128)(2,1)S(1)}, u32[]{:S(2)}, u32[]{:S(2)}) collective-permute-start(bf16[256,512]{1,0:T(8,128)(2,1)S(1)} %get-tuple-element.34), channel_id=1, source_target_pairs={{0,1},{1,0},{2,3},{3,2},{4,5},{5,4},{6,7},{7,6},{8,9},{9,8},{10,11... | collective-permute-start | bytes 786440 | tf_op jit(solution)/shard_map/ppermute | solution.py:29
  66.1 9.3 %collective-permute-start.16 = (bf16[2,2,256,128]{3,2,1,0:T(8,128)(2,1)S(1)}, bf16[2,2,256,128]{3,2,1,0:T(8,128)(2,1)S(1)}, u32[]{:S(2)}, u32[]{:S(2)}) collective-permute-start(bf16[2,2,256,128]{3,2,1,0:T(8,128)(2,1)S(1)} %get-tuple-element.43), channel_id=1, source_target_pairs={{4,0},{5,1},{6,2},{7,3},{8,4},{9,5},{10,6},{11,7},{12,8},{13,9},{1... | collective-permute-start | bytes 786440 | tf_op jit(solution)/shard_map/ppermute | solution.py:24
  68.1 11.0 %collective-permute-start.13 = (bf16[2,2,256,128]{3,2,1,0:T(8,128)(2,1)S(1)}, bf16[2,2,256,128]{3,2,1,0:T(8,128)(2,1)S(1)}, u32[]{:S(2)}, u32[]{:S(2)}) collective-permute-start(bf16[2,2,256,128]{3,2,1,0:T(8,128)(2,1)S(1)} %get-tuple-element.39), channel_id=1, source_target_pairs={{2,0},{3,1},{4,2},{5,3},{6,4},{7,5},{8,6},{9,7},{10,8},{11,9},{12,... | collective-permute-start | bytes 786440 | tf_op jit(solution)/shard_map/ppermute | solution.py:24
  70.0 16.6 %collective-permute-start.14 = (bf16[2,2,256,128]{3,2,1,0:T(8,128)(2,1)S(1)}, bf16[2,2,256,128]{3,2,1,0:T(8,128)(2,1)S(1)}, u32[]{:S(2)}, u32[]{:S(2)}) collective-permute-start(bf16[2,2,256,128]{3,2,1,0:T(8,128)(2,1)S(1)} %get-tuple-element.40), channel_id=1, source_target_pairs={{4,0},{5,1},{6,2},{7,3},{8,4},{9,5},{10,6},{11,7},{12,8},{13,9},{1... | collective-permute-start | bytes 786440 | tf_op jit(solution)/shard_map/ppermute | solution.py:24
  86.8 2.6 %collective-permute-start.17 = (bf16[2,2,256,128]{3,2,1,0:T(8,128)(2,1)S(1)}, bf16[2,2,256,128]{3,2,1,0:T(8,128)(2,1)S(1)}, u32[]{:S(2)}, u32[]{:S(2)}) collective-permute-start(bf16[2,2,256,128]{3,2,1,0:T(8,128)(2,1)S(1)} %get-tuple-element.46), channel_id=1, source_target_pairs={{0,1},{1,0},{2,3},{3,2},{4,5},{5,4},{6,7},{7,6},{8,9},{9,8},{10,11... | collective-permute-start | bytes 786440 | tf_op jit(solution)/shard_map/ppermute | solution.py:29

commit v3 on v2

--- a/solution.py
+++ b/solution.py
@@ -121,7 +121,8 @@
 
 def split_qg_call(where, query_rows, out_grad, loss_mask, after):
     rows = query_rows.shape[1]
-    width = MINE * GROUP * HD
+    heads = MINE * GROUP
+    width = heads * HD
 
     def kernel(where_ref, q_ref, g_ref, mask_ref, after_ref, give, own, token, g_s, sems):
         parity = where_ref[0] & 1
@@ -129,31 +130,37 @@
         for i, (base, out) in enumerate(((1 - parity, give), (parity, own))):
             columns = pl.ds(pl.multiple_of(base * width, width), width)
             g_copy = pltpu.make_async_copy(g_ref.at[0, :, columns], g_s.at[i], sems.at[i, 0])
-            q_copy = pltpu.make_async_copy(q_ref.at[0, :, columns], out.at[0], sems.at[i, 1])
             g_copy.start()
-            q_copy.start()
-            pieces.append((g_copy, q_copy, out))
+            q_copies = []
+            for h in range(heads):
+                one = pl.ds(pl.multiple_of(base * width + h * HD, HD), HD)
+                q_copies.append(
+                    pltpu.make_async_copy(q_ref.at[0, :, one], out.at[0, h], sems.at[i, 1 + h])
+                )
+                q_copies[-1].start()
+            pieces.append((g_copy, q_copies, out))
         keep_rows = mask_column(mask_ref)
         local = jnp.sum(mask_ref[...].astype(jnp.float32), axis=1, keepdims=True)
         token[...] = jnp.broadcast_to(local, token.shape)
-        for i, (g_copy, q_copy, out) in enumerate(pieces):
+        for i, (g_copy, q_copies, out) in enumerate(pieces):
             g_copy.wait()
-            for h in range(MINE * GROUP):
+            for h in range(heads):
                 columns = slice(h * HD, (h + 1) * HD)
-                out[1, :, columns] = (g_s[i, :, columns].astype(jnp.float32) * keep_rows).astype(
+                out[1, h] = (g_s[i, :, columns].astype(jnp.float32) * keep_rows).astype(
                     jnp.bfloat16
                 )
-            q_copy.wait()
+            for copy in q_copies:
+                copy.wait()
 
     shape = [
-        jax.ShapeDtypeStruct((2, rows, width), jnp.bfloat16),
-        jax.ShapeDtypeStruct((2, rows, width), jnp.bfloat16),
+        jax.ShapeDtypeStruct((2, heads, rows, HD), jnp.bfloat16),
+        jax.ShapeDtypeStruct((2, heads, rows, HD), jnp.bfloat16),
         jax.ShapeDtypeStruct((8, HD), jnp.float32),
     ]
     return simple_call(
         kernel, where, [in_hbm(), in_hbm(), in_vmem(), pl.BlockSpec(memory_space=pl.ANY)], shape,
         query_rows, out_grad, loss_mask, after,
-        scratch=[pltpu.VMEM((2, rows, width), jnp.bfloat16), pltpu.SemaphoreType.DMA((2, 2))],
+        scratch=[pltpu.VMEM((2, rows, width), jnp.bfloat16), pltpu.SemaphoreType.DMA((2, 1 + heads))],
     )
 
 
@@ -225,18 +232,11 @@
 def grads_kernel(
     where_ref, lengths_ref, own_qg, got_qg, kv0, kv1, kv2,
     own_dq, sib_dq, out0, out1, out2,
-    q_s, g_s, k_s, v_s, kt_s, e_s, dp_s, mb_s, m_s, l_s, w_s, dqt_s, dk_s, dv_s,
+    k_s, v_s, kt_s, e_s, dp_s, mb_s, m_s, l_s, w_s, dqt_s, dk_s, dv_s,
 ):
-    rows = own_qg.shape[1]
+    rows = own_qg.shape[2]
     my_index = where_ref[0]
     doc_count = lengths_ref.shape[1]
-    for h in range(GROUP):
-        columns = slice(h * HD, (h + 1) * HD)
-        at = slice(h * rows, (h + 1) * rows)
-        q_s[0, at] = own_qg[0, :, columns]
-        q_s[1, at] = got_qg[0, :, columns]
-        g_s[0, at] = own_qg[1, :, columns]
-        g_s[1, at] = got_qg[1, :, columns]
     for d, kv in enumerate((kv0, kv1, kv2)):
         for p in range(2):
             k_s[2 * d + p] = kv[p, 0]
@@ -245,7 +245,8 @@
     dk_s[...] = jnp.zeros_like(dk_s)
     dv_s[...] = jnp.zeros_like(dv_s)
 
-    def per_q(qb, _):
+    def per_q(qb, qg, dq):
+        q_s, g_s = qg.at[0], qg.at[1]
         q_start = (my_index ^ qb) * rows
 
         def doc_step(j, state):
@@ -280,14 +281,14 @@
                 k = k_s[kb]
                 v = v_s[kb]
                 for h in range(GROUP):
-                    s = nt(k, q_s[qb, h * rows : (h + 1) * rows]) * EXP2_SCALE
+                    s = nt(k, q_s[h])
                     if bias is not None:
                         s = s + bias
-                    dp = nt(v, g_s[qb, h * rows : (h + 1) * rows])
+                    dp = nt(v, g_s[h])
                     m_old = m_s[h]
                     m_new = jnp.maximum(m_old, jnp.max(s, axis=0, keepdims=True))
-                    keep = jnp.exp2(m_old - m_new)
-                    e = jnp.exp2(s - m_new)
+                    keep = jnp.exp2((m_old - m_new) * EXP2_SCALE)
+                    e = jnp.exp2((s - m_new) * EXP2_SCALE)
                     l_s[h] = l_s[h] * keep + jnp.sum(e, axis=0, keepdims=True)
                     w_s[h] = w_s[h] * keep + jnp.sum(e * dp, axis=0, keepdims=True)
                     m_s[h] = m_new
@@ -320,32 +321,24 @@
                 for h in range(GROUP):
                     inverse = 1.0 / l_s[h]
                     grad_dot = w_s[h] * inverse
-                    alpha = jnp.exp2(mb_s[kb * GROUP + h] - m_s[h]) * inverse
+                    alpha = jnp.exp2((mb_s[kb * GROUP + h] - m_s[h]) * EXP2_SCALE) * inverse
                     p = e_s[kb * GROUP + h] * alpha
                     ds_all.append((p * (dp_s[kb * GROUP + h] - grad_dot)).astype(jnp.bfloat16))
                     p_all.append(p.astype(jnp.bfloat16))
                 ds = jnp.concatenate(ds_all, 1)
-                dv_s[kb] += nn(jnp.concatenate(p_all, 1), g_s[qb])
-                dk_s[kb] += nn(ds, q_s[qb])
+                dv_s[kb] += nn(jnp.concatenate(p_all, 1), g_s[...].reshape(GROUP * rows, HD))
+                dk_s[kb] += nn(ds, q_s[...].reshape(GROUP * rows, HD))
                 dqt_s[...] += nn(kt_s[kb], ds)
 
             return 0
 
         lax.fori_loop(0, BLOCKS, phase_b, 0)
 
-        @pl.when(qb == 0)
-        def _():
-            for h in range(GROUP):
-                own_dq[:, h * HD : (h + 1) * HD] = dqt_s[:, h * rows : (h + 1) * rows].T.astype(own_dq.dtype)
-
-        @pl.when(qb == 1)
-        def _():
-            for h in range(GROUP):
-                sib_dq[:, h * HD : (h + 1) * HD] = dqt_s[:, h * rows : (h + 1) * rows].T.astype(sib_dq.dtype)
-
-        return 0
-
-    lax.fori_loop(0, 2, per_q, 0)
+        for h in range(GROUP):
+            dq[:, h * HD : (h + 1) * HD] = dqt_s[:, h * rows : (h + 1) * rows].T.astype(dq.dtype)
+
+    per_q(0, own_qg, own_dq)
+    per_q(1, got_qg, sib_dq)
     for d, out in enumerate((out0, out1, out2)):
         for p in range(2):
             out[p, 0] = dk_s[2 * d + p].astype(out.dtype)
@@ -353,9 +346,9 @@
 
 
 def grads_call(head, where, lengths, own_qg, got_qg, kv0, kv1, kv2):
-    rows = own_qg.shape[1]
+    rows = own_qg.shape[2]
     wide = GROUP * HD
-    half = pl.BlockSpec((2, rows, wide), lambda i, w: (0, 0, head))
+    half = pl.BlockSpec((2, GROUP, rows, HD), lambda i, w: (0, head, 0, 0))
     f32 = jnp.float32
     bf16 = jnp.bfloat16
     tiles = BLOCKS * GROUP
@@ -371,8 +364,6 @@
             ],
             out_specs=[in_vmem() for _ in range(5)],
             scratch_shapes=[
-                pltpu.VMEM((2, GROUP * rows, HD), bf16),
-                pltpu.VMEM((2, GROUP * rows, HD), bf16),
                 pltpu.VMEM((BLOCKS, rows, HD), bf16),
                 pltpu.VMEM((BLOCKS, rows, HD), bf16),
                 pltpu.VMEM((BLOCKS, HD, rows), bf16),

time: 90.7 us -> 90.4 us (level)
  no operation moved by 1% of the time
where the time goes in v3:
time: 90.4 us; the launch traced here: 90 us
  waiting for transfers between devices  33.9 us (38%)
  Pallas kernels  27.9 us (31%)
  starting transfers between devices  26.7 us (30%)
    pallas_call x2, Pallas kernels, grads_call(): pl.pallas_call(grads_kernel, grid_spec=pltpu.PrefetchScalarGridSpec(num_s...  22.7 us
    ppermute x8, waiting for transfers between devices, shifted(): return lax.ppermute(value, 'ctx', pairs)  19.1 us
    ppermute x8, starting transfers between devices, shifted(): return lax.ppermute(value, 'ctx', pairs)  17.9 us
    ppermute x9, waiting for transfers between devices, swapped(): return lax.ppermute(value, 'ctx', [(i, i ^ bit) for i in range(count)])  12 us
    ppermute x9, starting transfers between devices, swapped(): return lax.ppermute(value, 'ctx', [(i, i ^ bit) for i in range(count)])  8.81 us
    pallas_call x6, Pallas kernels, simple_call(): pl.pallas_call(kernel, grid_spec=pltpu.PrefetchScalarGridSpec(num_scalar_...  5.18 us
    ppermute x1, waiting for transfers between devices, everywhere_sum(): other = lax.ppermute(value, 'dp', [(i, i ^ step) for i in range(dp_count)])  2.75 us
  transfers between devices with their start and end apart: 18, of which 10 were waited for; matrix products, arithmetic and copies ran while one was open for 0% of the time, Pallas kernels for 27%

profile of v3, /device:TPU:17, one launch (start us, length us, event | category | flops | bytes accessed | tf_op | source)
XLA Modules:
  0.0 90.0 jit_solution(6982537365093112787)
XLA Ops:
  0.6 1.1 %shard_map.85 = (bf16[2,2,256,128]{3,2,1,0:T(8,128)(2,1)S(1)}, bf16[2,2,256,128]{3,2,1,0:T(8,128)(2,1)S(1)}) custom-call(s32[1]{0:T(128)} %bitcast.where_ref, bf16[1,256,512]{2,1,0:T(8,128)(2,1)} %k_ref.1, bf16[1,256,512]{2,1,0:T(8,128)(2,1)} %v_ref.1), custom_call_target="tpu_custom_call" | custom-call | bytes 1048576 | tf_op jit(solution)/shard_map/pallas_call | solution.py:66
  1.8 0.0 copy-start
  1.8 0.7 copy-done
  2.5 1.7 %shard_map.86 = (bf16[2,8,256,128]{3,2,1,0:T(8,128)(2,1)S(1)}, bf16[2,8,256,128]{3,2,1,0:T(8,128)(2,1)S(1)}, f32[8,128]{1,0:T(8,128)S(1)}) custom-call(s32[1]{0:T(128)} %bitcast.where_ref, bf16[1,256,2048]{2,1,0:T(8,128)(2,1)} %q_ref.1, bf16[1,256,2048]{2,1,0:T(8,128)(2,1)} %g_ref.1, s32[1,256]{1,0:T(1,128)S(1)} %copy-done, ...), custom_call_target="tpu_custom_call" | custom-call | bytes 1048576 | tf_op jit(solution)/shard_map/pallas_call | solution.py:66
  4.1 0.7 collective-permute-start
  4.9 0.1 collective-permute-start.1
  5.0 2.6 %collective-permute-done.1.got = bf16[2,2,256,128]{3,2,1,0:T(8,128)(2,1)S(1)} collective-permute-done((bf16[2,2,256,128]{3,2,1,0:T(8,128)(2,1)S(1)}, bf16[2,2,256,128]{3,2,1,0:T(8,128)(2,1)S(1)}, u32[]{:S(2)}, u32[]{:S(2)}) %collective-permute-start.1) | collective-permute-done | bytes 262176 | tf_op jit(solution)/shard_map/ppermute | solution.py:29
  7.6 3.2 %collective-permute-start.5 = (bf16[2,2,256,128]{3,2,1,0:T(8,128)(2,1)S(1)}, bf16[2,2,256,128]{3,2,1,0:T(8,128)(2,1)S(1)}, u32[]{:S(2)}, u32[]{:S(2)}) collective-permute-start(bf16[2,2,256,128]{3,2,1,0:T(8,128)(2,1)S(1)} %get-tuple-element.32.kv0), channel_id=1, source_target_pairs={{0,4},{1,5},{2,6},{3,7},{4,8},{5,9},{6,10},{7,11},{8,12},{9,13},{1... | collective-permute-start | bytes 786440 | tf_op jit(solution)/shard_map/ppermute | solution.py:24
  10.8 3.1 %collective-permute-start.4 = (bf16[2,2,256,128]{3,2,1,0:T(8,128)(2,1)S(1)}, bf16[2,2,256,128]{3,2,1,0:T(8,128)(2,1)S(1)}, u32[]{:S(2)}, u32[]{:S(2)}) collective-permute-start(bf16[2,2,256,128]{3,2,1,0:T(8,128)(2,1)S(1)} %get-tuple-element.32.kv0), channel_id=1, source_target_pairs={{0,2},{1,3},{2,4},{3,5},{4,6},{5,7},{6,8},{7,9},{8,10},{9,11},{10,... | collective-permute-start | bytes 786440 | tf_op jit(solution)/shard_map/ppermute | solution.py:24
  13.9 0.0 copy-start.1
  14.0 1.9 %collective-permute-start.3 = (bf16[2,2,256,128]{3,2,1,0:T(8,128)(2,1)S(1)}, bf16[2,2,256,128]{3,2,1,0:T(8,128)(2,1)S(1)}, u32[]{:S(2)}, u32[]{:S(2)}) collective-permute-start(bf16[2,2,256,128]{3,2,1,0:T(8,128)(2,1)S(1)} %get-tuple-element.30.kv0), channel_id=1, source_target_pairs={{0,4},{1,5},{2,6},{3,7},{4,8},{5,9},{6,10},{7,11},{8,12},{9,13},{1... | collective-permute-start | bytes 786440 | tf_op jit(solution)/shard_map/ppermute | solution.py:24
  15.9 1.9 %collective-permute-start.2 = (bf16[2,2,256,128]{3,2,1,0:T(8,128)(2,1)S(1)}, bf16[2,2,256,128]{3,2,1,0:T(8,128)(2,1)S(1)}, u32[]{:S(2)}, u32[]{:S(2)}) collective-permute-start(bf16[2,2,256,128]{3,2,1,0:T(8,128)(2,1)S(1)} %get-tuple-element.30.kv0), channel_id=1, source_target_pairs={{0,2},{1,3},{2,4},{3,5},{4,6},{5,7},{6,8},{7,9},{8,10},{9,11},{10,... | collective-permute-start | bytes 786440 | tf_op jit(solution)/shard_map/ppermute | solution.py:24
  17.8 0.0 collective-permute-done.5.kv2
  17.8 5.7 %collective-permute-done.4.kv1 = bf16[2,2,256,128]{3,2,1,0:T(8,128)(2,1)S(1)} collective-permute-done((bf16[2,2,256,128]{3,2,1,0:T(8,128)(2,1)S(1)}, bf16[2,2,256,128]{3,2,1,0:T(8,128)(2,1)S(1)}, u32[]{:S(2)}, u32[]{:S(2)}) %collective-permute-start.4) | collective-permute-done | bytes 262176 | tf_op jit(solution)/shard_map/ppermute | solution.py:24
  23.5 0.0 collective-permute-done.got_qg
  23.5 0.0 copy-done.1
  23.5 11.3 %grads.3 = (bf16[256,512]{1,0:T(8,128)(2,1)S(1)}, bf16[256,512]{1,0:T(8,128)(2,1)S(1)}, f32[2,2,256,128]{3,2,1,0:T(8,128)S(1)}, bf16[2,2,256,128]{3,2,1,0:T(8,128)(2,1)S(1)}, bf16[2,2,256,128]{3,2,1,0:T(8,128)(2,1)S(1)}) custom-call(s32[1]{0:T(128)} %bitcast.where_ref, s32[1,8]{1,0:T(1,128)S(1)} %copy-done.1, ...), custom_call_target="tpu_custom_call" | custom-call | flops 2013265920 | bytes 6291456 | tf_op jit(solution)/shard_map/grads/pallas_call | solution.py:356
  34.9 2.1 %collective-permute-start.7 = (bf16[256,512]{1,0:T(8,128)(2,1)S(1)}, bf16[256,512]{1,0:T(8,128)(2,1)S(1)}, u32[]{:S(2)}, u32[]{:S(2)}) collective-permute-start(bf16[256,512]{1,0:T(8,128)(2,1)S(1)} %get-tuple-element.35), channel_id=1, source_target_pairs={{0,1},{1,0},{2,3},{3,2},{4,5},{5,4},{6,7},{7,6},{8,9},{9,8},{10,11... | collective-permute-start | bytes 786440 | tf_op jit(solution)/shard_map/ppermute | solution.py:29
  37.0 0.0 collective-permute-start.8
  37.0 2.5 %collective-permute-done.8 = f32[8,128]{1,0:T(8,128)S(1)} collective-permute-done((f32[8,128]{1,0:T(8,128)S(1)}, f32[8,128]{1,0:T(8,128)S(1)}, u32[]{:S(2)}, u32[]{:S(2)}) %collective-permute-start.8) | collective-permute-done | bytes 4128 | tf_op jit(solution)/shard_map/ppermute | solution.py:29
  39.5 0.0 collective-permute-start.9
  39.5 2.5 %collective-permute-done.9 = f32[8,128]{1,0:T(8,128)S(1)} collective-permute-done((f32[8,128]{1,0:T(8,128)S(1)}, f32[8,128]{1,0:T(8,128)S(1)}, u32[]{:S(2)}, u32[]{:S(2)}) %collective-permute-start.9) | collective-permute-done | bytes 4128 | tf_op jit(solution)/shard_map/ppermute | solution.py:29
  41.9 0.0 collective-permute-start.10
  41.9 3.4 %collective-permute-done.10 = f32[8,128]{1,0:T(8,128)S(1)} collective-permute-done((f32[8,128]{1,0:T(8,128)S(1)}, f32[8,128]{1,0:T(8,128)S(1)}, u32[]{:S(2)}, u32[]{:S(2)}) %collective-permute-start.10) | collective-permute-done | bytes 4128 | tf_op jit(solution)/shard_map/ppermute | solution.py:29
  45.3 0.0 collective-permute-start.11
  45.3 2.7 %collective-permute-done.11 = f32[8,128]{1,0:T(8,128)S(1)} collective-permute-done((f32[8,128]{1,0:T(8,128)S(1)}, f32[8,128]{1,0:T(8,128)S(1)}, u32[]{:S(2)}, u32[]{:S(2)}) %collective-permute-start.11) | collective-permute-done | bytes 4128 | tf_op jit(solution)/shard_map/ppermute | solution.py:40
  48.1 4.4 %collective-permute-start.12 = (f32[8,128]{1,0:T(8,128)S(1)}, f32[8,128]{1,0:T(8,128)S(1)}, u32[]{:S(2)}, u32[]{:S(2)}) collective-permute-start(f32[8,128]{1,0:T(8,128)S(1)} %add.18), channel_id=1, source_target_pairs={{0,1},{1,0},{2,3},{3,2},{4,5},{5,4},{6,7},{7,6},{8,9},{9,8},{10,11... | collective-permute-start | bytes 12296 | tf_op jit(solution)/shard_map/ppermute | solution.py:29
  52.4 1.9 %collective-permute-start.15 = (bf16[2,2,256,128]{3,2,1,0:T(8,128)(2,1)S(1)}, bf16[2,2,256,128]{3,2,1,0:T(8,128)(2,1)S(1)}, u32[]{:S(2)}, u32[]{:S(2)}) collective-permute-start(bf16[2,2,256,128]{3,2,1,0:T(8,128)(2,1)S(1)} %get-tuple-element.42), channel_id=1, source_target_pairs={{2,0},{3,1},{4,2},{5,3},{6,4},{7,5},{8,6},{9,7},{10,8},{11,9},{12,... | collective-permute-start | bytes 786440 | tf_op jit(solution)/shard_map/ppermute | solution.py:24
  54.4 0.0 collective-permute-done.3.kv2
  54.4 0.0 collective-permute-done.2.kv1
  54.4 11.4 %grads.2 = (bf16[256,512]{1,0:T(8,128)(2,1)S(1)}, bf16[256,512]{1,0:T(8,128)(2,1)S(1)}, f32[2,2,256,128]{3,2,1,0:T(8,128)S(1)}, bf16[2,2,256,128]{3,2,1,0:T(8,128)(2,1)S(1)}, bf16[2,2,256,128]{3,2,1,0:T(8,128)(2,1)S(1)}) custom-call(s32[1]{0:T(128)} %bitcast.where_ref, s32[1,8]{1,0:T(1,128)S(1)} %copy-done.1, ...), custom_call_target="tpu_custom_call" | custom-call | flops 2013265920 | bytes 6291456 | tf_op jit(solution)/shard_map/grads/pallas_call | solution.py:356
  65.7 0.1 collective-permute-start.6
  65.8 1.9 %collective-permute-start.16 = (bf16[2,2,256,128]{3,2,1,0:T(8,128)(2,1)S(1)}, bf16[2,2,256,128]{3,2,1,0:T(8,128)(2,1)S(1)}, u32[]{:S(2)}, u32[]{:S(2)}) collective-permute-start(bf16[2,2,256,128]{3,2,1,0:T(8,128)(2,1)S(1)} %get-tuple-element.43), channel_id=1, source_target_pairs={{4,0},{5,1},{6,2},{7,3},{8,4},{9,5},{10,6},{11,7},{12,8},{13,9},{1... | collective-permute-start | bytes 786440 | tf_op jit(solution)/shard_map/ppermute | solution.py:24
  67.7 0.0 collective-permute-done.12
  67.8 1.9 %collective-permute-start.13 = (bf16[2,2,256,128]{3,2,1,0:T(8,128)(2,1)S(1)}, bf16[2,2,256,128]{3,2,1,0:T(8,128)(2,1)S(1)}, u32[]{:S(2)}, u32[]{:S(2)}) collective-permute-start(bf16[2,2,256,128]{3,2,1,0:T(8,128)(2,1)S(1)} %get-tuple-element.39), channel_id=1, source_target_pairs={{2,0},{3,1},{4,2},{5,3},{6,4},{7,5},{8,6},{9,7},{10,8},{11,9},{12,... | collective-permute-start | bytes 786440 | tf_op jit(solution)/shard_map/ppermute | solution.py:24
  69.7 0.0 collective-permute-done.7.refs_3_
  69.7 1.9 %collective-permute-start.14 = (bf16[2,2,256,128]{3,2,1,0:T(8,128)(2,1)S(1)}, bf16[2,2,256,128]{3,2,1,0:T(8,128)(2,1)S(1)}, u32[]{:S(2)}, u32[]{:S(2)}) collective-permute-start(bf16[2,2,256,128]{3,2,1,0:T(8,128)(2,1)S(1)} %get-tuple-element.40), channel_id=1, source_target_pairs={{4,0},{5,1},{6,2},{7,3},{8,4},{9,5},{10,6},{11,7},{12,8},{13,9},{1... | collective-permute-start | bytes 786440 | tf_op jit(solution)/shard_map/ppermute | solution.py:24
  71.6 0.0 collective-permute-done.6.refs_2_
  71.6 1.3 %shard_map.88 = (bf16[1,256,2048]{2,1,0:T(8,128)(2,1)}, f32[8,128]{1,0:T(8,128)S(1)}) custom-call(s32[1]{0:T(128)} %bitcast.where_ref, bf16[256,512]{1,0:T(8,128)(2,1)S(1)} %get-tuple-element.31.refs_0_, bf16[256,512]{1,0:T(8,128)(2,1)S(1)} %get-tuple-element.33.refs_1_, bf16[256,512]{1,0:T(8,128)(2,1)S(1)} %collective-permute-done.6.refs_2_, ...), custom_call_target="tpu_custom_call" | custom-call | bytes 1048576 | tf_op jit(solution)/shard_map/pallas_call | solution.py:66
  72.9 0.0 collective-permute-done.15.refs_4_
  72.9 2.2 %collective-permute-done.16.refs_5_ = bf16[2,2,256,128]{3,2,1,0:T(8,128)(2,1)S(1)} collective-permute-done((bf16[2,2,256,128]{3,2,1,0:T(8,128)(2,1)S(1)}, bf16[2,2,256,128]{3,2,1,0:T(8,128)(2,1)S(1)}, u32[]{:S(2)}, u32[]{:S(2)}) %collective-permute-start.16) | collective-permute-done | bytes 262176 | tf_op jit(solution)/shard_map/ppermute | solution.py:24
  75.1 3.7 %collective-permute-done.13.refs_1_ = bf16[2,2,256,128]{3,2,1,0:T(8,128)(2,1)S(1)} collective-permute-done((bf16[2,2,256,128]{3,2,1,0:T(8,128)(2,1)S(1)}, bf16[2,2,256,128]{3,2,1,0:T(8,128)(2,1)S(1)}, u32[]{:S(2)}, u32[]{:S(2)}) %collective-permute-start.13) | collective-permute-done | bytes 262176 | tf_op jit(solution)/shard_map/ppermute | solution.py:24
  78.8 7.5 %collective-permute-done.14.refs_2_ = bf16[2,2,256,128]{3,2,1,0:T(8,128)(2,1)S(1)} collective-permute-done((bf16[2,2,256,128]{3,2,1,0:T(8,128)(2,1)S(1)}, bf16[2,2,256,128]{3,2,1,0:T(8,128)(2,1)S(1)}, u32[]{:S(2)}, u32[]{:S(2)}) %collective-permute-start.14) | collective-permute-done | bytes 262176 | tf_op jit(solution)/shard_map/ppermute | solution.py:24
  86.3 0.2 shard_map.89
  86.5 1.4 %collective-permute-start.17 = (bf16[2,2,256,128]{3,2,1,0:T(8,128)(2,1)S(1)}, bf16[2,2,256,128]{3,2,1,0:T(8,128)(2,1)S(1)}, u32[]{:S(2)}, u32[]{:S(2)}) collective-permute-start(bf16[2,2,256,128]{3,2,1,0:T(8,128)(2,1)S(1)} %get-tuple-element.46), channel_id=1, source_target_pairs={{0,1},{1,0},{2,3},{3,2},{4,5},{5,4},{6,7},{7,6},{8,9},{9,8},{10,11... | collective-permute-start | bytes 786440 | tf_op jit(solution)/shard_map/ppermute | solution.py:29
  87.9 1.2 %collective-permute-done.17.got_ref = bf16[2,2,256,128]{3,2,1,0:T(8,128)(2,1)S(1)} collective-permute-done((bf16[2,2,256,128]{3,2,1,0:T(8,128)(2,1)S(1)}, bf16[2,2,256,128]{3,2,1,0:T(8,128)(2,1)S(1)}, u32[]{:S(2)}, u32[]{:S(2)}) %collective-permute-start.17) | collective-permute-done | bytes 262176 | tf_op jit(solution)/shard_map/ppermute | solution.py:29
  89.1 0.9 shard_map.90
  (6 shorter events, 0.1 us)
Async XLA Ops:
  1.8 0.7 copy-start
  4.1 19.4 %collective-permute-start = (bf16[2,8,256,128]{3,2,1,0:T(8,128)(2,1)S(1)}, bf16[2,8,256,128]{3,2,1,0:T(8,128)(2,1)S(1)}, u32[]{:S(2)}, u32[]{:S(2)}) collective-permute-start(bf16[2,8,256,128]{3,2,1,0:T(8,128)(2,1)S(1)} %get-tuple-element.28), channel_id=1, source_target_pairs={{0,1},{1,0},{2,3},{3,2},{4,5},{5,4},{6,7},{7,6},{8,9},{9,8},{10,11... | collective-permute-start | bytes 3145736 | tf_op jit(solution)/shard_map/ppermute | solution.py:29
  4.9 2.7 %collective-permute-start.1 = (bf16[2,2,256,128]{3,2,1,0:T(8,128)(2,1)S(1)}, bf16[2,2,256,128]{3,2,1,0:T(8,128)(2,1)S(1)}, u32[]{:S(2)}, u32[]{:S(2)}) collective-permute-start(bf16[2,2,256,128]{3,2,1,0:T(8,128)(2,1)S(1)} %get-tuple-element.26.after_ref), channel_id=1, source_target_pairs={{0,1},{1,0},{2,3},{3,2},{4,5},{5,4},{6,7},{7,6},{8,9},{9,8},{10,11... | collective-permute-start | bytes 786440 | tf_op jit(solution)/shard_map/ppermute | solution.py:29
  7.6 10.2 %collective-permute-start.5 = (bf16[2,2,256,128]{3,2,1,0:T(8,128)(2,1)S(1)}, bf16[2,2,256,128]{3,2,1,0:T(8,128)(2,1)S(1)}, u32[]{:S(2)}, u32[]{:S(2)}) collective-permute-start(bf16[2,2,256,128]{3,2,1,0:T(8,128)(2,1)S(1)} %get-tuple-element.32.kv0), channel_id=1, source_target_pairs={{0,4},{1,5},{2,6},{3,7},{4,8},{5,9},{6,10},{7,11},{8,12},{9,13},{1... | collective-permute-start | bytes 786440 | tf_op jit(solution)/shard_map/ppermute | solution.py:24
  10.8 12.7 %collective-permute-start.4 = (bf16[2,2,256,128]{3,2,1,0:T(8,128)(2,1)S(1)}, bf16[2,2,256,128]{3,2,1,0:T(8,128)(2,1)S(1)}, u32[]{:S(2)}, u32[]{:S(2)}) collective-permute-start(bf16[2,2,256,128]{3,2,1,0:T(8,128)(2,1)S(1)} %get-tuple-element.32.kv0), channel_id=1, source_target_pairs={{0,2},{1,3},{2,4},{3,5},{4,6},{5,7},{6,8},{7,9},{8,10},{9,11},{10,... | collective-permute-start | bytes 786440 | tf_op jit(solution)/shard_map/ppermute | solution.py:24
  13.9 9.6 %copy-start.1 = (s32[1,8]{1,0:T(1,128)S(1)}, s32[1,8]{1,0:T(1,128)}, u32[]{:S(2)}) copy-start(s32[1,8]{1,0:T(1,128)} %lengths_ref.3) | copy-start | bytes 100
  14.0 40.4 %collective-permute-start.3 = (bf16[2,2,256,128]{3,2,1,0:T(8,128)(2,1)S(1)}, bf16[2,2,256,128]{3,2,1,0:T(8,128)(2,1)S(1)}, u32[]{:S(2)}, u32[]{:S(2)}) collective-permute-start(bf16[2,2,256,128]{3,2,1,0:T(8,128)(2,1)S(1)} %get-tuple-element.30.kv0), channel_id=1, source_target_pairs={{0,4},{1,5},{2,6},{3,7},{4,8},{5,9},{6,10},{7,11},{8,12},{9,13},{1... | collective-permute-start | bytes 786440 | tf_op jit(solution)/shard_map/ppermute | solution.py:24
  15.9 38.5 %collective-permute-start.2 = (bf16[2,2,256,128]{3,2,1,0:T(8,128)(2,1)S(1)}, bf16[2,2,256,128]{3,2,1,0:T(8,128)(2,1)S(1)}, u32[]{:S(2)}, u32[]{:S(2)}) collective-permute-start(bf16[2,2,256,128]{3,2,1,0:T(8,128)(2,1)S(1)} %get-tuple-element.30.kv0), channel_id=1, source_target_pairs={{0,2},{1,3},{2,4},{3,5},{4,6},{5,7},{6,8},{7,9},{8,10},{9,11},{10,... | collective-permute-start | bytes 786440 | tf_op jit(solution)/shard_map/ppermute | solution.py:24
  34.9 34.8 %collective-permute-start.7 = (bf16[256,512]{1,0:T(8,128)(2,1)S(1)}, bf16[256,512]{1,0:T(8,128)(2,1)S(1)}, u32[]{:S(2)}, u32[]{:S(2)}) collective-permute-start(bf16[256,512]{1,0:T(8,128)(2,1)S(1)} %get-tuple-element.35), channel_id=1, source_target_pairs={{0,1},{1,0},{2,3},{3,2},{4,5},{5,4},{6,7},{7,6},{8,9},{9,8},{10,11... | collective-permute-start | bytes 786440 | tf_op jit(solution)/shard_map/ppermute | solution.py:29
  37.0 2.5 %collective-permute-start.8 = (f32[8,128]{1,0:T(8,128)S(1)}, f32[8,128]{1,0:T(8,128)S(1)}, u32[]{:S(2)}, u32[]{:S(2)}) collective-permute-start(f32[8,128]{1,0:T(8,128)S(1)} %get-tuple-element.36), channel_id=1, source_target_pairs={{0,2},{1,3},{2,0},{3,1},{4,6},{5,7},{6,4},{7,5},{8,10},{9,11},{10,... | collective-permute-start | bytes 12296 | tf_op jit(solution)/shard_map/ppermute | solution.py:29
  39.5 2.5 %collective-permute-start.9 = (f32[8,128]{1,0:T(8,128)S(1)}, f32[8,128]{1,0:T(8,128)S(1)}, u32[]{:S(2)}, u32[]{:S(2)}) collective-permute-start(f32[8,128]{1,0:T(8,128)S(1)} %add.15), channel_id=1, source_target_pairs={{0,4},{1,5},{2,6},{3,7},{4,0},{5,1},{6,2},{7,3},{8,12},{9,13},{10,... | collective-permute-start | bytes 12296 | tf_op jit(solution)/shard_map/ppermute | solution.py:29
  41.9 3.4 %collective-permute-start.10 = (f32[8,128]{1,0:T(8,128)S(1)}, f32[8,128]{1,0:T(8,128)S(1)}, u32[]{:S(2)}, u32[]{:S(2)}) collective-permute-start(f32[8,128]{1,0:T(8,128)S(1)} %add.16), channel_id=1, source_target_pairs={{0,8},{1,9},{2,10},{3,11},{4,12},{5,13},{6,14},{7,15},{8,0},{9,1},... | collective-permute-start | bytes 12296 | tf_op jit(solution)/shard_map/ppermute | solution.py:29
  45.3 2.8 %collective-permute-start.11 = (f32[8,128]{1,0:T(8,128)S(1)}, f32[8,128]{1,0:T(8,128)S(1)}, u32[]{:S(2)}, u32[]{:S(2)}) collective-permute-start(f32[8,128]{1,0:T(8,128)S(1)} %add.17), channel_id=1, source_target_pairs={{0,16},{16,0},{1,17},{17,1},{2,18},{18,2},{3,19},{19,3},{4,20},{20... | collective-permute-start | bytes 12296 | tf_op jit(solution)/shard_map/ppermute | solution.py:40
  48.1 19.7 %collective-permute-start.12 = (f32[8,128]{1,0:T(8,128)S(1)}, f32[8,128]{1,0:T(8,128)S(1)}, u32[]{:S(2)}, u32[]{:S(2)}) collective-permute-start(f32[8,128]{1,0:T(8,128)S(1)} %add.18), channel_id=1, source_target_pairs={{0,1},{1,0},{2,3},{3,2},{4,5},{5,4},{6,7},{7,6},{8,9},{9,8},{10,11... | collective-permute-start | bytes 12296 | tf_op jit(solution)/shard_map/ppermute | solution.py:29
  52.4 20.5 %collective-permute-start.15 = (bf16[2,2,256,128]{3,2,1,0:T(8,128)(2,1)S(1)}, bf16[2,2,256,128]{3,2,1,0:T(8,128)(2,1)S(1)}, u32[]{:S(2)}, u32[]{:S(2)}) collective-permute-start(bf16[2,2,256,128]{3,2,1,0:T(8,128)(2,1)S(1)} %get-tuple-element.42), channel_id=1, source_target_pairs={{2,0},{3,1},{4,2},{5,3},{6,4},{7,5},{8,6},{9,7},{10,8},{11,9},{12,... | collective-permute-start | bytes 786440 | tf_op jit(solution)/shard_map/ppermute | solution.py:24
  65.7 5.9 %collective-permute-start.6 = (bf16[256,512]{1,0:T(8,128)(2,1)S(1)}, bf16[256,512]{1,0:T(8,128)(2,1)S(1)}, u32[]{:S(2)}, u32[]{:S(2)}) collective-permute-start(bf16[256,512]{1,0:T(8,128)(2,1)S(1)} %get-tuple-element.34), channel_id=1, source_target_pairs={{0,1},{1,0},{2,3},{3,2},{4,5},{5,4},{6,7},{7,6},{8,9},{9,8},{10,11... | collective-permute-start | bytes 786440 | tf_op jit(solution)/shard_map/ppermute | solution.py:29
  65.8 9.3 %collective-permute-start.16 = (bf16[2,2,256,128]{3,2,1,0:T(8,128)(2,1)S(1)}, bf16[2,2,256,128]{3,2,1,0:T(8,128)(2,1)S(1)}, u32[]{:S(2)}, u32[]{:S(2)}) collective-permute-start(bf16[2,2,256,128]{3,2,1,0:T(8,128)(2,1)S(1)} %get-tuple-element.43), channel_id=1, source_target_pairs={{4,0},{5,1},{6,2},{7,3},{8,4},{9,5},{10,6},{11,7},{12,8},{13,9},{1... | collective-permute-start | bytes 786440 | tf_op jit(solution)/shard_map/ppermute | solution.py:24
  67.8 11.0 %collective-permute-start.13 = (bf16[2,2,256,128]{3,2,1,0:T(8,128)(2,1)S(1)}, bf16[2,2,256,128]{3,2,1,0:T(8,128)(2,1)S(1)}, u32[]{:S(2)}, u32[]{:S(2)}) collective-permute-start(bf16[2,2,256,128]{3,2,1,0:T(8,128)(2,1)S(1)} %get-tuple-element.39), channel_id=1, source_target_pairs={{2,0},{3,1},{4,2},{5,3},{6,4},{7,5},{8,6},{9,7},{10,8},{11,9},{12,... | collective-permute-start | bytes 786440 | tf_op jit(solution)/shard_map/ppermute | solution.py:24
  69.7 16.6 %collective-permute-start.14 = (bf16[2,2,256,128]{3,2,1,0:T(8,128)(2,1)S(1)}, bf16[2,2,256,128]{3,2,1,0:T(8,128)(2,1)S(1)}, u32[]{:S(2)}, u32[]{:S(2)}) collective-permute-start(bf16[2,2,256,128]{3,2,1,0:T(8,128)(2,1)S(1)} %get-tuple-element.40), channel_id=1, source_target_pairs={{4,0},{5,1},{6,2},{7,3},{8,4},{9,5},{10,6},{11,7},{12,8},{13,9},{1... | collective-permute-start | bytes 786440 | tf_op jit(solution)/shard_map/ppermute | solution.py:24
  86.5 2.6 %collective-permute-start.17 = (bf16[2,2,256,128]{3,2,1,0:T(8,128)(2,1)S(1)}, bf16[2,2,256,128]{3,2,1,0:T(8,128)(2,1)S(1)}, u32[]{:S(2)}, u32[]{:S(2)}) collective-permute-start(bf16[2,2,256,128]{3,2,1,0:T(8,128)(2,1)S(1)} %get-tuple-element.46), channel_id=1, source_target_pairs={{0,1},{1,0},{2,3},{3,2},{4,5},{5,4},{6,7},{7,6},{8,9},{9,8},{10,11... | collective-permute-start | bytes 786440 | tf_op jit(solution)/shard_map/ppermute | solution.py:29

commit v4 on v3

--- a/solution.py
+++ b/solution.py
@@ -16,6 +16,7 @@
 MINE = HK // 2
 BLOCKS = WIN + 2
 EXP2_SCALE = HD ** (-0.5) * math.log2(math.e)
+MOST_EXCESS = 60.0
 
 
 def shifted(value, by):
@@ -164,42 +165,38 @@
     )
 
 
-def total_call(where, numerator, parts, count):
-    rows = parts[0][0].shape[2]
+def total_call(where, numerator, part, count):
+    rows = part[0].shape[2]
+
+    def kernel(where_ref, d0, r1, r2, count_ref, own, give):
+        scale = numerator / count_ref[0:1, :]
+        for kv, factor in enumerate((scale * HD ** (-0.5), scale)):
+            for p, out in enumerate((own, give)):
+                out[kv] = (
+                    (d0[p, kv] + r1[p, kv].astype(jnp.float32) + r2[p, kv].astype(jnp.float32))
+                    * factor
+                ).astype(jnp.bfloat16)
+
+    shape = [jax.ShapeDtypeStruct((2, rows, HD), jnp.bfloat16)] * 2
+    return simple_call(kernel, where, [in_vmem() for _ in range(4)], shape, *part, count)
+
+
+def finish_kv_call(where, own, got):
+    rows = own[0].shape[1]
+    width = MINE * HD
 
     def kernel(where_ref, *refs):
-        own, give = refs[-2:]
-        scale = numerator / refs[-3][0:1, :]
-        for h in range(MINE):
-            d0, r1, r2 = refs[3 * h : 3 * h + 3]
-            for kv, factor in enumerate((scale * HD ** (-0.5), scale)):
-                for p, out in enumerate((own, give)):
-                    out[h, kv] = (
-                        (d0[p, kv] + r1[p, kv].astype(jnp.float32) + r2[p, kv].astype(jnp.float32))
-                        * factor
-                    ).astype(jnp.bfloat16)
-
-    args = [a for part in parts for a in part] + [count]
-    specs = [in_vmem() for _ in args]
-    shape = [jax.ShapeDtypeStruct((MINE, 2, rows, HD), jnp.bfloat16)] * 2
-    return simple_call(kernel, where, specs, shape, *args)
-
-
-def finish_kv_call(where, own, got):
-    rows = own.shape[2]
-    width = MINE * HD
-
-    def kernel(where_ref, own_ref, got_ref, *outs):
         parity = where_ref[0] & 1
-        for kv, out in enumerate(outs):
-            for h in range(MINE):
-                mine = pl.multiple_of(parity * width + h * HD, HD)
-                theirs = pl.multiple_of((1 - parity) * width + h * HD, HD)
-                out[0, :, pl.ds(mine, HD)] = own_ref[h, kv]
-                out[0, :, pl.ds(theirs, HD)] = got_ref[h, kv]
+        outs = refs[2 * MINE :]
+        for base, parts in ((parity, refs[:MINE]), (1 - parity, refs[MINE : 2 * MINE])):
+            for h, part in enumerate(parts):
+                at = pl.ds(pl.multiple_of(base * width + h * HD, HD), HD)
+                for kv, out in enumerate(outs):
+                    out[0, :, at] = part[kv]
 
     shape = [jax.ShapeDtypeStruct((1, rows, 2 * width), jnp.bfloat16)] * 2
-    return simple_call(kernel, where, [in_vmem()] * 2, shape, own, got)
+    args = list(own) + list(got)
+    return simple_call(kernel, where, [in_vmem() for _ in args], shape, *args)
 
 
 def finish_q_call(where, numerator, own, got, count):
@@ -232,7 +229,7 @@
 def grads_kernel(
     where_ref, lengths_ref, own_qg, got_qg, kv0, kv1, kv2,
     own_dq, sib_dq, out0, out1, out2,
-    k_s, v_s, kt_s, e_s, dp_s, mb_s, m_s, l_s, w_s, dqt_s, dk_s, dv_s,
+    k_s, v_s, kt_s, bias_s, e_s, dp_s, mb_s, m_s, top_s, l_s, w_s, dqt_s, dk_s, dv_s,
 ):
     rows = own_qg.shape[2]
     my_index = where_ref[0]
@@ -263,9 +260,6 @@
             0, doc_count, doc_step, (zero, zero, zero, jnp.zeros((1, rows), jnp.int32))
         )
         t_pos = q_start + lax.broadcasted_iota(jnp.int32, (1, rows), 1)
-        m_s[...] = jnp.full_like(m_s, -jnp.inf)
-        l_s[...] = jnp.zeros_like(l_s)
-        w_s[...] = jnp.zeros_like(w_s)
         dqt_s[...] = jnp.zeros_like(dqt_s)
 
         def locate(j):
@@ -274,42 +268,77 @@
             live = (k_start >= 0) & (k_start <= q_start) & (k_start + rows > first)
             return kb, k_start, live
 
-        def phase_a(j, _):
+        def is_full(k_start):
+            return (k_start < q_start) & (k_start >= last)
+
+        def mask_step(j, _):
             kb, k_start, live = locate(j)
 
-            def scores(bias):
-                k = k_s[kb]
-                v = v_s[kb]
-                for h in range(GROUP):
-                    s = nt(k, q_s[h])
-                    if bias is not None:
-                        s = s + bias
-                    dp = nt(v, g_s[h])
-                    m_old = m_s[h]
-                    m_new = jnp.maximum(m_old, jnp.max(s, axis=0, keepdims=True))
-                    keep = jnp.exp2((m_old - m_new) * EXP2_SCALE)
-                    e = jnp.exp2((s - m_new) * EXP2_SCALE)
-                    l_s[h] = l_s[h] * keep + jnp.sum(e, axis=0, keepdims=True)
-                    w_s[h] = w_s[h] * keep + jnp.sum(e * dp, axis=0, keepdims=True)
-                    m_s[h] = m_new
-                    mb_s[kb * GROUP + h] = m_new
-                    e_s[kb * GROUP + h] = e
-                    dp_s[kb * GROUP + h] = dp
-
-            full = (k_start < q_start) & (k_start >= last)
-
-            @pl.when(live & full)
-            def _():
-                scores(None)
-
-            @pl.when(live & jnp.logical_not(full))
+            @pl.when(live & jnp.logical_not(is_full(k_start)))
             def _():
                 u_pos = k_start + lax.broadcasted_iota(jnp.int32, (rows, rows), 0)
-                scores(jnp.where((u_pos >= lo) & (u_pos <= t_pos), 0.0, -jnp.inf))
+                bias_s[kb] = jnp.where((u_pos >= lo) & (u_pos <= t_pos), 0.0, -jnp.inf)
 
             return 0
 
-        lax.fori_loop(0, BLOCKS, phase_a, 0)
+        lax.fori_loop(0, BLOCKS, mask_step, 0)
+
+        def block(kb, masked, fixed):
+            k = k_s[kb]
+            v = v_s[kb]
+            for h in range(GROUP):
+                s = nt(k, q_s[h])
+                if masked:
+                    s = s + bias_s[kb]
+                dp = nt(v, g_s[h])
+                top = jnp.max(s, axis=0, keepdims=True)
+                if fixed:
+                    m_new = m_s[h]
+                    top_s[h] = jnp.maximum(top_s[h], top)
+                    old_l, old_w = l_s[h], w_s[h]
+                else:
+                    m_new = jnp.maximum(m_s[h], top)
+                    keep = jnp.exp2((m_s[h] - m_new) * EXP2_SCALE)
+                    old_l, old_w = l_s[h] * keep, w_s[h] * keep
+                    m_s[h] = m_new
+                    top_s[h] = m_new
+                e = jnp.exp2((s - m_new) * EXP2_SCALE)
+                l_s[h] = old_l + jnp.sum(e, axis=0, keepdims=True)
+                w_s[h] = old_w + jnp.sum(e * dp, axis=0, keepdims=True)
+                mb_s[kb * GROUP + h] = m_new
+                e_s[kb * GROUP + h] = e
+                dp_s[kb * GROUP + h] = dp
+
+        def steps(fixed):
+            def step(j, _):
+                kb, k_start, live = locate(j)
+
+                @pl.when(live & is_full(k_start))
+                def _():
+                    block(kb, False, fixed)
+
+                @pl.when(live & jnp.logical_not(is_full(k_start)))
+                def _():
+                    block(kb, True, fixed)
+
+                return 0
+
+            return step
+
+        def begin():
+            m_s[...] = jnp.full_like(m_s, -jnp.inf)
+            l_s[...] = jnp.zeros_like(l_s)
+            w_s[...] = jnp.zeros_like(w_s)
+
+        begin()
+        block(qb, True, False)
+        lax.fori_loop(1, BLOCKS, steps(True), 0)
+        excess = jnp.max((top_s[...] - m_s[...]) * EXP2_SCALE)
+
+        @pl.when(jnp.logical_not(excess <= MOST_EXCESS))
+        def _():
+            begin()
+            lax.fori_loop(0, BLOCKS, steps(False), 0)
 
         def phase_b(j, _):
             kb, _, live = locate(j)
@@ -367,9 +396,11 @@
                 pltpu.VMEM((BLOCKS, rows, HD), bf16),
                 pltpu.VMEM((BLOCKS, rows, HD), bf16),
                 pltpu.VMEM((BLOCKS, HD, rows), bf16),
+                pltpu.VMEM((BLOCKS, rows, rows), f32),
                 pltpu.VMEM((tiles, rows, rows), f32),
                 pltpu.VMEM((tiles, rows, rows), f32),
                 pltpu.VMEM((tiles, 1, rows), f32),
+                pltpu.VMEM((GROUP, 1, rows), f32),
                 pltpu.VMEM((GROUP, 1, rows), f32),
                 pltpu.VMEM((GROUP, 1, rows), f32),
                 pltpu.VMEM((GROUP, 1, rows), f32),
@@ -428,8 +459,13 @@
         got_dq.append(swapped(dq_s, 1))
     count = everywhere_sum(token)
     query_grad, count = finish_q_call(where, numerator, own_dq, got_dq, count)
-    own_total, give_total = total_call(where, numerator, parts, count)
-    key_grad, value_grad = finish_kv_call(where, own_total, swapped(give_total, 1))
+    own_totals = []
+    got_totals = []
+    for part in parts:
+        own_total, give_total = total_call(where, numerator, part, count)
+        own_totals.append(own_total)
+        got_totals.append(swapped(give_total, 1))
+    key_grad, value_grad = finish_kv_call(where, own_totals, got_totals)
     return query_grad, key_grad, value_grad
 
 

time: 90.4 us -> 94.1 us (1.041)
  the two profiles are of different devices: /device:TPU:17 before, /device:TPU:9 now
where the time goes in v4:
time: 94.1 us; the launch traced here: 93.7 us
  waiting for transfers between devices  35.1 us (37%)
  starting transfers between devices  32.6 us (35%)
  Pallas kernels  24.4 us (26%)
    ppermute x8, waiting for transfers between devices, shifted(): return lax.ppermute(value, 'ctx', pairs)  23.6 us
    pallas_call x2, Pallas kernels, grads_call(): pl.pallas_call(grads_kernel, grid_spec=pltpu.PrefetchScalarGridSpec(num_s...  19.2 us
    ppermute x8, starting transfers between devices, shifted(): return lax.ppermute(value, 'ctx', pairs)  19.2 us
    ppermute x10, starting transfers between devices, swapped(): return lax.ppermute(value, 'ctx', [(i, i ^ bit) for i in range(count)])  12.9 us
    ppermute x10, waiting for transfers between devices, swapped(): return lax.ppermute(value, 'ctx', [(i, i ^ bit) for i in range(count)])  9.48 us
    pallas_call x7, Pallas kernels, simple_call(): pl.pallas_call(kernel, grid_spec=pltpu.PrefetchScalarGridSpec(num_scalar_...  5.18 us
    ppermute x1, waiting for transfers between devices, everywhere_sum(): other = lax.ppermute(value, 'dp', [(i, i ^ step) for i in range(dp_count)])  2.05 us
  transfers between devices with their start and end apart: 19, of which 10 were waited for; matrix products, arithmetic and copies ran while one was open for 0% of the time, Pallas kernels for 22%

profile of v4, /device:TPU:9, one launch (start us, length us, event | category | flops | bytes accessed | tf_op | source)
XLA Modules:
  0.0 93.7 jit_solution(3993007282344318323)
XLA Ops:
  0.6 1.1 %shard_map.85 = (bf16[2,2,256,128]{3,2,1,0:T(8,128)(2,1)S(1)}, bf16[2,2,256,128]{3,2,1,0:T(8,128)(2,1)S(1)}) custom-call(s32[1]{0:T(128)} %bitcast.where_ref, bf16[1,256,512]{2,1,0:T(8,128)(2,1)} %k_ref.1, bf16[1,256,512]{2,1,0:T(8,128)(2,1)} %v_ref.1), custom_call_target="tpu_custom_call" | custom-call | bytes 1048576 | tf_op jit(solution)/shard_map/pallas_call | solution.py:67
  1.8 0.0 copy-start
  1.8 0.7 copy-done
  2.5 1.7 %shard_map.86 = (bf16[2,8,256,128]{3,2,1,0:T(8,128)(2,1)S(1)}, bf16[2,8,256,128]{3,2,1,0:T(8,128)(2,1)S(1)}, f32[8,128]{1,0:T(8,128)S(1)}) custom-call(s32[1]{0:T(128)} %bitcast.where_ref, bf16[1,256,2048]{2,1,0:T(8,128)(2,1)} %q_ref.1, bf16[1,256,2048]{2,1,0:T(8,128)(2,1)} %g_ref.1, s32[1,256]{1,0:T(1,128)S(1)} %copy-done, ...), custom_call_target="tpu_custom_call" | custom-call | bytes 1048576 | tf_op jit(solution)/shard_map/pallas_call | solution.py:67
  4.1 0.7 collective-permute-start
  4.9 0.1 collective-permute-start.1
  5.0 2.6 %collective-permute-done.1.got = bf16[2,2,256,128]{3,2,1,0:T(8,128)(2,1)S(1)} collective-permute-done((bf16[2,2,256,128]{3,2,1,0:T(8,128)(2,1)S(1)}, bf16[2,2,256,128]{3,2,1,0:T(8,128)(2,1)S(1)}, u32[]{:S(2)}, u32[]{:S(2)}) %collective-permute-start.1) | collective-permute-done | bytes 262176 | tf_op jit(solution)/shard_map/ppermute | solution.py:30
  7.6 3.2 %collective-permute-start.5 = (bf16[2,2,256,128]{3,2,1,0:T(8,128)(2,1)S(1)}, bf16[2,2,256,128]{3,2,1,0:T(8,128)(2,1)S(1)}, u32[]{:S(2)}, u32[]{:S(2)}) collective-permute-start(bf16[2,2,256,128]{3,2,1,0:T(8,128)(2,1)S(1)} %get-tuple-element.34.kv0), channel_id=1, source_target_pairs={{0,4},{1,5},{2,6},{3,7},{4,8},{5,9},{6,10},{7,11},{8,12},{9,13},{1... | collective-permute-start | bytes 786440 | tf_op jit(solution)/shard_map/ppermute | solution.py:25
  10.8 3.1 %collective-permute-start.4 = (bf16[2,2,256,128]{3,2,1,0:T(8,128)(2,1)S(1)}, bf16[2,2,256,128]{3,2,1,0:T(8,128)(2,1)S(1)}, u32[]{:S(2)}, u32[]{:S(2)}) collective-permute-start(bf16[2,2,256,128]{3,2,1,0:T(8,128)(2,1)S(1)} %get-tuple-element.34.kv0), channel_id=1, source_target_pairs={{0,2},{1,3},{2,4},{3,5},{4,6},{5,7},{6,8},{7,9},{8,10},{9,11},{10,... | collective-permute-start | bytes 786440 | tf_op jit(solution)/shard_map/ppermute | solution.py:25
  13.9 0.0 copy-start.1
  14.0 3.2 %collective-permute-start.3 = (bf16[2,2,256,128]{3,2,1,0:T(8,128)(2,1)S(1)}, bf16[2,2,256,128]{3,2,1,0:T(8,128)(2,1)S(1)}, u32[]{:S(2)}, u32[]{:S(2)}) collective-permute-start(bf16[2,2,256,128]{3,2,1,0:T(8,128)(2,1)S(1)} %get-tuple-element.32.kv0), channel_id=1, source_target_pairs={{0,4},{1,5},{2,6},{3,7},{4,8},{5,9},{6,10},{7,11},{8,12},{9,13},{1... | collective-permute-start | bytes 786440 | tf_op jit(solution)/shard_map/ppermute | solution.py:25
  17.2 1.9 %collective-permute-start.2 = (bf16[2,2,256,128]{3,2,1,0:T(8,128)(2,1)S(1)}, bf16[2,2,256,128]{3,2,1,0:T(8,128)(2,1)S(1)}, u32[]{:S(2)}, u32[]{:S(2)}) collective-permute-start(bf16[2,2,256,128]{3,2,1,0:T(8,128)(2,1)S(1)} %get-tuple-element.32.kv0), channel_id=1, source_target_pairs={{0,2},{1,3},{2,4},{3,5},{4,6},{5,7},{6,8},{7,9},{8,10},{9,11},{10,... | collective-permute-start | bytes 786440 | tf_op jit(solution)/shard_map/ppermute | solution.py:25
  19.1 0.0 collective-permute-done.5.kv2
  19.1 4.4 %collective-permute-done.4.kv1 = bf16[2,2,256,128]{3,2,1,0:T(8,128)(2,1)S(1)} collective-permute-done((bf16[2,2,256,128]{3,2,1,0:T(8,128)(2,1)S(1)}, bf16[2,2,256,128]{3,2,1,0:T(8,128)(2,1)S(1)}, u32[]{:S(2)}, u32[]{:S(2)}) %collective-permute-start.4) | collective-permute-done | bytes 262176 | tf_op jit(solution)/shard_map/ppermute | solution.py:25
  23.5 0.0 collective-permute-done.got_qg
  23.5 9.5 %grads.3 = (bf16[256,512]{1,0:T(8,128)(2,1)S(1)}, bf16[256,512]{1,0:T(8,128)(2,1)S(1)}, f32[2,2,256,128]{3,2,1,0:T(8,128)S(1)}, bf16[2,2,256,128]{3,2,1,0:T(8,128)(2,1)S(1)}, bf16[2,2,256,128]{3,2,1,0:T(8,128)(2,1)S(1)}) custom-call(s32[1]{0:T(128)} %bitcast.where_ref, s32[1,8]{1,0:T(1,128)S(1)} %copy-done.1, ...), custom_call_target="tpu_custom_call" | custom-call | flops 2013265920 | bytes 6291456 | tf_op jit(solution)/shard_map/grads/pallas_call | solution.py:385
  33.1 2.1 %collective-permute-start.7 = (bf16[256,512]{1,0:T(8,128)(2,1)S(1)}, bf16[256,512]{1,0:T(8,128)(2,1)S(1)}, u32[]{:S(2)}, u32[]{:S(2)}) collective-permute-start(bf16[256,512]{1,0:T(8,128)(2,1)S(1)} %get-tuple-element.37), channel_id=1, source_target_pairs={{0,1},{1,0},{2,3},{3,2},{4,5},{5,4},{6,7},{7,6},{8,9},{9,8},{10,11... | collective-permute-start | bytes 786440 | tf_op jit(solution)/shard_map/ppermute | solution.py:30
  35.2 0.0 collective-permute-start.8
  35.2 2.5 %collective-permute-done.8 = f32[8,128]{1,0:T(8,128)S(1)} collective-permute-done((f32[8,128]{1,0:T(8,128)S(1)}, f32[8,128]{1,0:T(8,128)S(1)}, u32[]{:S(2)}, u32[]{:S(2)}) %collective-permute-start.8) | collective-permute-done | bytes 4128 | tf_op jit(solution)/shard_map/ppermute | solution.py:30
  37.6 0.0 collective-permute-start.9
  37.6 2.5 %collective-permute-done.9 = f32[8,128]{1,0:T(8,128)S(1)} collective-permute-done((f32[8,128]{1,0:T(8,128)S(1)}, f32[8,128]{1,0:T(8,128)S(1)}, u32[]{:S(2)}, u32[]{:S(2)}) %collective-permute-start.9) | collective-permute-done | bytes 4128 | tf_op jit(solution)/shard_map/ppermute | solution.py:30
  40.1 3.0 %collective-permute-start.10 = (f32[8,128]{1,0:T(8,128)S(1)}, f32[8,128]{1,0:T(8,128)S(1)}, u32[]{:S(2)}, u32[]{:S(2)}) collective-permute-start(f32[8,128]{1,0:T(8,128)S(1)} %add.16), channel_id=1, source_target_pairs={{0,8},{1,9},{2,10},{3,11},{4,12},{5,13},{6,14},{7,15},{8,0},{9,1},... | collective-permute-start | bytes 12296 | tf_op jit(solution)/shard_map/ppermute | solution.py:30
  43.1 1.0 %collective-permute-done.10 = f32[8,128]{1,0:T(8,128)S(1)} collective-permute-done((f32[8,128]{1,0:T(8,128)S(1)}, f32[8,128]{1,0:T(8,128)S(1)}, u32[]{:S(2)}, u32[]{:S(2)}) %collective-permute-start.10) | collective-permute-done | bytes 4128 | tf_op jit(solution)/shard_map/ppermute | solution.py:30
  44.1 0.5 collective-permute-start.11
  44.6 2.1 %collective-permute-done.11 = f32[8,128]{1,0:T(8,128)S(1)} collective-permute-done((f32[8,128]{1,0:T(8,128)S(1)}, f32[8,128]{1,0:T(8,128)S(1)}, u32[]{:S(2)}, u32[]{:S(2)}) %collective-permute-start.11) | collective-permute-done | bytes 4128 | tf_op jit(solution)/shard_map/ppermute | solution.py:41
  46.7 4.0 %collective-permute-start.12 = (f32[8,128]{1,0:T(8,128)S(1)}, f32[8,128]{1,0:T(8,128)S(1)}, u32[]{:S(2)}, u32[]{:S(2)}) collective-permute-start(f32[8,128]{1,0:T(8,128)S(1)} %add.18), channel_id=1, source_target_pairs={{0,1},{1,0},{2,3},{3,2},{4,5},{5,4},{6,7},{7,6},{8,9},{9,8},{10,11... | collective-permute-start | bytes 12296 | tf_op jit(solution)/shard_map/ppermute | solution.py:30
  50.7 0.0 collective-permute-done.3.kv2
  50.7 0.0 collective-permute-done.2.kv1
  50.7 9.7 %grads.2 = (bf16[256,512]{1,0:T(8,128)(2,1)S(1)}, bf16[256,512]{1,0:T(8,128)(2,1)S(1)}, f32[2,2,256,128]{3,2,1,0:T(8,128)S(1)}, bf16[2,2,256,128]{3,2,1,0:T(8,128)(2,1)S(1)}, bf16[2,2,256,128]{3,2,1,0:T(8,128)(2,1)S(1)}) custom-call(s32[1]{0:T(128)} %bitcast.where_ref, s32[1,8]{1,0:T(1,128)S(1)} %copy-done.1, ...), custom_call_target="tpu_custom_call" | custom-call | flops 2013265920 | bytes 6291456 | tf_op jit(solution)/shard_map/grads/pallas_call | solution.py:385
  60.4 0.1 collective-permute-start.6
  60.4 1.9 %collective-permute-start.15 = (bf16[2,2,256,128]{3,2,1,0:T(8,128)(2,1)S(1)}, bf16[2,2,256,128]{3,2,1,0:T(8,128)(2,1)S(1)}, u32[]{:S(2)}, u32[]{:S(2)}) collective-permute-start(bf16[2,2,256,128]{3,2,1,0:T(8,128)(2,1)S(1)} %get-tuple-element.46), channel_id=1, source_target_pairs={{2,0},{3,1},{4,2},{5,3},{6,4},{7,5},{8,6},{9,7},{10,8},{11,9},{12,... | collective-permute-start | bytes 786440 | tf_op jit(solution)/shard_map/ppermute | solution.py:25
  62.4 1.9 %collective-permute-start.16 = (bf16[2,2,256,128]{3,2,1,0:T(8,128)(2,1)S(1)}, bf16[2,2,256,128]{3,2,1,0:T(8,128)(2,1)S(1)}, u32[]{:S(2)}, u32[]{:S(2)}) collective-permute-start(bf16[2,2,256,128]{3,2,1,0:T(8,128)(2,1)S(1)} %get-tuple-element.47), channel_id=1, source_target_pairs={{4,0},{5,1},{6,2},{7,3},{8,4},{9,5},{10,6},{11,7},{12,8},{13,9},{1... | collective-permute-start | bytes 786440 | tf_op jit(solution)/shard_map/ppermute | solution.py:25
  64.3 0.0 collective-permute-done.12
  64.3 1.9 %collective-permute-start.13 = (bf16[2,2,256,128]{3,2,1,0:T(8,128)(2,1)S(1)}, bf16[2,2,256,128]{3,2,1,0:T(8,128)(2,1)S(1)}, u32[]{:S(2)}, u32[]{:S(2)}) collective-permute-start(bf16[2,2,256,128]{3,2,1,0:T(8,128)(2,1)S(1)} %get-tuple-element.41), channel_id=1, source_target_pairs={{2,0},{3,1},{4,2},{5,3},{6,4},{7,5},{8,6},{9,7},{10,8},{11,9},{12,... | collective-permute-start | bytes 786440 | tf_op jit(solution)/shard_map/ppermute | solution.py:25
  66.2 0.0 collective-permute-done.7.refs_3_
  66.3 1.9 %collective-permute-start.14 = (bf16[2,2,256,128]{3,2,1,0:T(8,128)(2,1)S(1)}, bf16[2,2,256,128]{3,2,1,0:T(8,128)(2,1)S(1)}, u32[]{:S(2)}, u32[]{:S(2)}) collective-permute-start(bf16[2,2,256,128]{3,2,1,0:T(8,128)(2,1)S(1)} %get-tuple-element.42), channel_id=1, source_target_pairs={{4,0},{5,1},{6,2},{7,3},{8,4},{9,5},{10,6},{11,7},{12,8},{13,9},{1... | collective-permute-start | bytes 786440 | tf_op jit(solution)/shard_map/ppermute | solution.py:25
  68.2 0.0 collective-permute-done.6.refs_2_
  68.2 1.3 %shard_map.88 = (bf16[1,256,2048]{2,1,0:T(8,128)(2,1)}, f32[8,128]{1,0:T(8,128)S(1)}) custom-call(s32[1]{0:T(128)} %bitcast.where_ref, bf16[256,512]{1,0:T(8,128)(2,1)S(1)} %get-tuple-element.33.refs_0_, bf16[256,512]{1,0:T(8,128)(2,1)S(1)} %get-tuple-element.35.refs_1_, bf16[256,512]{1,0:T(8,128)(2,1)S(1)} %collective-permute-done.6.refs_2_, ...), custom_call_target="tpu_custom_call" | custom-call | bytes 1048576 | tf_op jit(solution)/shard_map/pallas_call | solution.py:67
  69.5 0.2 collective-permute-done.15.r1
  69.7 9.6 %collective-permute-done.16.r2 = bf16[2,2,256,128]{3,2,1,0:T(8,128)(2,1)S(1)} collective-permute-done((bf16[2,2,256,128]{3,2,1,0:T(8,128)(2,1)S(1)}, bf16[2,2,256,128]{3,2,1,0:T(8,128)(2,1)S(1)}, u32[]{:S(2)}, u32[]{:S(2)}) %collective-permute-start.16) | collective-permute-done | bytes 262176 | tf_op jit(solution)/shard_map/ppermute | solution.py:25
  79.3 0.1 shard_map.90
  79.4 1.8 %collective-permute-start.18 = (bf16[2,256,128]{2,1,0:T(8,128)(2,1)S(1)}, bf16[2,256,128]{2,1,0:T(8,128)(2,1)S(1)}, u32[]{:S(2)}, u32[]{:S(2)}) collective-permute-start(bf16[2,256,128]{2,1,0:T(8,128)(2,1)S(1)} %get-tuple-element.50), channel_id=1, source_target_pairs={{0,1},{1,0},{2,3},{3,2},{4,5},{5,4},{6,7},{7,6},{8,9},{9,8},{10,11... | collective-permute-start | bytes 393224 | tf_op jit(solution)/shard_map/ppermute | solution.py:30
  81.2 0.0 collective-permute-done.13.r1
  81.2 9.3 %collective-permute-done.14.r2 = bf16[2,2,256,128]{3,2,1,0:T(8,128)(2,1)S(1)} collective-permute-done((bf16[2,2,256,128]{3,2,1,0:T(8,128)(2,1)S(1)}, bf16[2,2,256,128]{3,2,1,0:T(8,128)(2,1)S(1)}, u32[]{:S(2)}, u32[]{:S(2)}) %collective-permute-start.14) | collective-permute-done | bytes 262176 | tf_op jit(solution)/shard_map/ppermute | solution.py:25
  90.6 0.1 shard_map.89
  90.7 1.1 %collective-permute-start.17 = (bf16[2,256,128]{2,1,0:T(8,128)(2,1)S(1)}, bf16[2,256,128]{2,1,0:T(8,128)(2,1)S(1)}, u32[]{:S(2)}, u32[]{:S(2)}) collective-permute-start(bf16[2,256,128]{2,1,0:T(8,128)(2,1)S(1)} %get-tuple-element.49), channel_id=1, source_target_pairs={{0,1},{1,0},{2,3},{3,2},{4,5},{5,4},{6,7},{7,6},{8,9},{9,8},{10,11... | collective-permute-start | bytes 393224 | tf_op jit(solution)/shard_map/ppermute | solution.py:30
  91.8 1.0 %collective-permute-done.17.refs_2_ = bf16[2,256,128]{2,1,0:T(8,128)(2,1)S(1)} collective-permute-done((bf16[2,256,128]{2,1,0:T(8,128)(2,1)S(1)}, bf16[2,256,128]{2,1,0:T(8,128)(2,1)S(1)}, u32[]{:S(2)}, u32[]{:S(2)}) %collective-permute-start.17) | collective-permute-done | bytes 131104 | tf_op jit(solution)/shard_map/ppermute | solution.py:30
  92.8 0.9 shard_map.91
  (8 shorter events, 0.1 us)
Async XLA Ops:
  1.8 0.7 copy-start
  4.1 19.4 %collective-permute-start = (bf16[2,8,256,128]{3,2,1,0:T(8,128)(2,1)S(1)}, bf16[2,8,256,128]{3,2,1,0:T(8,128)(2,1)S(1)}, u32[]{:S(2)}, u32[]{:S(2)}) collective-permute-start(bf16[2,8,256,128]{3,2,1,0:T(8,128)(2,1)S(1)} %get-tuple-element.30), channel_id=1, source_target_pairs={{0,1},{1,0},{2,3},{3,2},{4,5},{5,4},{6,7},{7,6},{8,9},{9,8},{10,11... | collective-permute-start | bytes 3145736 | tf_op jit(solution)/shard_map/ppermute | solution.py:30
  4.9 2.7 %collective-permute-start.1 = (bf16[2,2,256,128]{3,2,1,0:T(8,128)(2,1)S(1)}, bf16[2,2,256,128]{3,2,1,0:T(8,128)(2,1)S(1)}, u32[]{:S(2)}, u32[]{:S(2)}) collective-permute-start(bf16[2,2,256,128]{3,2,1,0:T(8,128)(2,1)S(1)} %get-tuple-element.28.after_ref), channel_id=1, source_target_pairs={{0,1},{1,0},{2,3},{3,2},{4,5},{5,4},{6,7},{7,6},{8,9},{9,8},{10,11... | collective-permute-start | bytes 786440 | tf_op jit(solution)/shard_map/ppermute | solution.py:30
  7.6 11.5 %collective-permute-start.5 = (bf16[2,2,256,128]{3,2,1,0:T(8,128)(2,1)S(1)}, bf16[2,2,256,128]{3,2,1,0:T(8,128)(2,1)S(1)}, u32[]{:S(2)}, u32[]{:S(2)}) collective-permute-start(bf16[2,2,256,128]{3,2,1,0:T(8,128)(2,1)S(1)} %get-tuple-element.34.kv0), channel_id=1, source_target_pairs={{0,4},{1,5},{2,6},{3,7},{4,8},{5,9},{6,10},{7,11},{8,12},{9,13},{1... | collective-permute-start | bytes 786440 | tf_op jit(solution)/shard_map/ppermute | solution.py:25
  10.8 12.7 %collective-permute-start.4 = (bf16[2,2,256,128]{3,2,1,0:T(8,128)(2,1)S(1)}, bf16[2,2,256,128]{3,2,1,0:T(8,128)(2,1)S(1)}, u32[]{:S(2)}, u32[]{:S(2)}) collective-permute-start(bf16[2,2,256,128]{3,2,1,0:T(8,128)(2,1)S(1)} %get-tuple-element.34.kv0), channel_id=1, source_target_pairs={{0,2},{1,3},{2,4},{3,5},{4,6},{5,7},{6,8},{7,9},{8,10},{9,11},{10,... | collective-permute-start | bytes 786440 | tf_op jit(solution)/shard_map/ppermute | solution.py:25
  13.9 9.6 %copy-start.1 = (s32[1,8]{1,0:T(1,128)S(1)}, s32[1,8]{1,0:T(1,128)}, u32[]{:S(2)}) copy-start(s32[1,8]{1,0:T(1,128)} %lengths_ref.3) | copy-start | bytes 100
  14.0 36.7 %collective-permute-start.3 = (bf16[2,2,256,128]{3,2,1,0:T(8,128)(2,1)S(1)}, bf16[2,2,256,128]{3,2,1,0:T(8,128)(2,1)S(1)}, u32[]{:S(2)}, u32[]{:S(2)}) collective-permute-start(bf16[2,2,256,128]{3,2,1,0:T(8,128)(2,1)S(1)} %get-tuple-element.32.kv0), channel_id=1, source_target_pairs={{0,4},{1,5},{2,6},{3,7},{4,8},{5,9},{6,10},{7,11},{8,12},{9,13},{1... | collective-permute-start | bytes 786440 | tf_op jit(solution)/shard_map/ppermute | solution.py:25
  17.2 33.5 %collective-permute-start.2 = (bf16[2,2,256,128]{3,2,1,0:T(8,128)(2,1)S(1)}, bf16[2,2,256,128]{3,2,1,0:T(8,128)(2,1)S(1)}, u32[]{:S(2)}, u32[]{:S(2)}) collective-permute-start(bf16[2,2,256,128]{3,2,1,0:T(8,128)(2,1)S(1)} %get-tuple-element.32.kv0), channel_id=1, source_target_pairs={{0,2},{1,3},{2,4},{3,5},{4,6},{5,7},{6,8},{7,9},{8,10},{9,11},{10,... | collective-permute-start | bytes 786440 | tf_op jit(solution)/shard_map/ppermute | solution.py:25
  33.1 33.2 %collective-permute-start.7 = (bf16[256,512]{1,0:T(8,128)(2,1)S(1)}, bf16[256,512]{1,0:T(8,128)(2,1)S(1)}, u32[]{:S(2)}, u32[]{:S(2)}) collective-permute-start(bf16[256,512]{1,0:T(8,128)(2,1)S(1)} %get-tuple-element.37), channel_id=1, source_target_pairs={{0,1},{1,0},{2,3},{3,2},{4,5},{5,4},{6,7},{7,6},{8,9},{9,8},{10,11... | collective-permute-start | bytes 786440 | tf_op jit(solution)/shard_map/ppermute | solution.py:30
  35.2 2.5 %collective-permute-start.8 = (f32[8,128]{1,0:T(8,128)S(1)}, f32[8,128]{1,0:T(8,128)S(1)}, u32[]{:S(2)}, u32[]{:S(2)}) collective-permute-start(f32[8,128]{1,0:T(8,128)S(1)} %get-tuple-element.38), channel_id=1, source_target_pairs={{0,2},{1,3},{2,0},{3,1},{4,6},{5,7},{6,4},{7,5},{8,10},{9,11},{10,... | collective-permute-start | bytes 12296 | tf_op jit(solution)/shard_map/ppermute | solution.py:30
  37.6 2.5 %collective-permute-start.9 = (f32[8,128]{1,0:T(8,128)S(1)}, f32[8,128]{1,0:T(8,128)S(1)}, u32[]{:S(2)}, u32[]{:S(2)}) collective-permute-start(f32[8,128]{1,0:T(8,128)S(1)} %add.15), channel_id=1, source_target_pairs={{0,4},{1,5},{2,6},{3,7},{4,0},{5,1},{6,2},{7,3},{8,12},{9,13},{10,... | collective-permute-start | bytes 12296 | tf_op jit(solution)/shard_map/ppermute | solution.py:30
  40.1 4.0 %collective-permute-start.10 = (f32[8,128]{1,0:T(8,128)S(1)}, f32[8,128]{1,0:T(8,128)S(1)}, u32[]{:S(2)}, u32[]{:S(2)}) collective-permute-start(f32[8,128]{1,0:T(8,128)S(1)} %add.16), channel_id=1, source_target_pairs={{0,8},{1,9},{2,10},{3,11},{4,12},{5,13},{6,14},{7,15},{8,0},{9,1},... | collective-permute-start | bytes 12296 | tf_op jit(solution)/shard_map/ppermute | solution.py:30
  44.1 2.6 %collective-permute-start.11 = (f32[8,128]{1,0:T(8,128)S(1)}, f32[8,128]{1,0:T(8,128)S(1)}, u32[]{:S(2)}, u32[]{:S(2)}) collective-permute-start(f32[8,128]{1,0:T(8,128)S(1)} %add.17), channel_id=1, source_target_pairs={{0,16},{16,0},{1,17},{17,1},{2,18},{18,2},{3,19},{19,3},{4,20},{20... | collective-permute-start | bytes 12296 | tf_op jit(solution)/shard_map/ppermute | solution.py:41
  46.7 17.6 %collective-permute-start.12 = (f32[8,128]{1,0:T(8,128)S(1)}, f32[8,128]{1,0:T(8,128)S(1)}, u32[]{:S(2)}, u32[]{:S(2)}) collective-permute-start(f32[8,128]{1,0:T(8,128)S(1)} %add.18), channel_id=1, source_target_pairs={{0,1},{1,0},{2,3},{3,2},{4,5},{5,4},{6,7},{7,6},{8,9},{9,8},{10,11... | collective-permute-start | bytes 12296 | tf_op jit(solution)/shard_map/ppermute | solution.py:30
  60.4 7.8 %collective-permute-start.6 = (bf16[256,512]{1,0:T(8,128)(2,1)S(1)}, bf16[256,512]{1,0:T(8,128)(2,1)S(1)}, u32[]{:S(2)}, u32[]{:S(2)}) collective-permute-start(bf16[256,512]{1,0:T(8,128)(2,1)S(1)} %get-tuple-element.36), channel_id=1, source_target_pairs={{0,1},{1,0},{2,3},{3,2},{4,5},{5,4},{6,7},{7,6},{8,9},{9,8},{10,11... | collective-permute-start | bytes 786440 | tf_op jit(solution)/shard_map/ppermute | solution.py:30
  60.4 9.3 %collective-permute-start.15 = (bf16[2,2,256,128]{3,2,1,0:T(8,128)(2,1)S(1)}, bf16[2,2,256,128]{3,2,1,0:T(8,128)(2,1)S(1)}, u32[]{:S(2)}, u32[]{:S(2)}) collective-permute-start(bf16[2,2,256,128]{3,2,1,0:T(8,128)(2,1)S(1)} %get-tuple-element.46), channel_id=1, source_target_pairs={{2,0},{3,1},{4,2},{5,3},{6,4},{7,5},{8,6},{9,7},{10,8},{11,9},{12,... | collective-permute-start | bytes 786440 | tf_op jit(solution)/shard_map/ppermute | solution.py:25
  62.4 16.9 %collective-permute-start.16 = (bf16[2,2,256,128]{3,2,1,0:T(8,128)(2,1)S(1)}, bf16[2,2,256,128]{3,2,1,0:T(8,128)(2,1)S(1)}, u32[]{:S(2)}, u32[]{:S(2)}) collective-permute-start(bf16[2,2,256,128]{3,2,1,0:T(8,128)(2,1)S(1)} %get-tuple-element.47), channel_id=1, source_target_pairs={{4,0},{5,1},{6,2},{7,3},{8,4},{9,5},{10,6},{11,7},{12,8},{13,9},{1... | collective-permute-start | bytes 786440 | tf_op jit(solution)/shard_map/ppermute | solution.py:25
  64.3 16.9 %collective-permute-start.13 = (bf16[2,2,256,128]{3,2,1,0:T(8,128)(2,1)S(1)}, bf16[2,2,256,128]{3,2,1,0:T(8,128)(2,1)S(1)}, u32[]{:S(2)}, u32[]{:S(2)}) collective-permute-start(bf16[2,2,256,128]{3,2,1,0:T(8,128)(2,1)S(1)} %get-tuple-element.41), channel_id=1, source_target_pairs={{2,0},{3,1},{4,2},{5,3},{6,4},{7,5},{8,6},{9,7},{10,8},{11,9},{12,... | collective-permute-start | bytes 786440 | tf_op jit(solution)/shard_map/ppermute | solution.py:25
  66.3 24.3 %collective-permute-start.14 = (bf16[2,2,256,128]{3,2,1,0:T(8,128)(2,1)S(1)}, bf16[2,2,256,128]{3,2,1,0:T(8,128)(2,1)S(1)}, u32[]{:S(2)}, u32[]{:S(2)}) collective-permute-start(bf16[2,2,256,128]{3,2,1,0:T(8,128)(2,1)S(1)} %get-tuple-element.42), channel_id=1, source_target_pairs={{4,0},{5,1},{6,2},{7,3},{8,4},{9,5},{10,6},{11,7},{12,8},{13,9},{1... | collective-permute-start | bytes 786440 | tf_op jit(solution)/shard_map/ppermute | solution.py:25
  79.4 12.4 %collective-permute-start.18 = (bf16[2,256,128]{2,1,0:T(8,128)(2,1)S(1)}, bf16[2,256,128]{2,1,0:T(8,128)(2,1)S(1)}, u32[]{:S(2)}, u32[]{:S(2)}) collective-permute-start(bf16[2,256,128]{2,1,0:T(8,128)(2,1)S(1)} %get-tuple-element.50), channel_id=1, source_target_pairs={{0,1},{1,0},{2,3},{3,2},{4,5},{5,4},{6,7},{7,6},{8,9},{9,8},{10,11... | collective-permute-start | bytes 393224 | tf_op jit(solution)/shard_map/ppermute | solution.py:30
  90.7 2.1 %collective-permute-start.17 = (bf16[2,256,128]{2,1,0:T(8,128)(2,1)S(1)}, bf16[2,256,128]{2,1,0:T(8,128)(2,1)S(1)}, u32[]{:S(2)}, u32[]{:S(2)}) collective-permute-start(bf16[2,256,128]{2,1,0:T(8,128)(2,1)S(1)} %get-tuple-element.49), channel_id=1, source_target_pairs={{0,1},{1,0},{2,3},{3,2},{4,5},{5,4},{6,7},{7,6},{8,9},{9,8},{10,11... | collective-permute-start | bytes 393224 | tf_op jit(solution)/shard_map/ppermute | solution.py:30
